TPU v7x, 32 devices: a whole 2x2x4 slice. The times are simulated.
32 devices in a mesh: head: 4 (over x, core), blk: 8 (over z, y).
Axes of the slice: x: 2, y: 2, z: 4, core: 2. Of those that a mesh axis runs over, the one named last changes fastest.
Arguments:
- layer_input: bfloat16 [4096, 1024], P(('head', 'blk')), may hold values from -6 to 6
- out_grad: bfloat16 [4096, 1024], P(('head', 'blk')), may hold values from -6 to 6
- lengths: int32 [4], replicated, may hold values from 1 to 2048, 3072 in all
- ln_attn: bfloat16 [1024], P(('head', 'blk')), may hold values from 0.5 to 1.5
- w_qkv: bfloat16 [1024, 3072], P(('head', 'blk')), may hold values from -0.1875 to 0.1875
- w_attn_out: bfloat16 [1024, 1024], P(('head', 'blk')), may hold values from -6 to 6
- ln_mlp: bfloat16 [1024], P(('head', 'blk')), may hold values from 0.5 to 1.5
- w_in: bfloat16 [1024, 5248], P(('head', 'blk')), may hold values from -0.1875 to 0.1875
- w_mlp_out: bfloat16 [2624, 1024], P(None, ('head', 'blk')), may hold values from -0.125 to 0.125
Outputs:
- layer_output: float32 [4096, 1024], P(('head', 'blk'))
- input_grad: float32 [4096, 1024], P(('head', 'blk'))
- d_ln_attn: float32 [1024], P(('head', 'blk'))
- d_w_qkv: float32 [1024, 3072], P(('head', 'blk'))
- d_w_attn_out: float32 [1024, 1024], P(('head', 'blk'))
- d_ln_mlp: float32 [1024], P(('head', 'blk'))
- d_w_in: float32 [1024, 5248], P(('head', 'blk'))
- d_w_mlp_out: float32 [2624, 1024], P(None, ('head', 'blk'))
Inputs may be any that keep to these rules, and one draw needn't show every extreme that they name: lengths of the 4 sequences packed from slot 0; they sum to 3072 and the longest is exactly 2048; the remaining slots are padding.
All inputs are finite; a program needn't handle non-finite values.
Results may differ from a plain program's by a relative error of at most 0.023.
Values may be sent and summed in bfloat16 or wider, within the bound.
A program may use at most 192 MiB of HBM per device.

v0:
```python
import jax
import jax.numpy as jnp
from jax import lax
from jax.sharding import PartitionSpec as P

DH = 64


ROPE_BASE = 160000.0
NORM_EPS = 1e-05
MASK_FLOOR = -1e30


def norm_forward(values, gain):
    centre = values - jnp.mean(values, axis=-1, keepdims=True)
    variance = jnp.mean(centre * centre, axis=-1, keepdims=True)
    scale_row = lax.rsqrt(variance + NORM_EPS)
    normed = centre * scale_row
    return (normed * gain, normed, scale_row)


def norm_backward(grad_rows, gain, normed, scale_row):
    scaled_grad = grad_rows * gain
    gain_grad = jnp.sum(grad_rows * normed, axis=0)
    mean_one = jnp.mean(scaled_grad, axis=-1, keepdims=True)
    mean_two = jnp.mean(scaled_grad * normed, axis=-1, keepdims=True)
    return (scale_row * (scaled_grad - mean_one - normed * mean_two), gain_grad)


def locate(rows_at, lengths):
    seq_ends = jnp.cumsum(lengths)
    segment = jnp.sum((rows_at[:, None] >= seq_ends[None, :]).astype(jnp.int32), axis=1)
    seq_starts = jnp.concatenate([seq_ends - lengths, seq_ends[-1:]])
    picked = segment[:, None] == lax.iota(jnp.int32, seq_starts.shape[0])[None, :]
    begins = jnp.sum(jnp.where(picked, seq_starts[None, :], 0), axis=1)
    return (segment, rows_at - begins)


def rotate(values, position, sign_value):
    half_dim = values.shape[-1] // 2
    inv_freq = jnp.power(ROPE_BASE, -2.0 * lax.iota(jnp.float32, half_dim) / values.shape[-1])
    angles = position.astype(jnp.float32)[:, None] * inv_freq[None, :]
    cosine = jnp.cos(angles)[:, None, :]
    sine_part = sign_value * jnp.sin(angles)[:, None, :]
    front_part = values[..., :half_dim]
    back_part = values[..., half_dim:]
    return jnp.concatenate(
        [front_part * cosine - back_part * sine_part, back_part * cosine + front_part * sine_part],
        axis=-1,
    )


def spread(flat_rows, rows_dev, group_rows, cycle_size):
    owner = flat_rows // group_rows
    inner = flat_rows % group_rows
    return inner // rows_dev * (cycle_size * rows_dev) + owner * rows_dev + inner % rows_dev


def block_size(row_count, base_rows):
    for block_rows in (512, base_rows):
        return block_rows
    return row_count


def take_rows(array_in, block_at, block_rows):
    return lax.dynamic_slice_in_dim(array_in, block_at * block_rows, block_rows, 0)


def online(carried, queries, keys_in, values_in, seg_query, seg_key):
    top_score, row_total, weighted = carried
    scores = (
        jnp.einsum("qhd,khd->hqk", queries, keys_in, preferred_element_type=jnp.float32) * 0.125
    )
    same_seq = (seg_query[:, None] == seg_key[None, :])[None]
    scores = jnp.where(same_seq, scores, MASK_FLOOR)
    new_top = jnp.maximum(top_score, jnp.max(scores, axis=-1))
    weights = jnp.where(same_seq, jnp.exp(scores - new_top[:, :, None]), 0.0)
    rescale = jnp.exp(top_score - new_top)
    row_total = row_total * rescale + jnp.sum(weights, axis=-1)
    weighted = weighted * rescale.T[:, :, None] + jnp.einsum(
        "hqk,khd->qhd", weights.astype(jnp.bfloat16), values_in, preferred_element_type=jnp.float32
    )
    return (new_top, row_total, weighted)


def score_grads(query_in, key_in, value_in, grad_rows, lse_in, delta_in, seg_query, seg_key):
    scores = (
        jnp.einsum("qhd,khd->hqk", query_in, key_in, preferred_element_type=jnp.float32) * 0.125
    )
    same_seq = (seg_query[:, None] == seg_key[None, :])[None]
    probs = jnp.exp(jnp.where(same_seq, scores - lse_in[:, :, None], MASK_FLOOR))
    grad_probs = jnp.einsum("qhd,khd->hqk", grad_rows, value_in, preferred_element_type=jnp.float32)
    grad_scores = (probs * (grad_probs - delta_in[:, :, None])).astype(jnp.bfloat16)
    return (probs, grad_scores)


def key_grad_rows(query_in, grad_rows, lse_in, delta_in, seg_query, keys_in, values_in, seg_key):
    probs, grad_scores = score_grads(
        query_in, keys_in, values_in, grad_rows, lse_in, delta_in, seg_query, seg_key
    )
    grad_keys = 0.125 * jnp.einsum(
        "hqk,qhd->khd", grad_scores, query_in, preferred_element_type=jnp.float32
    )
    grad_values = jnp.einsum(
        "hqk,qhd->khd", probs.astype(jnp.bfloat16), grad_rows, preferred_element_type=jnp.float32
    )
    return (grad_keys, grad_values)


def shards(layer_input, out_grad, lengths, ln_attn, w_qkv, w_attn_out, ln_mlp, w_in, w_mlp_out):
    head_groups = lax.axis_size("head")
    cycle_size = lax.axis_size("blk")
    rows_dev = layer_input.shape[0]
    width = layer_input.shape[1]
    all_heads = width // DH
    local_heads = all_heads // head_groups
    local_width = local_heads * DH
    group_rows = head_groups * rows_dev
    nseq_count = lengths.shape[0]
    gain_one, wqkv_full, wout_full, gain_two, win_full, wdown_full = (
        lax.all_gather(ln_attn, ("head", "blk"), axis=0, tiled=True),
        lax.all_gather(w_qkv, ("head", "blk"), axis=0, tiled=True),
        lax.all_gather(w_attn_out, ("head", "blk"), axis=0, tiled=True),
        lax.all_gather(ln_mlp, ("head", "blk"), axis=0, tiled=True),
        lax.all_gather(w_in, ("head", "blk"), axis=0, tiled=True),
        lax.all_gather(w_mlp_out, ("head", "blk"), axis=1, tiled=True),
    )
    gain_one = gain_one.astype(jnp.float32)
    gain_two = gain_two.astype(jnp.float32)
    blk_index = lax.axis_index("blk")
    own_rows = (lax.axis_index("head") * cycle_size + blk_index) * rows_dev + lax.iota(
        jnp.int32, rows_dev
    )
    segment, position = locate(own_rows, lengths)
    valid = (segment < nseq_count).astype(jnp.float32)[:, None]

    def cycle_segments(first_row, row_count):
        flat_rows = first_row + lax.iota(jnp.int32, row_count)
        return locate(spread(flat_rows, rows_dev, group_rows, cycle_size), lengths)[0]

    x_float = layer_input.astype(jnp.float32)
    norm_one, normed_one, scale_one = norm_forward(x_float, gain_one)
    input_bf = norm_one.astype(jnp.bfloat16)
    qkv_all = jnp.dot(input_bf, wqkv_full, preferred_element_type=jnp.float32).reshape(
        rows_dev, 3, all_heads, DH
    )
    stacked = jnp.stack(
        [rotate(qkv_all[:, 0], position, 1.0), rotate(qkv_all[:, 1], position, 1.0), qkv_all[:, 2]],
        axis=1,
    )
    stacked = stacked.astype(jnp.bfloat16).reshape(rows_dev, 3, head_groups, local_width)
    regrouped = lax.all_to_all(stacked, "head", split_axis=2, concat_axis=0, tiled=True)
    queries = regrouped[:, 0, 0].reshape(group_rows, local_heads, DH)
    key_value = regrouped[:, 1:, 0]
    own_keys = key_value[:, 0].reshape(group_rows, local_heads, DH)
    own_values = key_value[:, 1].reshape(group_rows, local_heads, DH)
    query_seg = cycle_segments(blk_index * group_rows, group_rows)
    start_state = (
        jnp.full((local_heads, group_rows), MASK_FLOOR, jnp.float32),
        jnp.zeros((local_heads, group_rows), jnp.float32),
        jnp.zeros((group_rows, local_heads, DH), jnp.float32),
    )
    carried = start_state
    key_part = lax.all_gather(key_value, "blk", axis=0, tiled=True)
    row_count = key_part.shape[0]
    block_rows = block_size(row_count, group_rows)
    key_seg = cycle_segments(jnp.int32(0), row_count)

    def attend_one_step(inner, block_at):
        part_rows = take_rows(key_part, block_at, block_rows)
        part_seg = take_rows(key_seg, block_at, block_rows)
        keys_in = part_rows[:, 0].reshape(block_rows, local_heads, DH)
        values_in = part_rows[:, 1].reshape(block_rows, local_heads, DH)
        return (online(inner, queries, keys_in, values_in, query_seg, part_seg), None)

    carried, ignored = lax.scan(
        attend_one_step, carried, lax.iota(jnp.int32, row_count // block_rows)
    )
    top_score, row_total, weighted = carried
    log_total = top_score + jnp.log(row_total)
    attended = weighted / row_total.T[:, :, None]
    attended_bf = attended.reshape(group_rows, local_width).astype(jnp.bfloat16)
    mixed = lax.all_to_all(attended_bf, "head", split_axis=0, concat_axis=1, tiled=True)
    attn_out = jnp.dot(mixed, wout_full, preferred_element_type=jnp.float32)
    hidden = x_float + attn_out
    norm_two, normed_two, scale_two = norm_forward(hidden, gain_two)
    middle_bf = norm_two.astype(jnp.bfloat16)
    gate_up = jnp.dot(middle_bf, win_full, preferred_element_type=jnp.float32)
    ff_width = gate_up.shape[1] // 2
    gate_part = gate_up[:, :ff_width]
    up_part = gate_up[:, ff_width:]
    gelu_gate, gelu_pull = jax.vjp(
        lambda gate_in: jax.nn.gelu(gate_in, approximate=False), gate_part
    )
    product = (gelu_gate * up_part).astype(jnp.bfloat16)
    mlp_out = jnp.dot(product, wdown_full, preferred_element_type=jnp.float32)
    y_out = valid * (hidden + mlp_out)
    grad_out = (out_grad.astype(jnp.float32) * valid).astype(jnp.bfloat16)
    grad_down = jnp.dot(product.T, grad_out, preferred_element_type=jnp.float32)
    grad_product = jnp.dot(grad_out, wdown_full.T, preferred_element_type=jnp.float32)
    grad_gate = gelu_pull(grad_product * up_part)[0]
    grad_gate_up = jnp.concatenate([grad_gate, grad_product * gelu_gate], axis=1).astype(
        jnp.bfloat16
    )
    grad_win = jnp.dot(middle_bf.T, grad_gate_up, preferred_element_type=jnp.float32)
    grad_middle = jnp.dot(grad_gate_up, win_full.T, preferred_element_type=jnp.float32)
    grad_hidden_ln, grad_gain_two = norm_backward(grad_middle, gain_two, normed_two, scale_two)
    grad_hidden = grad_out.astype(jnp.float32) + grad_hidden_ln
    grad_attn_bf = grad_hidden.astype(jnp.bfloat16)
    grad_wout = jnp.dot(mixed.T, grad_attn_bf, preferred_element_type=jnp.float32)
    grad_mixed = jnp.dot(grad_attn_bf, wout_full.T, preferred_element_type=jnp.float32).astype(
        jnp.bfloat16
    )
    grad_heads = lax.all_to_all(
        grad_mixed, "head", split_axis=1, concat_axis=0, tiled=True
    ).reshape(group_rows, local_heads, DH)
    row_delta = jnp.sum(grad_heads.astype(jnp.float32) * attended, axis=-1).T
    zero_grad = jnp.zeros((group_rows, local_heads, DH), jnp.float32)
    total_grad = zero_grad
    query_key_part = lax.all_gather(key_value, "blk", axis=0, tiled=True)
    row_count = query_key_part.shape[0]
    query_block_rows = block_size(row_count, group_rows)
    query_key_seg = cycle_segments(jnp.int32(0), row_count)

    def query_one_step(inner, block_at):
        part_rows = take_rows(query_key_part, block_at, query_block_rows)
        part_seg = take_rows(query_key_seg, block_at, query_block_rows)
        keys_in = part_rows[:, 0].reshape(query_block_rows, local_heads, DH)
        values_in = part_rows[:, 1].reshape(query_block_rows, local_heads, DH)
        probs, grad_scores = score_grads(
            queries, keys_in, values_in, grad_heads, log_total, row_delta, query_seg, part_seg
        )
        return (
            inner
            + 0.125
            * jnp.einsum("hqk,khd->qhd", grad_scores, keys_in, preferred_element_type=jnp.float32),
            None,
        )

    total_grad, ignored = lax.scan(
        query_one_step, total_grad, lax.iota(jnp.int32, row_count // query_block_rows)
    )
    carried = (zero_grad, zero_grad)
    query_rows = lax.all_gather(queries.astype(jnp.float32), "blk", axis=0, tiled=True)
    grad_rows = lax.all_gather(grad_heads.astype(jnp.float32), "blk", axis=0, tiled=True)
    lse_rows = lax.all_gather(log_total.T, "blk", axis=0, tiled=True)
    delta_rows = lax.all_gather(row_delta.T, "blk", axis=0, tiled=True)
    row_count = query_rows.shape[0]
    gather_block_rows = block_size(row_count, group_rows)
    seg_rows = cycle_segments(jnp.int32(0), row_count)

    def gather_one_step(inner, block_at):
        grad_keys, grad_values = key_grad_rows(
            take_rows(query_rows, block_at, gather_block_rows).astype(jnp.bfloat16),
            take_rows(grad_rows, block_at, gather_block_rows).astype(jnp.bfloat16),
            take_rows(lse_rows, block_at, gather_block_rows).T,
            take_rows(delta_rows, block_at, gather_block_rows).T,
            take_rows(seg_rows, block_at, gather_block_rows),
            own_keys,
            own_values,
            query_seg,
        )
        return ((inner[0] + grad_keys, inner[1] + grad_values), None)

    carried, ignored = lax.scan(
        gather_one_step, carried, lax.iota(jnp.int32, row_count // gather_block_rows)
    )
    grad_keys_all, grad_values_all = carried
    grad_stack = jnp.stack(
        [
            total_grad.reshape(group_rows, local_width),
            grad_keys_all.reshape(group_rows, local_width),
            grad_values_all.reshape(group_rows, local_width),
        ],
        axis=1,
    )
    grad_stack = grad_stack.astype(jnp.bfloat16).reshape(group_rows, 3, 1, local_width)
    grad_tokens = (
        lax.all_to_all(grad_stack, "head", split_axis=0, concat_axis=2, tiled=True)
        .reshape(rows_dev, 3, all_heads, DH)
        .astype(jnp.float32)
    )
    grad_qkv = jnp.stack(
        [
            rotate(grad_tokens[:, 0], position, -1.0),
            rotate(grad_tokens[:, 1], position, -1.0),
            grad_tokens[:, 2],
        ],
        axis=1,
    )
    grad_qkv = grad_qkv.reshape(rows_dev, 3 * width).astype(jnp.bfloat16)
    grad_wqkv = jnp.dot(input_bf.T, grad_qkv, preferred_element_type=jnp.float32)
    grad_input = jnp.dot(grad_qkv, wqkv_full.T, preferred_element_type=jnp.float32)
    grad_x_ln, grad_gain_one = norm_backward(grad_input, gain_one, normed_one, scale_one)
    dx_out = grad_hidden + grad_x_ln
    summed = (
        lax.psum_scatter(grad_gain_one, ("head", "blk"), scatter_dimension=0, tiled=True),
        lax.psum_scatter(grad_wqkv, ("head", "blk"), scatter_dimension=0, tiled=True),
        lax.psum_scatter(grad_wout, ("head", "blk"), scatter_dimension=0, tiled=True),
        lax.psum_scatter(grad_gain_two, ("head", "blk"), scatter_dimension=0, tiled=True),
        lax.psum_scatter(grad_win, ("head", "blk"), scatter_dimension=0, tiled=True),
        lax.psum_scatter(grad_down, ("head", "blk"), scatter_dimension=1, tiled=True),
    )
    return (y_out, dx_out, summed[0], summed[1], summed[2], summed[3], summed[4], summed[5])


def solution(mesh):
    return jax.shard_map(
        shards,
        mesh=mesh,
        in_specs=(
            P(("head", "blk"), None),
            P(("head", "blk"), None),
            P(),
            P(("head", "blk")),
            P(("head", "blk"), None),
            P(("head", "blk"), None),
            P(("head", "blk")),
            P(("head", "blk"), None),
            P(None, ("head", "blk")),
        ),
        out_specs=(
            P(("head", "blk"), None),
            P(("head", "blk"), None),
            P(("head", "blk")),
            P(("head", "blk"), None),
            P(("head", "blk"), None),
            P(("head", "blk")),
            P(("head", "blk"), None),
            P(None, ("head", "blk")),
        ),
        check_vma=False,
    )
```

profile of v0, /device:TPU:0, one launch (start us, length us, event | category | flops | bytes accessed | tf_op | source)
XLA Modules:
  0.0 1423.2 jit_solution(2221315387794891188)
XLA Ops:
  9.7 43.0 %all-reduce.5 = (bf16[1024]{0:T(1024)(128)(2,1)S(1)}, bf16[1024]{0:T(1024)(128)(2,1)S(1)}) all-reduce(bf16[1024]{0:T(1024)(128)(2,1)S(1)} %dynamic-update-slice, bf16[1024]{0:T(1024)(128)(2,1)S(1)} %dynamic-update-slice.1), channel_id=1, replica_groups=mesh['head'=4,'blk'=8] {'head','blk'}, use_global_device_ids=true, to_apply=%add | all-reduce | flops 2048 | bytes 8192
  58.1 25.4 %all-gather.9.cloned.1.call-done = bf16[1024,3072]{1,0:T(8,128)(2,1)} async-done(((bf16[32,3072]{1,0:T(8,128)(2,1)}), bf16[1024,3072]{1,0:T(8,128)(2,1)}) %all-gather.9.cloned.1.call-update) | async-done | bytes 6291472 | tf_op jit(solution)/shard_map/all_gather | solution.py:122
  83.5 5.5 fusion.107
  89.5 14.1 all_to_all.59
  107.2 69.6 %all-gather.21.cloned.1.call-done = bf16[4096,2,1,256]{3,0,1,2:T(8,128)(2,1)} async-done(((bf16[512,2,1,256]{3,0,1,2:T(8,128)(2,1)}), bf16[4096,2,1,256]{3,0,1,2:T(8,128)(2,1)}) %all-gather.21.cloned.1.call-update) | async-done | bytes 4194320 | tf_op jit(solution)/shard_map/all_gather | solution.py:164
  176.8 6.4 copy.132
  183.2 83.1 %while.39 = (s32[]{:T(128)}, f32[4,512]{1,0:T(4,128)S(1)}, f32[4,512]{1,0:T(4,128)S(1)}, f32[512,4,64]{0,2,1:T(8,128)S(1)}, s32[512]{0:T(512)S(1)}, /*index=5*/s...) while((s32[]{:T(128)}, f32[4,512]{1,0:T(4,128)S(1)}, ...), condition=%wide.region_10.11_spmd.clone, body=%wide.region_7.10_spmd.clone.sunk | while | flops 282734592 | bytes 33431812 | solution.py:176
  271.5 6.5 all-to-all-done.1
  280.3 46.5 %all-gather.13.cloned.1.call-done = bf16[1024,5248]{1,0:T(8,128)(2,1)} async-done(((bf16[32,5248]{1,0:T(8,128)(2,1)}), bf16[1024,5248]{1,0:T(8,128)(2,1)}) %all-gather.13.cloned.1.call-update) | async-done | bytes 10747920 | tf_op jit(solution)/shard_map/all_gather | solution.py:125
  326.8 7.2 fusion.109
  334.0 60.3 %all-gather.15.cloned.1.call-done = bf16[2624,1024]{0,1:T(8,128)(2,1)} async-done(((bf16[2624,32]{0,1:T(8,128)(2,1)}), bf16[2624,1024]{0,1:T(8,128)(2,1)}) %all-gather.15.cloned.1.call-update) | async-done | bytes 5373968 | tf_op jit(solution)/shard_map/all_gather | solution.py:126
  394.3 7.3 add_convert_fusion
  407.8 9.1 all_to_all.60
  424.4 31.0 %all_gather.42 = f32[4096,4]{0,1:T(4,128)S(1)} all-gather(f32[512,4]{0,1:T(4,128)S(1)} %bitcast.236), channel_id=1, replica_groups=mesh['head'=4,'blk'=8] {'blk'}, dimensions={0}, use_global_device_ids=true | all-gather | bytes 73728 | tf_op jit(solution)/shard_map/all_gather | solution.py:246
  455.5 5.8 fusion.103
  463.3 30.8 %all_gather.44 = f32[4096,4]{0,1:T(4,128)S(1)} all-gather(f32[512,4]{0,1:T(4,128)S(1)} %multiply_reduce_fusion.1), channel_id=1, replica_groups=mesh['head'=4,'blk'=8] {'blk'}, dimensions={0}, use_global_device_ids=true | all-gather | bytes 73728 | tf_op jit(solution)/shard_map/all_gather | solution.py:247
  494.2 82.9 %while.40 = (s32[]{:T(128)}, f32[512,4,64]{0,2,1:T(8,128)}, s32[8]{0:T(128)S(1)}, bf16[4096,2,256]{0,2,1:T(8,128)(2,1)}, s32[512]{0:T(512)S(1)}, /*index=5*/s32[...) while((s32[]{:T(128)}, f32[512,4,64]{0,2,1:T(8,128)}, ...), condition=%wide.region_17.18_spmd.clone, body=%wide.region_16.17_spmd.clone.sunk | while | flops 409600000 | bytes 12345585 | solution.py:240
  509.8 5.0 fusion.175
  520.1 5.0 fusion.175
  530.5 5.0 fusion.175
  540.9 5.0 fusion.175
  551.3 5.0 fusion.175
  572.0 5.0 fusion.175
  578.2 116.7 %while.41 = (s32[]{:T(128)}, f32[512,4,64]{0,2,1:T(8,128)}, f32[512,4,64]{0,2,1:T(8,128)}, s32[8]{0:T(128)S(1)}, bf16[4096,4,64]{0,2,1:T(8,128)(2,1)}, /*index=5...) while((s32[]{:T(128)}, f32[512,4,64]{0,2,1:T(8,128)}, ...), condition=%wide.region_19.20_spmd.clone, body=%wide.region_18.19_spmd.clone.sunk | while | flops 548274176 | bytes 21301032 | solution.py:265
  700.4 23.2 %all_to_all.61 = bf16[512,3,1,256]{3,1,2,0:T(4,128)(2,1)S(1)} all-to-all(bf16[512,3,1,256]{3,1,2,0:T(4,128)(2,1)} %copy.141), channel_id=1, replica_groups=mesh['head'=4,'blk'=8] {'head'}, dimensions={0} | all-to-all | bytes 1572864 | tf_op jit(solution)/shard_map/all_to_all | solution.py:279
  730.5 6.7 fusion.105
  738.3 10.3 fusion.56
  749.2 5.3 fusion.55
  754.6 5.7 fusion.69
  760.3 39.8 %all-reduce.4 = (f32[1024]{0:T(1024)S(1)}, f32[1024]{0:T(1024)S(1)}) all-reduce(f32[1024]{0:T(1024)S(1)} %get-tuple-element.440, f32[1024]{0:T(1024)S(1)} %copy-done.19), channel_id=3, replica_groups=mesh['head'=4,'blk'=8] {'head','blk'}, use_global_device_ids=true, to_apply=%region_23.24.clone | all-reduce | flops 2048 | bytes 16384
  802.4 156.2 %reduce-scatter.5.cloned.1.call-done = f32[32,3072]{1,0:T(8,128)} async-done(((f32[1024,3072]{1,0:T(8,128)}), f32[32,3072]{1,0:T(8,128)}) %reduce-scatter.5.cloned.1.call-update) | async-done | bytes 393232 | tf_op jit(solution)/shard_map/reduce_scatter | solution.py:298
  958.6 457.6 %reduce-scatter.9.cloned.1.call-done = f32[32,5248]{1,0:T(8,128)} async-done(((f32[1024,5248]{1,0:T(8,128)}), f32[32,5248]{1,0:T(8,128)}) %reduce-scatter.9.cloned.1.call-update) | async-done | bytes 671760 | tf_op jit(solution)/shard_map/reduce_scatter | solution.py:301
  (373 shorter events, 288.2 us)
Async XLA Ops:
  7.2 76.3 %all-gather.9.cloned.1.call-start = ((), (), s32[]{:S(2)}) async-start(), calls=%async_computation.8 | async-start | bytes 6488064 | tf_op jit(solution)/shard_map/all_gather | solution.py:122
  7.9 168.9 %all-gather.21.cloned.1.call-start = ((), (), s32[]{:S(2)}) async-start(), calls=%async_computation.18 | async-start | bytes 4718592 | tf_op jit(solution)/shard_map/all_gather | solution.py:164
  104.9 166.6 %all-gather.11.cloned.1.call-start = ((), (), s32[]{:S(2)}) async-start(), calls=%async_computation.9 | async-start | bytes 2162688 | tf_op jit(solution)/shard_map/all_gather | solution.py:123
  105.6 221.2 %all-gather.13.cloned.1.call-start = ((), (), s32[]{:S(2)}) async-start(), calls=%async_computation.10 | async-start | bytes 11083776 | tf_op jit(solution)/shard_map/all_gather | solution.py:125
  106.2 288.1 %all-gather.15.cloned.1.call-start = ((), (), s32[]{:S(2)}) async-start(), calls=%async_computation.11 | async-start | bytes 5677056 | tf_op jit(solution)/shard_map/all_gather | solution.py:126
  266.3 4.4 copy-start.1
  266.3 13.7 copy-start.11
  266.4 11.6 copy-start.4
  267.2 10.7 all-to-all-start.1
  270.6 307.5 %all-gather.17.cloned.1.call-start = ((), (), s32[]{:S(2)}) async-start(), calls=%async_computation.12 | async-start | bytes 2359296 | tf_op jit(solution)/shard_map/all_gather | solution.py:244
  270.7 184.8 %copy-start.17 = (f32[128]{0:T(128)}, f32[128]{0:T(128)S(1)}, u32[]{:S(2)}) copy-start(f32[128]{0:T(128)S(1)} %compare_convert_fusion) | copy-start | bytes 1540
  271.2 307.0 %all-gather.19.cloned.1.call-start = ((), (), s32[]{:S(2)}) async-start(), calls=%async_computation.13 | async-start | bytes 2359296 | tf_op jit(solution)/shard_map/all_gather | solution.py:245
  280.3 114.0 %copy-start.13 = (bf16[128,1024]{1,0:T(8,128)(2,1)S(1)}, bf16[128,1024]{1,0:T(8,128)(2,1)}, u32[]{:S(2)}) copy-start(bf16[128,1024]{1,0:T(8,128)(2,1)} %param.16) | copy-start | bytes 786436
  394.3 7.3 copy-start.5
  394.3 8.2 copy-start.3
  402.2 4.5 copy-start.9
  402.5 4.5 copy-start.6
  418.9 383.5 %reduce-scatter.7.cloned.1.call-start = ((), (), s32[]{:S(2)}) async-start(), calls=%async_computation.15 | async-start | bytes 4325376 | tf_op jit(solution)/shard_map/reduce_scatter | solution.py:299
  421.7 380.7 %reduce-scatter.11.cloned.1.call-start = ((), (), s32[]{:S(2)}) async-start(), calls=%async_computation.17 | async-start | bytes 11354112 | tf_op jit(solution)/shard_map/reduce_scatter | solution.py:302
  461.2 32.9 %copy-start.2 = (bf16[512,4,64]{0,2,1:T(8,128)(2,1)S(1)}, bf16[512,4,64]{0,2,1:T(8,128)(2,1)}, u32[]{:S(2)}) copy-start(bf16[512,4,64]{0,2,1:T(8,128)(2,1)} %copy-done.1) | copy-start | bytes 786436
  461.3 497.3 %reduce-scatter.5.cloned.1.call-start = ((), (), s32[]{:S(2)}) async-start(), calls=%async_computation.14 | async-start | bytes 12976128 | tf_op jit(solution)/shard_map/reduce_scatter | solution.py:298
  588.0 4.5 copy-start.16
  602.3 4.7 copy-start.16
  616.7 4.7 copy-start.16
  631.2 4.7 copy-start.16
  645.6 4.7 copy-start.16
  660.3 4.9 copy-start.16
  675.3 4.9 copy-start.16
  690.2 4.7 copy-start.16
  737.2 679.1 %reduce-scatter.9.cloned.1.call-start = ((), (), s32[]{:S(2)}) async-start(), calls=%async_computation.16 | async-start | bytes 22167552 | tf_op jit(solution)/shard_map/reduce_scatter | solution.py:301
  749.2 5.3 copy-start.8
  754.6 5.8 copy-start.19
  (21 other events, 65.0 us)
Sparse Core Ops, SparseCore 0:
  10.9 72.5 all-gather.8
  105.0 71.7 all-gather.20
  179.8 54.8 all-gather.10
  237.4 89.4 all-gather.12
  329.6 64.6 all-gather.14
  396.8 50.7 all-gather.16
  449.7 49.6 all-gather.18
  502.2 142.2 reduce-scatter.6
  651.0 146.7 reduce-scatter.10
  804.2 154.3 reduce-scatter.4
  961.6 454.5 reduce-scatter.8
where the time goes:
time: 1430 us; the launch traced here: 1420 us
  waiting for transfers between devices  825 us (58%)
  matrix products  263 us (18%)
  blocking collectives  191 us (13%)
  local copies, waits for them, and re-layouts  61.3 us (4%)
  other arithmetic  46.9 us (3%)
  loops' own time  16.5 us (1%)
  between operations  14.8 us (1%)
    reduce_scatter x1, waiting for transfers between devices, shards(): lax.psum_scatter(grad_win, ('head', 'blk'), scatter_dimension=0, tiled=True)  458 us
    reduce_scatter x1, waiting for transfers between devices, shards(): lax.psum_scatter(grad_wqkv, ('head', 'blk'), scatter_dimension=0, tiled=T...  156 us
    unnamed x2, blocking collectives  82.9 us
    all_gather x1, waiting for transfers between devices, shards(): key_part = lax.all_gather(key_value, 'blk', axis=0, tiled=True)  69.6 us
    all_gather x1, waiting for transfers between devices, shards(): lax.all_gather(w_mlp_out, ('head', 'blk'), axis=1, tiled=True)  60.3 us
    dot_general x16, matrix products, score_grads(): jnp.einsum('qhd,khd->hqk', query_in, key_in, preferred_element_type=jnp.f...  51.3 us
    all_gather x1, waiting for transfers between devices, shards(): lax.all_gather(w_in, ('head', 'blk'), axis=0, tiled=True)  46.5 us
    dot_general x8, matrix products, query_one_step(): jnp.einsum('hqk,khd->qhd', grad_scores, keys_in, preferred_element_type=j...  40.1 us
  transfers between devices with their start and end apart: 12, of which 7 were waited for; matrix products, arithmetic and copies ran while one was open for 25% of the time, Pallas kernels for 0%

commit v1 on v0

v1 whole, which is shorter than its diff:
```python
import functools
import math

import jax
import jax.numpy as jnp
from jax import lax
from jax.experimental import pallas as pl
from jax.experimental.pallas import tpu as pltpu
from jax.sharding import PartitionSpec as P

DH = 64
ROPE_BASE = 160000.0
NORM_EPS = 1e-05
MASK_FLOOR = -1e30
KEY_BLOCK = 512
EXP_SCALE = 0.125 * math.log2(math.e)
BF16 = jnp.bfloat16
F32 = jnp.float32
MESH_ID = pl.DeviceIdType.MESH
ANY = pl.BlockSpec(memory_space=pl.ANY)
VM = pl.BlockSpec(memory_space=pltpu.VMEM)


def dims():
    nh = lax.axis_size("head")
    nb = lax.axis_size("blk")
    return nh, nb


def me():
    return lax.axis_index("head"), lax.axis_index("blk")


def comm_call(body, name, cid, out_shape, in_specs, out_specs, scratch, args, vmem=None):
    return pl.pallas_call(
        body,
        out_shape=out_shape,
        in_specs=in_specs,
        out_specs=out_specs,
        scratch_shapes=scratch,
        name=name,
        compiler_params=pltpu.CompilerParams(
            collective_id=cid, has_side_effects=True, vmem_limit_bytes=vmem
        ),
    )(*args)


def remote(src, dst, send, recv, h, b):
    return pltpu.make_async_remote_copy(
        src_ref=src,
        dst_ref=dst,
        send_sem=send,
        recv_sem=recv,
        device_id=(h, b),
        device_id_type=MESH_ID,
    )


def barrier_with(peers):
    sem = pltpu.get_barrier_semaphore()
    for h, b in peers:
        pl.semaphore_signal(sem, inc=1, device_id=(h, b), device_id_type=MESH_ID)
    pl.semaphore_wait(sem, len(peers))


def barrier_all(nh, nb, h, b):
    sem = pltpu.get_barrier_semaphore()

    @pl.loop(1, nh * nb)
    def _(i):
        pl.semaphore_signal(
            sem,
            inc=1,
            device_id=((h + i // nb) % nh, (b + i % nb) % nb),
            device_id_type=MESH_ID,
        )

    pl.semaphore_wait(sem, nh * nb - 1)


def head_peers(nh, h, b):
    return [((h + i) % nh, b) for i in range(1, nh)]


class HeadGather:
    def __init__(self, nh, h, b, src, dst, sems):
        self.nh, self.h, self.b, self.dst, self.sems = nh, h, b, dst, sems
        nx = nh // 2
        self.nx = nx
        x, c = h // 2, h % 2
        sib = x * 2 + 1 - c
        self.sib = sib
        self.across = []
        for k in range(1, nx):
            self.across.append(
                remote(src, dst.at[h], sems.at[0, k], sems.at[1, k], ((x + k) % nx) * 2 + c, b)
            )
        self.near = remote(src, dst.at[h], sems.at[0, 0], sems.at[1, 0], sib, b)
        self.local = pltpu.make_async_copy(src, dst.at[h], sems.at[2, 0])
        self.forward = []
        for k in range(1, nx):
            got = ((x + nx - k) % nx) * 2 + c
            self.forward.append(
                remote(dst.at[got], dst.at[got], sems.at[2, k], sems.at[3, k], sib, b)
            )

    @staticmethod
    def sem_shape(nh):
        return pltpu.SemaphoreType.DMA((4, nh // 2))

    def start(self):
        for cp in self.across:
            cp.start()
        self.near.start()
        self.local.start()

    def pass_on(self):
        for cp, fw in zip(self.across, self.forward):
            cp.wait_recv()
            fw.start()

    def finish(self):
        for cp in self.across:
            cp.wait_send()
        self.near.wait()
        self.local.wait()
        for fw in self.forward:
            fw.wait()


def first_body(nh, nb, x_ref, g_ref, wq_ref, wo_ref, wm_ref, xg, gg, wq_all, wo_all, wm_h, xs, gs, qsem, osem, msem, lsem):
    h, b = me()
    barrier_all(nh, nb, h, b)
    own = h * nb + b
    gx = HeadGather(nh, h, b, x_ref, xg, xs)
    gg_ = HeadGather(nh, h, b, g_ref, gg, gs)
    gx.start()

    def wq_copy(i):
        th, tb = (h + i // nb) % nh, (b + i % nb) % nb
        return remote(wq_ref.at[th], wq_all.at[own], qsem.at[0, i], qsem.at[1, i], th, tb)

    def wo_copy(i):
        return remote(wo_ref, wo_all.at[b], osem.at[0, i], osem.at[1, i], h, (b + i) % nb)

    @pl.loop(1, nh * nb)
    def _(i):
        wq_copy(i).start()

    lq = pltpu.make_async_copy(wq_ref.at[h], wq_all.at[own], lsem.at[0])
    lo = pltpu.make_async_copy(wo_ref, wo_all.at[b], lsem.at[1])
    lm = pltpu.make_async_copy(wm_ref.at[h], wm_h.at[h], lsem.at[2])
    for cp in (lq, lo, lm):
        cp.start()
    mcs = [
        remote(wm_ref.at[(h + i) % nh], wm_h.at[h], msem.at[0, i], msem.at[1, i], (h + i) % nh, b)
        for i in range(1, nh)
    ]
    for cp in mcs:
        cp.start()
    gx.pass_on()
    gg_.start()

    @pl.loop(1, nb)
    def _(i):
        wo_copy(i).start()

    gg_.pass_on()
    gx.finish()
    gg_.finish()
    for cp in (lq, lo, lm):
        cp.wait()
    for cp in mcs:
        cp.wait()

    @pl.loop(1, nh * nb)
    def _(i):
        wq_copy(i).wait()

    @pl.loop(1, nb)
    def _(i):
        wo_copy(i).wait()


def first_exchange(x, g, wq, wo, wm):
    nh, nb = dims()
    rows, width = x.shape
    own_rows = wq.shape[1]
    shapes = (
        jax.ShapeDtypeStruct((nh, rows, width), BF16),
        jax.ShapeDtypeStruct((nh, rows, width), BF16),
        jax.ShapeDtypeStruct((nh * nb, own_rows, wq.shape[2]), BF16),
        jax.ShapeDtypeStruct((nb,) + wo.shape, BF16),
        jax.ShapeDtypeStruct(wm.shape, BF16),
    )
    dma = pltpu.SemaphoreType.DMA
    return comm_call(
        functools.partial(first_body, nh, nb),
        "first_exchange",
        0,
        shapes,
        [ANY] * 5,
        [ANY] * 5,
        [
            HeadGather.sem_shape(nh),
            HeadGather.sem_shape(nh),
            dma((2, nh * nb)),
            dma((2, nb)),
            dma((2, nh)),
            dma((3,)),
        ],
        (x, g, wq, wo, wm),
    )


class Place:
    def __init__(self, nh, nb, hl):
        h, b = me()
        self.h, self.b, self.hl = h, b, hl
        self.x, self.c = h // 2, h % 2
        self.cb = nb // (2 * hl)
        self.qs = 2 * self.cb
        self.nz = nb // self.qs
        self.sib = self.x * 2 + 1 - self.c
        self.split = b % self.qs
        self.zi = b // self.qs
        self.t = b // self.cb
        self.u = b % self.cb
        self.my_l = self.t // 2
        self.my_src_h = self.x * 2 + self.t % 2

    def query_dest(self, l):
        return self.x * 2 + self.split % 2, (2 * l + self.c) * self.cb + self.split // 2

    def query_source(self, zi):
        return self.my_src_h, zi * self.qs + self.u * 2 + self.c


def barrier_plane(pc, nb):
    sem = pltpu.get_barrier_semaphore()

    @pl.loop(0, nb)
    def _(i):
        pl.semaphore_signal(
            sem, inc=1, device_id=(pc.sib, (pc.b + i) % nb), device_id_type=MESH_ID
        )

    @pl.loop(1, nb)
    def _(i):
        pl.semaphore_signal(sem, inc=1, device_id=(pc.h, (pc.b + i) % nb), device_id_type=MESH_ID)

    pl.semaphore_wait(sem, 2 * nb - 1)


def routed(pc, src, dst, send, recv, th, tb, act):
    mine = jnp.logical_and(th == pc.h, tb == pc.b)

    @pl.when(mine)
    def _():
        if act == "start":
            pltpu.make_async_copy(src, dst, recv).start()

    @pl.when(jnp.logical_not(mine))
    def _():
        cp = remote(src, dst, send, recv, th, tb)
        if act == "start":
            cp.start()
        else:
            cp.wait_send()


def wait_on(ref, sem):
    pltpu.make_async_copy(ref, ref, sem).wait()


def queries_out(pc, q_ref, qin, qsem, act):
    for l in range(pc.hl):
        th, tb = pc.query_dest(l)
        routed(pc, q_ref.at[l], qin.at[pc.zi], qsem.at[0, l], qsem.at[1, pc.zi], th, tb, act)


def queries_back(pc, o_ref, og, osem, act):
    for zi in range(pc.nz):
        th, tb = pc.query_source(zi)
        routed(pc, o_ref.at[zi], og.at[pc.my_l], osem.at[0, zi], osem.at[1, pc.my_l], th, tb, act)


def to_heads_body(nh, nb, hl, q_ref, kv_ref, qin, kvin, qsem, ksem, fsem):
    pc = Place(nh, nb, hl)
    barrier_plane(pc, nb)
    core = pc.b % 2

    def keys_out(act):
        for l in range(hl):
            for u in range(pc.cb):
                routed(
                    pc,
                    kv_ref.at[l],
                    kvin.at[:, pc.b],
                    ksem.at[0, l * pc.cb + u],
                    ksem.at[1, pc.b // 2],
                    pc.x * 2 + core,
                    (2 * l + pc.c) * pc.cb + u,
                    act,
                )

    keys_out("start")
    queries_out(pc, q_ref, qin, qsem, "start")

    def forward(k):
        at = kvin.at[:, 2 * k + pc.c]
        return remote(at, at, fsem.at[0, k], fsem.at[1, k], pc.sib, pc.b)

    @pl.loop(0, nb // 2)
    def _(k):
        wait_on(kvin.at[:, 2 * k + pc.c], ksem.at[1, k])
        forward(k).start()

    keys_out("wait_send")
    queries_out(pc, q_ref, qin, qsem, "wait_send")
    for zi in range(pc.nz):
        wait_on(qin.at[zi], qsem.at[1, zi])

    @pl.loop(0, nb // 2)
    def _(k):
        forward(k).wait()


def to_heads(q, kv):
    nh, nb = dims()
    hl, _, group = q.shape
    cb = nb // (2 * hl)
    nz = nb // (2 * cb)
    rows = group // nh
    dma = pltpu.SemaphoreType.DMA
    return comm_call(
        functools.partial(to_heads_body, nh, nb, hl),
        "to_heads",
        1,
        (
            jax.ShapeDtypeStruct((nz, DH, group), BF16),
            jax.ShapeDtypeStruct((nh, nb, rows, 2 * DH), BF16),
        ),
        [ANY] * 2,
        [ANY] * 2,
        [dma((2, max(hl, nz))), dma((2, max(hl * cb, nb // 2))), dma((2, nb // 2))],
        (q, kv),
    )


def move_body(nh, nb, hl, outward, q_ref, qin, qsem):
    pc = Place(nh, nb, hl)
    barrier_plane(pc, nb)
    fn = queries_out if outward else queries_back
    fn(pc, q_ref, qin, qsem, "start")
    fn(pc, q_ref, qin, qsem, "wait_send")
    for i in range(pc.nz if outward else hl):
        wait_on(qin.at[i], qsem.at[1, i])


def move_queries(q, hl, outward, cid):
    nh, nb = dims()
    nz = nb // (2 * (nb // (2 * hl)))
    count = nz if outward else hl
    return comm_call(
        functools.partial(move_body, nh, nb, hl, outward),
        "queries_out" if outward else "queries_back",
        cid,
        jax.ShapeDtypeStruct((count,) + q.shape[1:], BF16),
        [ANY],
        ANY,
        [pltpu.SemaphoreType.DMA((2, max(hl, nz)))],
        (q,),
    )


def grads_back_body(nh, nb, hl, dq_ref, dkv_ref, dq_out, dkv_out, got, sums, qsem, psem, ksem):
    pc = Place(nh, nb, hl)
    barrier_plane(pc, nb)

    def pair(k):
        return remote(
            dkv_ref.at[:, 2 * k + 1 - pc.c], got.at[k], psem.at[0, k], psem.at[1, k], pc.sib, pc.b
        )

    def back(k, act):
        routed(
            pc,
            sums.at[k],
            dkv_out.at[pc.my_l, pc.u],
            ksem.at[0, k],
            ksem.at[1, pc.my_l * pc.cb + pc.u],
            pc.my_src_h,
            2 * k + pc.c,
            act,
        )

    half = nb // 2

    @pl.loop(0, half)
    def _(k):
        pair(k).start()

    queries_back(pc, dq_ref, dq_out, qsem, "start")

    @pl.loop(0, half)
    def _(k):
        pair(k).wait_recv()
        sums[k] = (dkv_ref[:, 2 * k + pc.c].astype(F32) + got[k].astype(F32)).astype(BF16)
        back(k, "start")

    @pl.loop(0, half)
    def _(k):
        pair(k).wait_send()
        back(k, "wait_send")

    queries_back(pc, dq_ref, dq_out, qsem, "wait_send")
    for l in range(hl):
        wait_on(dq_out.at[l], qsem.at[1, l])
        for u in range(pc.cb):
            wait_on(dkv_out.at[l, u], ksem.at[1, l * pc.cb + u])


def grads_back(dq, dkv, hl):
    nh, nb = dims()
    cb = nb // (2 * hl)
    nz = nb // (2 * cb)
    rows = dkv.shape[2]
    dma = pltpu.SemaphoreType.DMA
    return comm_call(
        functools.partial(grads_back_body, nh, nb, hl),
        "grads_back",
        2,
        (
            jax.ShapeDtypeStruct((hl,) + dq.shape[1:], BF16),
            jax.ShapeDtypeStruct((hl, cb, nh, rows, 2 * DH), BF16),
        ),
        [ANY, VM],
        [ANY, ANY],
        [
            pltpu.VMEM((nb // 2, nh, rows, 2 * DH), BF16),
            pltpu.VMEM((nb // 2, nh, rows, 2 * DH), BF16),
            dma((2, max(hl, nz))),
            dma((2, nb // 2)),
            dma((2, max(hl * cb, nb // 2))),
        ],
        (dq, dkv),
        vmem=40 << 20,
    )


def query_tile(ref):
    return jnp.concatenate([ref[0], ref[1]], axis=1)


def allowed(block_at, first_ref, last_ref, lanes):
    at = block_at * KEY_BLOCK + lax.broadcasted_iota(jnp.int32, (KEY_BLOCK, lanes), 0)
    return jnp.logical_and(at >= first_ref[0], at < last_ref[0])


def attend_body(lo_ref, hi_ref, q_ref, kv_ref, first_ref, last_ref, o_ref, of_ref, lse_ref):
    tile = pl.program_id(0)
    q = query_tile(q_ref)
    lanes = q.shape[1]
    q_pad = jnp.concatenate([q, jnp.zeros_like(q)], axis=0)

    def step(j, carry):
        top, total, acc = carry
        kv = kv_ref[pl.ds(pl.multiple_of(j * KEY_BLOCK, KEY_BLOCK), KEY_BLOCK), :]
        s = jnp.dot(kv, q_pad, preferred_element_type=F32)
        s = jnp.where(allowed(j, first_ref, last_ref, lanes), s, MASK_FLOOR)
        new_top = jnp.maximum(top, jnp.max(s, axis=0, keepdims=True))
        p = jnp.exp2((s - new_top) * EXP_SCALE)
        alpha = jnp.exp2((top - new_top) * EXP_SCALE)
        total = total * alpha + jnp.sum(p, axis=0, keepdims=True)
        acc = acc * alpha + lax.dot_general(
            kv, p.astype(BF16), (((0,), (0,)), ((), ())), preferred_element_type=F32
        )
        return new_top, total, acc

    top, total, acc = lax.fori_loop(
        lo_ref[tile],
        hi_ref[tile],
        step,
        (
            jnp.full((1, lanes), MASK_FLOOR, F32),
            jnp.zeros((1, lanes), F32),
            jnp.zeros((2 * DH, lanes), F32),
        ),
    )
    o = acc[DH:] / total
    half = lanes // 2
    for i in range(2):
        part = o[:, i * half : (i + 1) * half]
        of_ref[i] = part
        o_ref[i] = part.astype(BF16)
    lse_ref[0] = top * EXP_SCALE + jnp.log2(total)


def attend_specs(kv_rows, rows, pairs):
    tile_spec = pl.BlockSpec((2, DH, rows), lambda i, *_: (i % pairs, 0, i // pairs))
    row_spec = pl.BlockSpec((1, 1, 2 * rows), lambda i, *_: (i, 0, 0))
    kv_spec = pl.BlockSpec((kv_rows, 2 * DH), lambda i, *_: (0, 0))
    return tile_spec, row_spec, kv_spec


def attend(q, kv, first, last, lo, hi, rows):
    nz, _, group = q.shape
    tiles = lo.shape[0]
    tile_spec, row_spec, kv_spec = attend_specs(kv.shape[0], rows, nz // 2)
    return pl.pallas_call(
        attend_body,
        grid_spec=pltpu.PrefetchScalarGridSpec(
            num_scalar_prefetch=2,
            grid=(tiles,),
            in_specs=[tile_spec, kv_spec, row_spec, row_spec],
            out_specs=[tile_spec, tile_spec, row_spec],
        ),
        out_shape=(
            jax.ShapeDtypeStruct(q.shape, BF16),
            jax.ShapeDtypeStruct(q.shape, F32),
            jax.ShapeDtypeStruct((tiles, 1, 2 * rows), F32),
        ),
        name="attend",
        compiler_params=pltpu.CompilerParams(vmem_limit_bytes=48 << 20),
    )(lo, hi, q, kv, first, last)


def attend_grad_body(lo_ref, hi_ref, q_ref, do_ref, of_ref, kv_ref, first_ref, last_ref, lse_ref, dq_ref, dkv_ref, acc_ref):
    tile = pl.program_id(0)

    @pl.when(tile == 0)
    def _():
        acc_ref[...] = jnp.zeros_like(acc_ref)

    q = query_tile(q_ref)
    do = query_tile(do_ref)
    lanes = q.shape[1]
    zero = jnp.zeros_like(q)
    both = jnp.concatenate(
        [jnp.concatenate([q, zero], axis=0), jnp.concatenate([zero, do], axis=0)], axis=1
    )
    delta = jnp.sum(do.astype(F32) * query_tile(of_ref), axis=0, keepdims=True)
    lse = lse_ref[0]

    def step(j, dq):
        at = pl.ds(pl.multiple_of(j * KEY_BLOCK, KEY_BLOCK), KEY_BLOCK)
        kv = kv_ref[at, :]
        sd = jnp.dot(kv, both, preferred_element_type=F32)
        s, dp = sd[:, :lanes], sd[:, lanes:]
        p = jnp.exp2(
            jnp.where(
                allowed(j, first_ref, last_ref, lanes), s * EXP_SCALE - lse, MASK_FLOOR
            )
        )
        ds = (p * (dp - delta)).astype(BF16)
        acc_ref[at, :] += lax.dot_general(
            jnp.concatenate([ds, p.astype(BF16)], axis=1),
            both,
            (((1,), (1,)), ((), ())),
            preferred_element_type=F32,
        )
        return dq + lax.dot_general(
            kv, ds, (((0,), (0,)), ((), ())), preferred_element_type=F32
        )

    dq = lax.fori_loop(lo_ref[tile], hi_ref[tile], step, jnp.zeros((2 * DH, lanes), F32))
    half = lanes // 2
    for i in range(2):
        dq_ref[i] = (dq[:DH, i * half : (i + 1) * half] * 0.125).astype(BF16)

    @pl.when(tile == pl.num_programs(0) - 1)
    def _():
        lane = lax.broadcasted_iota(jnp.int32, (1, 2 * DH), 1)
        dkv_ref[...] = (acc_ref[...] * jnp.where(lane < DH, 0.125, 1.0)).astype(BF16)


def attend_grad(q, do, of, kv, first, last, lse, lo, hi, rows):
    nz, _, group = q.shape
    tiles = lo.shape[0]
    tile_spec, row_spec, kv_spec = attend_specs(kv.shape[0], rows, nz // 2)
    return pl.pallas_call(
        attend_grad_body,
        grid_spec=pltpu.PrefetchScalarGridSpec(
            num_scalar_prefetch=2,
            grid=(tiles,),
            in_specs=[tile_spec, tile_spec, tile_spec, kv_spec, row_spec, row_spec, row_spec],
            out_specs=[tile_spec, kv_spec],
            scratch_shapes=[pltpu.VMEM(kv.shape, F32)],
        ),
        out_shape=(jax.ShapeDtypeStruct(q.shape, BF16), jax.ShapeDtypeStruct(kv.shape, BF16)),
        name="attend_grad",
        compiler_params=pltpu.CompilerParams(vmem_limit_bytes=56 << 20),
    )(lo, hi, q, do, of, kv, first, last, lse)


class HeadSum:
    def __init__(self, nh, h, b, part, near, far, out, sems):
        self.nx = nh // 2
        self.x, self.c = h // 2, h % 2
        self.h, self.part, self.near, self.far, self.out = h, part, near, far, out
        sib = self.x * 2 + 1 - self.c
        self.pairs = [
            remote(
                part.at[((self.x + k) % self.nx) * 2 + 1 - self.c],
                near.at[k],
                sems.at[0, k],
                sems.at[1, k],
                sib,
                b,
            )
            for k in range(self.nx)
        ]
        self.across = [
            remote(
                out.at[k],
                far.at[k],
                sems.at[2, k],
                sems.at[3, k],
                ((self.x + k) % self.nx) * 2 + self.c,
                b,
            )
            for k in range(1, self.nx)
        ]

    @staticmethod
    def sem_shape(nh):
        return pltpu.SemaphoreType.DMA((4, nh // 2))

    @staticmethod
    def buffers(nh, rows, width):
        return [pltpu.VMEM((nh // 2, rows, width), BF16)] * 3

    def start(self):
        for k in list(range(1, self.nx)) + [0]:
            self.pairs[k].start()

    def send(self):
        for k in range(1, self.nx):
            self.pairs[k].wait_recv()
            at = ((self.x + k) % self.nx) * 2 + self.c
            self.out[k] = (self.part[at].astype(F32) + self.near[k].astype(F32)).astype(BF16)
            self.across[k - 1].start()

    def total(self):
        self.pairs[0].wait_recv()
        total = self.part[self.h].astype(F32) + self.near[0].astype(F32)
        for k in range(1, self.nx):
            self.across[k - 1].wait_recv()
            total = total + self.far[k].astype(F32)
        return total

    def finish(self):
        for cp in self.pairs:
            cp.wait_send()
        for cp in self.across:
            cp.wait_send()


def norm_of(values):
    centre = values - jnp.mean(values, axis=-1, keepdims=True)
    scale = lax.rsqrt(jnp.mean(centre * centre, axis=-1, keepdims=True) + NORM_EPS)
    return centre * scale, scale


def norm_pull(grad, normed, scale):
    one = jnp.mean(grad, axis=-1, keepdims=True)
    two = jnp.mean(grad * normed, axis=-1, keepdims=True)
    return scale * (grad - one - normed * two)


def mid_body(nh, part, x_ref, hid_ref, ng_ref, near, far, out, nbuf, ssem, gsem):
    h, b = me()
    barrier_with(head_peers(nh, h, b))
    hs = HeadSum(nh, h, b, part, near, far, out, ssem)
    hs.start()
    hs.send()
    hid = x_ref[...].astype(F32) + hs.total()
    hid_ref[...] = hid
    nbuf[...] = norm_of(hid)[0].astype(BF16)
    hg = HeadGather(nh, h, b, nbuf, ng_ref, gsem)
    hg.start()
    hg.pass_on()
    hs.finish()
    hg.finish()


def mid_exchange(part, x):
    nh, _ = dims()
    rows, width = x.shape
    return comm_call(
        functools.partial(mid_body, nh),
        "mid_exchange",
        3,
        (jax.ShapeDtypeStruct(x.shape, F32), jax.ShapeDtypeStruct((nh, rows, width), BF16)),
        [VM, VM],
        [VM, VM],
        HeadSum.buffers(nh, rows, width)
        + [pltpu.VMEM((rows, width), BF16), HeadSum.sem_shape(nh), HeadGather.sem_shape(nh)],
        (part, x),
    )


def back_body(nh, dpart, ypart, hid_ref, g_ref, valid_ref, y_ref, dh_ref, dg_ref, n1, f1, o1, n2, f2, o2, dbuf, s1, s2, gsem):
    h, b = me()
    barrier_with(head_peers(nh, h, b))
    hd = HeadSum(nh, h, b, dpart, n1, f1, o1, s1)
    hy = HeadSum(nh, h, b, ypart, n2, f2, o2, s2)
    hd.start()
    hd.send()
    hy.start()
    hid = hid_ref[...]
    normed, scale = norm_of(hid)
    valid = valid_ref[...]
    gy = g_ref[...].astype(F32) * valid
    dh = gy + norm_pull(hd.total(), normed, scale)
    dh_ref[...] = dh
    dbuf[...] = dh.astype(BF16)
    hg = HeadGather(nh, h, b, dbuf, dg_ref, gsem)
    hg.start()
    hy.send()
    hg.pass_on()
    y_ref[...] = valid * (hid + hy.total())
    hd.finish()
    hy.finish()
    hg.finish()


def back_exchange(dpart, ypart, hid, g, valid):
    nh, _ = dims()
    rows, width = hid.shape
    return comm_call(
        functools.partial(back_body, nh),
        "back_exchange",
        4,
        (
            jax.ShapeDtypeStruct(hid.shape, F32),
            jax.ShapeDtypeStruct(hid.shape, F32),
            jax.ShapeDtypeStruct((nh, rows, width), BF16),
        ),
        [VM] * 5,
        [VM] * 3,
        HeadSum.buffers(nh, rows, width)
        + HeadSum.buffers(nh, rows, width)
        + [
            pltpu.VMEM((rows, width), BF16),
            HeadSum.sem_shape(nh),
            HeadSum.sem_shape(nh),
            HeadGather.sem_shape(nh),
        ],
        (dpart, ypart, hid, g, valid),
    )


def last_body(nh, nb, dpart, x_ref, dh_ref, gq_ref, go_ref, gm_ref, dx_ref, gq_all, go_all, gm_all, near, far, out, ssem, qsem, osem, msem, lsem):
    h, b = me()
    barrier_all(nh, nb, h, b)
    own = h * nb + b
    hs = HeadSum(nh, h, b, dpart, near, far, out, ssem)
    hs.start()

    def gq_copy(i):
        th, tb = (h + i // nb) % nh, (b + i % nb) % nb
        return remote(
            gq_ref.at[th * nb + tb], gq_all.at[own], qsem.at[0, i], qsem.at[1, i], th, tb
        )

    def go_copy(i):
        tb = (b + i) % nb
        return remote(go_ref.at[tb], go_all.at[b], osem.at[0, i], osem.at[1, i], h, tb)

    @pl.loop(1, nh * nb)
    def _(i):
        gq_copy(i).start()

    @pl.loop(1, nb)
    def _(i):
        go_copy(i).start()

    lq = pltpu.make_async_copy(gq_ref.at[own], gq_all.at[own], lsem.at[0])
    lo = pltpu.make_async_copy(go_ref.at[b], go_all.at[b], lsem.at[1])
    lm = pltpu.make_async_copy(gm_ref.at[h], gm_all.at[h], lsem.at[2])
    for cp in (lq, lo, lm):
        cp.start()
    mcs = [
        remote(gm_ref.at[(h + i) % nh], gm_all.at[h], msem.at[0, i], msem.at[1, i], (h + i) % nh, b)
        for i in range(1, nh)
    ]
    for cp in mcs:
        cp.start()
    hs.send()
    normed, scale = norm_of(x_ref[...].astype(F32))
    dx_ref[...] = dh_ref[...] + norm_pull(hs.total(), normed, scale)
    hs.finish()
    for cp in (lq, lo, lm):
        cp.wait()
    for cp in mcs:
        cp.wait()

    @pl.loop(1, nh * nb)
    def _(i):
        gq_copy(i).wait()

    @pl.loop(1, nb)
    def _(i):
        go_copy(i).wait()


def last_exchange(dpart, x, dh, gq, go, gm):
    nh, nb = dims()
    rows, width = x.shape
    dma = pltpu.SemaphoreType.DMA
    return comm_call(
        functools.partial(last_body, nh, nb),
        "last_exchange",
        5,
        (
            jax.ShapeDtypeStruct(x.shape, F32),
            jax.ShapeDtypeStruct(gq.shape, BF16),
            jax.ShapeDtypeStruct(go.shape, BF16),
            jax.ShapeDtypeStruct(gm.shape, BF16),
        ),
        [VM, VM, VM, ANY, ANY, ANY],
        [VM, ANY, ANY, ANY],
        HeadSum.buffers(nh, rows, width)
        + [HeadSum.sem_shape(nh), dma((2, nh * nb)), dma((2, nb)), dma((2, nh)), dma((3,))],
        (dpart, x, dh, gq, go, gm),
    )


def dot(a, b, ca=1, cb=0):
    return lax.dot_general(a, b, (((ca,), (cb,)), ((), ())), preferred_element_type=F32)


def spans(rows_at, lengths):
    ends = jnp.cumsum(lengths)
    total = ends[-1]
    starts = ends - lengths
    inside = jnp.logical_and(rows_at[..., None] >= starts, rows_at[..., None] < ends)
    first = jnp.sum(jnp.where(inside, starts, 0), axis=-1)
    last = jnp.sum(jnp.where(inside, ends, 0), axis=-1)
    pad = rows_at >= total
    return jnp.where(pad, total, first), last, pad


def turn(values, cos, sin):
    half = DH // 2
    a, b = values[:, :half], values[:, half:]
    return jnp.concatenate([a * cos - b * sin, b * cos + a * sin], axis=1)


def shards(layer_input, out_grad, lengths, ln_attn, w_qkv, w_attn_out, ln_mlp, w_in, w_mlp_out):
    nh, nb = dims()
    h, b = me()
    rows, width = layer_input.shape
    heads = width // DH
    hl = heads // nh
    lw = hl * DH
    group = nh * rows
    slots = nh * nb * rows
    own_rows = w_qkv.shape[0]
    ff = w_mlp_out.shape[0]
    fl = ff // nh
    cb = nb // (2 * hl)
    qs = 2 * cb
    nz = nb // qs

    gain_attn = ln_attn.astype(F32)[:, None]
    gain_mlp = ln_mlp.astype(F32)[:, None]
    wq_own = w_qkv.astype(F32).reshape(own_rows, 3, nh, lw).transpose(2, 0, 1, 3)
    wq_own = wq_own.reshape(nh, own_rows, 3 * lw)
    win_own = w_in.astype(F32).reshape(own_rows, 2, nh, fl).transpose(2, 0, 1, 3)
    win_own = win_own.reshape(nh, own_rows, 2 * fl)
    wd_own = w_mlp_out.T.reshape(own_rows, nh, fl).transpose(1, 0, 2)
    wq_send = (wq_own * gain_attn).astype(BF16)
    wm_send = jnp.concatenate([(win_own * gain_mlp).astype(BF16), wd_own], axis=2)

    xg, gg, wq, wo, wm_h = first_exchange(layer_input, out_grad, wq_send, w_attn_out, wm_send)
    wm = lax.all_gather(wm_h, "blk", axis=1, tiled=True).reshape(width, 3 * fl)
    wq = wq.reshape(width, 3 * lw)
    wo = wo.reshape(lw, width)

    row = lax.iota(jnp.int32, rows)
    group_at = ((lax.iota(jnp.int32, nh) * nb + b)[:, None] * rows + row).reshape(group)
    first, _, pad = spans(group_at, lengths)
    position = (group_at - first).astype(F32)
    half = DH // 2
    inv_freq = jnp.power(ROPE_BASE, -2.0 * lax.iota(F32, half) / DH)
    angles = inv_freq[:, None] * position[None, :]
    cos, sin = jnp.cos(angles), jnp.sin(angles)
    valid_group = jnp.where(pad, 0.0, 1.0)
    own_at = (h * nb + b) * rows + row
    valid = jnp.where(spans(own_at, lengths)[2], 0.0, 1.0)[:, None]

    split = (b % cb) * 2 + h % 2
    tile_block = (
        lax.iota(jnp.int32, nh)[:, None, None] * nb
        + (lax.iota(jnp.int32, nz // 2)[None, :, None] * 2 + lax.iota(jnp.int32, 2)) * qs
        + split
    )
    tiles = nh * nz // 2
    query_at = (tile_block[..., None] * rows + row).reshape(tiles, 1, 2 * rows)
    q_first, q_last, q_pad = spans(query_at, lengths)
    q_last = jnp.where(q_pad, slots, q_last)
    lo = q_first[:, 0, 0] // KEY_BLOCK
    hi = (q_last[:, 0, -1] + KEY_BLOCK - 1) // KEY_BLOCK

    n1 = norm_of(xg.reshape(group, width).astype(F32))[0].astype(BF16)
    qt = dot(wq[:, :lw], n1, 0, 1).reshape(hl, DH, group)
    kt = dot(wq[:, lw : 2 * lw], n1, 0, 1).reshape(hl, DH, group)
    vt = dot(wq[:, 2 * lw :], n1, 0, 1).reshape(hl, DH, group)
    qt = turn(qt, cos, sin).astype(BF16)
    kt = turn(kt, cos, sin).astype(BF16)
    kv = jnp.concatenate([kt, vt.astype(BF16)], axis=1).transpose(0, 2, 1)
    qin, kvin = to_heads(qt, kv.reshape(hl, nh, rows, 2 * DH))
    kv_all = kvin.reshape(slots, 2 * DH)
    ot, of, lse = attend(qin, kv_all, q_first, q_last, lo, hi, rows)
    og = move_queries(ot, hl, False, 6).reshape(lw, group)
    part = dot(og, wo, 0, 0).astype(BF16).reshape(nh, rows, width)
    hid, n2 = mid_exchange(part, layer_input)

    n2 = n2.reshape(group, width)
    gy = (gg.reshape(group, width).astype(F32) * valid_group[:, None]).astype(BF16)
    win, wd = wm[:, : 2 * fl], wm[:, 2 * fl :]
    z = dot(n2, win)
    dm = dot(gy, wd)
    gate, up = z[:, :fl], z[:, fl:]
    cdf = 0.5 * (1.0 + lax.erf(gate * math.sqrt(0.5)))
    act = gate * cdf
    slope = cdf + gate * jnp.exp(-0.5 * gate * gate) * (1.0 / math.sqrt(2.0 * math.pi))
    m = (act * up).astype(BF16)
    dz = jnp.concatenate([dm * up * slope, dm * act], axis=1).astype(BF16)
    ypart = dot(m, wd, 1, 1).astype(BF16).reshape(nh, rows, width)
    dpart = dot(dz, win, 1, 1).astype(BF16).reshape(nh, rows, width)
    y_out, dh, dg = back_exchange(dpart, ypart, hid, out_grad, valid)
    g_in = dot(n2, dz, 0, 0).astype(BF16)
    g_down = dot(gy, m, 0, 0).astype(BF16)
    gm = jnp.concatenate([g_in, g_down], axis=1).reshape(nh, nb * own_rows, 3 * fl)
    gm = lax.psum_scatter(gm, "blk", scatter_dimension=1, tiled=True)

    dg = dg.reshape(group, width)
    dot_t = dot(wo, dg, 1, 1).astype(BF16).reshape(hl, DH, group)
    g_out = dot(og, dg).astype(BF16).reshape(nb, own_rows, width)
    do_in = move_queries(dot_t, hl, True, 7)
    dq, dkv = attend_grad(qin, do_in, of, kv_all, q_first, q_last, lse, lo, hi, rows)
    dqg, dkvg = grads_back(dq, dkv.reshape(nh, nb, rows, 2 * DH), hl)
    dkv_t = jnp.sum(dkvg.astype(F32), axis=1).reshape(hl, group, 2 * DH).transpose(0, 2, 1)
    dq_t = turn(dqg.astype(F32), cos, -sin).astype(BF16).reshape(lw, group)
    dk_t = turn(dkv_t[:, :DH].astype(BF16).astype(F32), cos, -sin).astype(BF16).reshape(lw, group)
    dv_t = dkv_t[:, DH:].astype(BF16).reshape(lw, group)
    dqkv_t = jnp.concatenate([dq_t, dk_t, dv_t], axis=0)
    g_qkv = dot(n1, dqkv_t, 0, 1).astype(BF16).reshape(nh * nb, own_rows, 3 * lw)
    dpart1 = dot(dqkv_t, wq, 0, 1).astype(BF16).reshape(nh, rows, width)
    dx, gq_all, go_all, gm_all = last_exchange(
        dpart1, layer_input, dh, g_qkv, g_out, gm.reshape(nh, own_rows, 3 * fl)
    )

    gq_sum = jnp.sum(gq_all.astype(F32).reshape(nh, nb, own_rows, 3 * lw), axis=1)
    d_ln_attn = jnp.sum(gq_sum * wq_own, axis=(0, 2))
    d_wqkv = (gq_sum * gain_attn).reshape(nh, own_rows, 3, lw).transpose(1, 2, 0, 3)
    d_wqkv = d_wqkv.reshape(own_rows, 3 * width)
    d_wout = jnp.sum(go_all.astype(F32), axis=0)
    gm_all = gm_all.astype(F32)
    gin = gm_all[:, :, : 2 * fl]
    d_ln_mlp = jnp.sum(gin * win_own, axis=(0, 2))
    d_win = (gin * gain_mlp).reshape(nh, own_rows, 2, fl).transpose(1, 2, 0, 3)
    d_win = d_win.reshape(own_rows, 2 * ff)
    d_wdown = gm_all[:, :, 2 * fl :].transpose(0, 2, 1).reshape(ff, own_rows)
    return (y_out, dx, d_ln_attn, d_wqkv, d_wout, d_ln_mlp, d_win, d_wdown)


def solution(mesh):
    both = ("head", "blk")
    row_split = P(both, None)
    return jax.shard_map(
        shards,
        mesh=mesh,
        in_specs=(
            row_split,
            row_split,
            P(),
            P(both),
            row_split,
            row_split,
            P(both),
            row_split,
            P(None, both),
        ),
        out_specs=(
            row_split,
            row_split,
            P(both),
            row_split,
            row_split,
            P(both),
            row_split,
            P(None, both),
        ),
        check_vma=False,
    )
```

time: 1430 us -> 386 us (0.27)
  waiting for transfers between devices: 825 us -> 0.04 us
  Pallas kernels: 0 us -> 286 us
  matrix products: 263 us -> 29.8 us
  blocking collectives: 191 us -> 0 us
  other arithmetic: 46.9 us -> 21.1 us
  local copies, waits for them, and re-layouts: 61.3 us -> 35.5 us
  loops' own time: 16.5 us -> 0 us
    reduce_scatter x4 -> x1, waiting for transfers between devices: 614 us -> 0.01 us  [shards(): gm = lax.psum_scatter(gm, 'blk', scatter_dimension=1, tiled=True)]
    pallas_call x0 -> x10, Pallas kernels: none -> 286 us  [the longest x8 247 us: comm_call(): pl.pallas_call(body, out_shape=out_shape, in_specs=in_specs, out_specs=ou...]
    dot_general x68 -> x14, matrix products: 263 us -> 29.8 us  [dot(): lax.dot_general(a, b, (((ca,), (cb,)), ((), ())), preferred_element_type=...]
    all_gather x7 -> x1, waiting for transfers between devices: 202 us -> 0.01 us  [shards(): wm = lax.all_gather(wm_h, 'blk', axis=1, tiled=True).reshape(width, 3 * fl)]
    unnamed x2 -> x0, blocking collectives: 82.9 us -> none
    all_gather x2 -> x0, blocking collectives: 61.9 us -> none  [the longest x1 31 us: shards(): lse_rows = lax.all_gather(log_total.T, 'blk', axis=0, tiled=True)]
    all_to_all x3 -> x0, blocking collectives: 46.4 us -> none  [the longest x1 23.2 us: shards(): lax.all_to_all(grad_stack, 'head', split_axis=0, concat_axis=2, tiled=True)]
    reduce_sum x16 -> x7, other arithmetic: 31 us -> 4.8 us  [the longest x1 1.72 us: shards(): jnp.sum(gq_all.astype(F32).reshape(nh, nb, own_rows, 3 * lw), axis=1)]
  transfers between devices with their start and end apart: 12 -> 2, of which waited for: 7 -> 0; matrix products, arithmetic and copies ran while one was open for 25% -> 10% of each run, Pallas kernels for 0% -> 47%
where the time goes in v1:
time: 386 us; the launch traced here: 387 us
  Pallas kernels  286 us (74%)
  local copies, waits for them, and re-layouts  35.5 us (9%)
  matrix products  29.8 us (8%)
  other arithmetic  21.1 us (5%)
  between operations  14.7 us (4%)
    pallas_call x8, Pallas kernels, comm_call(): pl.pallas_call(body, out_shape=out_shape, in_specs=in_specs, out_specs=ou...  247 us
    dot_general x14, matrix products, dot(): lax.dot_general(a, b, (((ca,), (cb,)), ((), ())), preferred_element_type=...  29.8 us
    pallas_call x1, Pallas kernels, attend_grad(): pl.pallas_call(attend_grad_body, grid_spec=pltpu.PrefetchScalarGridSpec(n...  21.1 us
    pallas_call x1, Pallas kernels, attend(): pl.pallas_call(attend_body, grid_spec=pltpu.PrefetchScalarGridSpec(num_sc...  17.9 us
    unnamed x78, local copies, waits for them, and re-layouts  10.9 us
  transfers between devices with their start and end apart: 2, of which 0 were waited for; matrix products, arithmetic and copies ran while one was open for 10% of the time, Pallas kernels for 47%

profile of v1, /device:TPU:0, one launch (start us, length us, event | category | flops | bytes accessed | tf_op | source)
XLA Modules:
  0.0 387.4 jit_solution(4079574528117046102)
XLA Ops:
  8.6 1.2 reshape.545
  15.2 51.0 %first_exchange.1 = (bf16[4,128,1024]{2,1,0:T(8,128)(2,1)}, bf16[4,128,1024]{2,1,0:T(8,128)(2,1)}, bf16[32,32,768]{2,1,0:T(8,128)(2,1)}, bf16[8,32,1024]{2,1,0:T(8,128)(2,1)}, bf16[4,32,1968]{2,1,0:T(8,128)(2,1)}) custom-call(bf16[128,1024]{1,0:T(8,128)(2,1)} %x_ref.5, bf16[128,1024]{1,0:T(8,128)(2,1)} %g_ref.3, ...), custom_call_target="tpu_custom_call" | custom-call | tf_op jit(solution)/shard_map/first_exchange/pallas_call | solution.py:35
  67.0 2.4 slice_bitcast_fusion.1
  69.7 1.4 copy.55
  71.0 2.0 copy.53
  80.0 34.3 %to_heads.1 = (bf16[4,64,512]{2,1,0:T(8,128)(2,1)}, bf16[4,8,128,128]{3,2,1,0:T(8,128)(2,1)}) custom-call(bf16[4,64,512]{2,1,0:T(8,128)(2,1)} %pad_maximum_fusion.8.q_ref, bf16[4,4,128,128]{3,2,1,0:T(8,128)(2,1)} %bitcast.129), custom_call_target="tpu_custom_call" | custom-call | tf_op jit(solution)/shard_map/to_heads/pallas_call | solution.py:35
  116.5 1.3 copy-done
  118.8 17.9 %attend.1 = (bf16[4,64,512]{2,1,0:T(8,128)(2,1)S(1)}, f32[4,64,512]{2,1,0:T(8,128)S(1)}, f32[8,1,256]{2,1,0:T(1,128)S(1)}) custom-call(s32[8]{0:T(128)S(1)} %and_select_fusion.1.lo_ref, s32[8]{0:T(128)S(1)} %and_select_fusion.hi_ref, bf16[4,64,512]{2,1,0:T(8,128)(2,1)S(1)} %copy-done.2, bf16[4096,128]{1,0:T(8,128)(2,1)S(1)} %bitcast.110, ...), custom_call_target="tpu_custom_call" | custom-call | tf_op jit(solution)/shard_map/attend/pallas_call | solution.py:511
  138.8 13.5 %queries_back.1 = bf16[4,64,512]{2,1,0:T(8,128)(2,1)} custom-call(bf16[4,64,512]{2,1,0:T(8,128)(2,1)} %copy-done.5), custom_call_target="tpu_custom_call" | custom-call | tf_op jit(solution)/shard_map/queries_back/pallas_call | solution.py:35
  152.3 2.4 convolution_convert_fusion.5
  154.7 21.7 %mid_exchange.1 = (f32[128,1024]{1,0:T(8,128)}, bf16[4,128,1024]{2,1,0:T(8,128)(2,1)}) custom-call(bf16[4,128,1024]{2,1,0:T(8,128)(2,1)} %bitcast.119, bf16[128,1024]{1,0:T(8,128)(2,1)} %x_ref.5), custom_call_target="tpu_custom_call" | custom-call | tf_op jit(solution)/shard_map/mid_exchange/pallas_call | solution.py:35
  177.1 3.0 fusion.4
  180.1 3.8 fusion.2
  184.0 3.5 fusion.18
  189.5 1.6 convolution_convert_fusion
  191.1 2.3 pad_maximum_fusion
  193.4 6.5 %copy.58 = bf16[1024,1968]{1,0:T(8,128)(2,1)} copy(bf16[1024,1968]{0,1:T(8,128)(2,1)} %pad_maximum_fusion) | data formatting | bytes 8060928 | tf_op jit(solution)/shard_map/concatenate | solution.py:938
  200.0 1.3 fusion.20.valid_ref
  201.4 4.2 %convolution_convert_fusion.4 = bf16[512,1024]{1,0:T(8,128)(2,1)} fusion(bf16[512,656]{0,1:T(8,128)(2,1)S(1)} %copy-done.34, bf16[1024,1968]{1,0:T(8,128)(2,1)} %bitcast.154), kind=kOutput, calls=%fused_computation.20 | convolution fusion | flops 688390144 | bytes 3293184 | tf_op jit(solution)/shard_map/dot_general | solution.py:832
  205.5 4.0 %fusion.7 = bf16[512,1024]{1,0:T(8,128)(2,1)} fusion(bf16[1024,1968]{1,0:T(8,128)(2,1)S(1)} %bitcast.155, bf16[512,656]{0,1:T(8,128)(2,1)} %copy-done.37, bf16[512,656]{0,1:T(8,128)(2,1)S(1)} %copy-done.36), kind=kOutput, calls=%fused_computation.19 | convolution fusion | flops 1378942976 | bytes 5275648 | tf_op jit(solution)/shard_map/dot_general | solution.py:832
  209.5 26.4 %back_exchange.1 = (f32[128,1024]{1,0:T(8,128)}, f32[128,1024]{1,0:T(8,128)}, bf16[4,128,1024]{2,1,0:T(8,128)(2,1)}) custom-call(bf16[4,128,1024]{2,1,0:T(8,128)(2,1)} %bitcast.138, bf16[4,128,1024]{2,1,0:T(8,128)(2,1)} %bitcast.137, f32[128,1024]{1,0:T(8,128)} %get-tuple-element.40.hid_ref, bf16[128,1024]{1,0:T(8,128)(2,1)} %g_ref.3, f32[128,1]{1,0:T(8,128)} %fusion.20.valid_ref), custom_call_target="tpu_custom_call" | custom-call | tf_op jit(solution)/shard_map/back_exchange/pallas_call | solution.py:35
  235.9 2.4 convolution_convert_fusion.7
  238.3 14.6 %queries_out.1.do_ref = bf16[4,64,512]{2,1,0:T(8,128)(2,1)} custom-call(bf16[4,64,512]{2,1,0:T(8,128)(2,1)} %bitcast.139), custom_call_target="tpu_custom_call" | custom-call | tf_op jit(solution)/shard_map/queries_out/pallas_call | solution.py:35
  252.9 21.1 %attend_grad.1 = (bf16[4,64,512]{2,1,0:T(8,128)(2,1)}, bf16[4096,128]{1,0:T(8,128)(2,1)}) custom-call(s32[8]{0:T(128)} %copy-done.9, s32[8]{0:T(128)} %copy-done.10, bf16[4,64,512]{2,1,0:T(8,128)(2,1)} %get-tuple-element.35.q_ref, bf16[4,64,512]{2,1,0:T(8,128)(2,1)} %queries_out.1.do_ref, f32[4,64,512]{2,1,0:T(8,128)} %copy-done.3, ...), custom_call_target="tpu_custom_call" | custom-call | tf_op jit(solution)/shard_map/attend_grad/pallas_call | solution.py:582
  274.0 1.3 copy-done.1
  276.3 32.2 %grads_back.1 = (bf16[4,64,512]{2,1,0:T(8,128)(2,1)S(1)}, bf16[4,1,4,128,128]{4,3,2,1,0:T(8,128)(2,1)S(1)}) custom-call(bf16[4,64,512]{2,1,0:T(8,128)(2,1)S(1)} %copy-done.4, bf16[4,8,128,128]{3,2,1,0:T(8,128)(2,1)S(1)} %bitcast.111), custom_call_target="tpu_custom_call" | custom-call | tf_op jit(solution)/shard_map/grads_back/pallas_call | solution.py:35
  310.0 1.2 convolution_convert_fusion.6
  311.3 2.2 convolution_convert_fusion.1
  313.5 2.0 convolution_convert_fusion.3
  315.5 53.4 %last_exchange.1 = (f32[128,1024]{1,0:T(8,128)}, bf16[32,32,768]{2,1,0:T(8,128)(2,1)}, bf16[8,32,1024]{2,1,0:T(8,128)(2,1)}, bf16[4,32,1968]{2,1,0:T(8,128)(2,1)}) custom-call(bf16[4,128,1024]{2,1,0:T(8,128)(2,1)} %bitcast.136, bf16[128,1024]{1,0:T(8,128)(2,1)} %x_ref.5, f32[128,1024]{1,0:T(8,128)} %get-tuple-element.49.dh_ref, ...), custom_call_target="tpu_custom_call" | custom-call | tf_op jit(solution)/shard_map/last_exchange/pallas_call | solution.py:35
  369.0 1.7 convert_reduce_fusion
  377.5 1.5 reshape.571
  (149 shorter events, 33.0 us)
Async XLA Ops:
  7.2 4.2 %copy-start.23 = (bf16[32,5248]{1,0:T(8,128)(2,1)S(1)}, bf16[32,5248]{1,0:T(8,128)(2,1)}, u32[]{:S(2)}) copy-start(bf16[32,5248]{1,0:T(8,128)(2,1)} %param.16) | copy-start | bytes 1007620
  7.2 173.0 %all-gather.2.cloned.1.call-start = ((), (), s32[]{:S(2)}) async-start(), calls=%async_computation.1 | async-start | bytes 4718592 | tf_op jit(solution)/shard_map/all_gather | solution.py:879
  7.9 5.4 %copy-start.26 = (f32[32]{0:T(128)}, f32[32]{0:T(128)S(1)}, u32[]{:S(2)}) copy-start(f32[32]{0:T(128)S(1)} %convert_element_type.115) | copy-start | bytes 388
  8.6 5.5 %copy-start.28 = (f32[32]{0:T(128)}, f32[32]{0:T(128)S(1)}, u32[]{:S(2)}) copy-start(f32[32]{0:T(128)S(1)} %convert_element_type.117) | copy-start | bytes 388
  14.1 52.2 %copy-start.32 = (s32[4]{0:T(128)S(1)}, s32[4]{0:T(128)}, u32[]{:S(2)}) copy-start(s32[4]{0:T(128)} %param.11) | copy-start | bytes 52
  66.2 249.3 %reduce-scatter.2.cloned.1.call-start = ((), (), s32[]{:S(2)}) async-start(), calls=%async_computation.2 | async-start | bytes 4718592 | tf_op jit(solution)/shard_map/reduce_scatter | solution.py:939
  69.5 4.2 %copy-start.11 = (bf16[4,128,1024]{2,1,0:T(8,128)(2,1)S(1)}, bf16[4,128,1024]{2,1,0:T(8,128)(2,1)}, u32[]{:S(2)}) copy-start(bf16[4,128,1024]{2,1,0:T(8,128)(2,1)} %get-tuple-element.34) | copy-start | bytes 3145732
  75.9 1.1 copy-start.15
  78.2 74.0 %copy-start.14 = (bf16[8,32,1024]{2,1,0:T(8,128)(2,1)S(1)}, bf16[8,32,1024]{2,1,0:T(8,128)(2,1)}, u32[]{:S(2)}) copy-start(bf16[8,32,1024]{2,1,0:T(8,128)(2,1)} %get-tuple-element.38) | copy-start | bytes 1572868
  116.0 60.4 %copy-start.6 = (s32[8,1,256]{2,1,0:T(1,128)}, s32[8,1,256]{2,1,0:T(1,128)S(1)}, u32[]{:S(2)}) copy-start(s32[8,1,256]{2,1,0:T(1,128)S(1)} %get-tuple-element.78.last_ref) | copy-start | bytes 24580
  116.0 60.4 %copy-start.7 = (s32[8,1,256]{2,1,0:T(1,128)}, s32[8,1,256]{2,1,0:T(1,128)S(1)}, u32[]{:S(2)}) copy-start(s32[8,1,256]{2,1,0:T(1,128)S(1)} %get-tuple-element.79.first_ref) | copy-start | bytes 24580
  116.4 60.0 %copy-start.9 = (s32[8]{0:T(128)}, s32[8]{0:T(128)S(1)}, u32[]{:S(2)}) copy-start(s32[8]{0:T(128)S(1)} %and_select_fusion.1.lo_ref) | copy-start | bytes 100
  116.4 60.0 %copy-start.10 = (s32[8]{0:T(128)}, s32[8]{0:T(128)S(1)}, u32[]{:S(2)}) copy-start(s32[8]{0:T(128)S(1)} %and_select_fusion.hi_ref) | copy-start | bytes 100
  116.4 1.4 copy-start
  180.1 3.8 copy-start.18
  187.5 1.1 copy-start.35
  187.5 1.3 copy-start.37
  187.6 1.9 copy-start.31
  200.0 1.4 copy-start.34
  201.3 4.2 %copy-start.30 = (bf16[4,256,1968]{2,1,0:T(8,128)(2,1)S(1)}, bf16[4,256,1968]{2,1,0:T(8,128)(2,1)}, u32[]{:S(2)}) copy-start(bf16[4,256,1968]{2,1,0:T(8,128)(2,1)} %all-gather.2.cloned.1.call-done) | copy-start | bytes 12091396
  201.3 4.2 %copy-start.36 = (bf16[512,656]{0,1:T(8,128)(2,1)S(1)}, bf16[512,656]{0,1:T(8,128)(2,1)}, u32[]{:S(2)}) copy-start(bf16[512,656]{0,1:T(8,128)(2,1)} %copy-done.35) | copy-start | bytes 2015236
  274.0 1.3 copy-start.1
  276.3 32.6 %copy-start.24 = (f32[32,512]{1,0:T(8,128)S(1)}, f32[32,512]{1,0:T(8,128)}, u32[]{:S(2)}) copy-start(f32[32,512]{1,0:T(8,128)} %get-tuple-element.80) | copy-start | bytes 196612
  308.8 1.2 copy-start.12
  308.8 1.3 copy-start.13
  308.9 2.4 copy-start.17
  311.3 2.2 copy-start.16
  369.0 2.9 copy-start.27
  369.0 3.0 copy-start.19
  370.7 1.4 copy-start.29
  376.2 2.7 copy-start.21
  377.0 2.8 copy-start.22
  (8 other events, 6.5 us)
Sparse Core Ops, SparseCore 0:
  66.3 95.1 all-gather.1
  200.1 111.1 reduce-scatter.1

commit v2 on v1

v2 whole, which is shorter than its diff:
```python
import functools
import math

import jax
import jax.numpy as jnp
from jax import lax
from jax.experimental import pallas as pl
from jax.experimental.pallas import tpu as pltpu
from jax.sharding import PartitionSpec as P

DH = 64
ROPE_BASE = 160000.0
NORM_EPS = 1e-05
MASK_FLOOR = -1e30
KEY_BLOCK = 512
EXP_SCALE = 0.125 * math.log2(math.e)
BF16 = jnp.bfloat16
F32 = jnp.float32
MESH_ID = pl.DeviceIdType.MESH
ANY = pl.BlockSpec(memory_space=pl.ANY)
VM = pl.BlockSpec(memory_space=pltpu.VMEM)


def dims():
    nh = lax.axis_size("head")
    nb = lax.axis_size("blk")
    return nh, nb


def me():
    return lax.axis_index("head"), lax.axis_index("blk")


def comm_call(body, name, cid, out_shape, in_specs, out_specs, scratch, args, vmem=None):
    return pl.pallas_call(
        body,
        out_shape=out_shape,
        in_specs=in_specs,
        out_specs=out_specs,
        scratch_shapes=scratch,
        name=name,
        compiler_params=pltpu.CompilerParams(
            collective_id=cid, has_side_effects=True, vmem_limit_bytes=vmem
        ),
    )(*args)


def remote(src, dst, send, recv, h, b):
    return pltpu.make_async_remote_copy(
        src_ref=src,
        dst_ref=dst,
        send_sem=send,
        recv_sem=recv,
        device_id=(h, b),
        device_id_type=MESH_ID,
    )


def signal(h, b):
    pl.semaphore_signal(
        pltpu.get_barrier_semaphore(), inc=1, device_id=(h, b), device_id_type=MESH_ID
    )


def signal_head(nh, h, b):
    for i in range(1, nh):
        signal((h + i) % nh, b)


def wait_head(nh):
    pl.semaphore_wait(pltpu.get_barrier_semaphore(), nh - 1)


def signal_all(nh, nb, h, b):
    @pl.loop(1, nh * nb)
    def _(i):
        signal((h + i // nb) % nh, (b + i % nb) % nb)


def wait_all(nh, nb):
    pl.semaphore_wait(pltpu.get_barrier_semaphore(), nh * nb - 1)


class HeadGather:
    def __init__(self, nh, h, b, src, dst, sems):
        self.nh, self.h, self.b, self.dst, self.sems = nh, h, b, dst, sems
        nx = nh // 2
        self.nx = nx
        x, c = h // 2, h % 2
        sib = x * 2 + 1 - c
        self.sib = sib
        self.across = []
        for k in range(1, nx):
            self.across.append(
                remote(src, dst.at[h], sems.at[0, k], sems.at[1, k], ((x + k) % nx) * 2 + c, b)
            )
        self.near = remote(src, dst.at[h], sems.at[0, 0], sems.at[1, 0], sib, b)
        self.local = pltpu.make_async_copy(src, dst.at[h], sems.at[2, 0])
        self.forward = []
        for k in range(1, nx):
            got = ((x + nx - k) % nx) * 2 + c
            self.forward.append(
                remote(dst.at[got], dst.at[got], sems.at[2, k], sems.at[3, k], sib, b)
            )

    @staticmethod
    def sem_shape(nh):
        return pltpu.SemaphoreType.DMA((4, nh // 2))

    def start(self):
        for cp in self.across:
            cp.start()
        self.near.start()
        self.local.start()

    def pass_on(self):
        for cp, fw in zip(self.across, self.forward):
            cp.wait_recv()
            fw.start()

    def finish(self):
        for cp in self.across:
            cp.wait_send()
        self.near.wait()
        self.local.wait()
        for fw in self.forward:
            fw.wait()


def lane_roll(values, shift):
    return pltpu.roll(values, shift % values.shape[1], 1)


def lanes_of(values):
    return lax.broadcasted_iota(jnp.int32, (1, values.shape[1]), 1)


def widen(values, width):
    extra = width - values.shape[1]
    if extra <= 0:
        return values[:, :width]
    return jnp.concatenate([values, jnp.zeros((values.shape[0], extra), values.dtype)], axis=1)


def ff_widths(fl):
    up = lambda v: (v + 127) // 128 * 128
    return up(3 * fl), up(2 * fl), 2 * fl // 128 * 128


class PairedSpread:
    def __init__(self, nh, nb, h, b, block, out, sems, over_head):
        self.nh = nh if over_head else 1
        self.nb, self.h, self.b, self.block, self.out, self.sems = nb, h, b, block, out, sems
        self.over_head = over_head
        self.nk = nb // 2
        self.y, self.k = b % 2, b // 2
        self.count = self.nh * self.nk

    @staticmethod
    def sem_shape(n):
        return pltpu.SemaphoreType.DMA((4, n))

    def place(self, h, b):
        return self.out.at[h * self.nb + b] if self.over_head else self.out.at[b]

    def target(self, i, sign):
        dh, dk = i // self.nk, i % self.nk
        if sign < 0:
            dh, dk = self.nh - dh, self.nk - dk
        th = (self.h + dh) % self.nh if self.over_head else self.h
        return th, ((self.k + dk) % self.nk) * 2 + self.y

    def send(self, i):
        th, tb = self.target(i, 1)
        return remote(
            self.block(th), self.place(self.h, self.b), self.sems.at[0, i], self.sems.at[1, i], th, tb
        )

    def forward(self, i):
        ref = self.place(*self.target(i, -1))
        return remote(
            ref, ref, self.sems.at[2, i], self.sems.at[3, i], self.h, self.b + 1 - 2 * self.y
        )

    def local(self):
        return pltpu.make_async_copy(
            self.block(self.h), self.place(self.h, self.b), self.sems.at[0, 0]
        )

    def start(self):
        @pl.loop(1, self.count)
        def _(i):
            self.send(i).start()

        self.local().start()

    def pass_on(self):
        self.local().wait()
        self.forward(0).start()

        @pl.loop(1, self.count)
        def _(i):
            self.send(i).wait_recv()
            self.forward(i).start()

    def finish(self):
        @pl.loop(1, self.count)
        def _(i):
            self.send(i).wait_send()

        @pl.loop(0, self.count)
        def _(i):
            self.forward(i).wait()


def first_body(nh, nb, lw, fl, x_ref, wq_ref, ga_ref, win_hbm, gf_ref, wd_hbm, xg, wm_h, wq_all, pack, wmp, win_ref, wd_ref, xs, sems, msem, stage):
    h, b = me()
    loads = [
        pltpu.make_async_copy(win_hbm, win_ref, stage.at[0]),
        pltpu.make_async_copy(wd_hbm, wd_ref, stage.at[1]),
    ]
    for cp in loads:
        cp.start()
    signal_all(nh, nb, h, b)
    gain = ga_ref[...]
    width = nh * lw
    for i in range(nh):
        for c in range(3):
            at = c * width + i * lw
            pack[i, :, c * lw : (c + 1) * lw] = (
                wq_ref[:, at : at + lw].astype(F32) * gain
            ).astype(BF16)
    wait_all(nh, nb)
    spread = PairedSpread(nh, nb, h, b, lambda th: pack.at[th], wq_all, sems, True)
    gx = HeadGather(nh, h, b, x_ref, xg, xs)
    gx.start()
    spread.start()
    for cp in loads:
        cp.wait()
    total, _, _ = ff_widths(fl)
    ff = nh * fl
    win = win_ref[...].astype(F32) * gf_ref[...]
    wd = widen(wd_ref[...].astype(F32), total if total > ff else (ff + 127) // 128 * 128)
    lane = lax.broadcasted_iota(jnp.int32, (1, total), 1)
    for i in range(nh):
        gate = widen(lane_roll(win, -i * fl), total)
        up = widen(lane_roll(win, fl - ff - i * fl), total)
        down = widen(lane_roll(wd, 2 * fl - i * fl), total)
        piece = jnp.where(
            lane < fl,
            gate,
            jnp.where(lane < 2 * fl, up, jnp.where(lane < 3 * fl, down, 0.0)),
        )
        wmp[i] = piece.astype(BF16)
    own = pltpu.make_async_copy(wmp.at[h], wm_h.at[h], msem.at[0, 0])
    own.start()
    copies = [
        remote(wmp.at[(h + i) % nh], wm_h.at[h], msem.at[0, i], msem.at[1, i], (h + i) % nh, b)
        for i in range(1, nh)
    ]
    for cp in copies:
        cp.start()
    gx.pass_on()
    spread.pass_on()
    spread.finish()
    gx.finish()
    own.wait()
    for cp in copies:
        cp.wait()


def first_exchange(x, w_qkv, gain_attn, w_in, gain_mlp, wd_t, fl):
    nh, nb = dims()
    rows, width = x.shape
    lw = width // nh
    own_rows = w_in.shape[0]
    total = ff_widths(fl)[0]
    dma = pltpu.SemaphoreType.DMA
    return comm_call(
        functools.partial(first_body, nh, nb, lw, fl),
        "first_exchange",
        0,
        (
            jax.ShapeDtypeStruct((nh, rows, width), BF16),
            jax.ShapeDtypeStruct((nh, own_rows, total), BF16),
            jax.ShapeDtypeStruct((nh * nb, own_rows, 3 * lw), BF16),
        ),
        [ANY, VM, VM, ANY, VM, ANY],
        [ANY, ANY, ANY],
        [
            pltpu.VMEM((nh, own_rows, 3 * lw), BF16),
            pltpu.VMEM((nh, own_rows, total), BF16),
            pltpu.VMEM(w_in.shape, BF16),
            pltpu.VMEM(wd_t.shape, BF16),
            HeadGather.sem_shape(nh),
            PairedSpread.sem_shape(nh * nb // 2),
            dma((2, nh)),
            dma((2,)),
        ],
        (x, w_qkv, gain_attn, w_in, gain_mlp, wd_t),
        vmem=60 << 20,
    )


class Place:
    def __init__(self, nh, nb, hl):
        h, b = me()
        self.h, self.b, self.hl = h, b, hl
        self.x, self.c = h // 2, h % 2
        self.cb = nb // (2 * hl)
        self.qs = 2 * self.cb
        self.nz = nb // self.qs
        self.sib = self.x * 2 + 1 - self.c
        self.split = b % self.qs
        self.zi = b // self.qs
        self.t = b // self.cb
        self.u = b % self.cb
        self.my_l = self.t // 2
        self.my_src_h = self.x * 2 + self.t % 2

    def query_dest(self, l):
        return self.x * 2 + self.split % 2, (2 * l + self.c) * self.cb + self.split // 2

    def query_source(self, zi):
        return self.my_src_h, zi * self.qs + self.u * 2 + self.c


def signal_plane(pc, nb):
    @pl.loop(0, nb)
    def _(i):
        signal(pc.sib, (pc.b + i) % nb)

    @pl.loop(1, nb)
    def _(i):
        signal(pc.h, (pc.b + i) % nb)


def signal_plane_and_head(pc, nh, nb):
    signal_plane(pc, nb)
    for k in range(1, nh // 2):
        for core in range(2):
            signal(((pc.x + k) % (nh // 2)) * 2 + core, pc.b)


def wait_plane(nb):
    pl.semaphore_wait(pltpu.get_barrier_semaphore(), 2 * nb - 1)


def wait_plane_and_head(nh, nb):
    pl.semaphore_wait(pltpu.get_barrier_semaphore(), 2 * nb - 1 + nh - 2)


def routed(pc, src, dst, send, recv, th, tb, act):
    mine = jnp.logical_and(th == pc.h, tb == pc.b)

    @pl.when(mine)
    def _():
        if act == "start":
            pltpu.make_async_copy(src, dst, recv).start()

    @pl.when(jnp.logical_not(mine))
    def _():
        cp = remote(src, dst, send, recv, th, tb)
        if act == "start":
            cp.start()
        else:
            cp.wait_send()


def wait_on(ref, sem):
    pltpu.make_async_copy(ref, ref, sem).wait()


def queries_out(pc, q_ref, qin, qsem, act):
    for l in range(pc.hl):
        th, tb = pc.query_dest(l)
        routed(pc, q_ref.at[l], qin.at[pc.zi], qsem.at[0, l], qsem.at[1, pc.zi], th, tb, act)


def queries_back(pc, o_ref, og, osem, act):
    for zi in range(pc.nz):
        th, tb = pc.query_source(zi)
        routed(pc, o_ref.at[zi], og.at[pc.my_l], osem.at[0, zi], osem.at[1, pc.my_l], th, tb, act)


def halves_swapped(tile):
    lane = lanes_of(tile)
    return jnp.where(lane % DH < DH // 2, lane_roll(tile, -(DH // 2)), lane_roll(tile, DH // 2))


def turned(tile, cos, sin):
    return tile * cos + halves_swapped(tile) * sin


def to_heads_body(nh, nb, hl, xg_hbm, w_hbm, cos_ref, sin_ref, g_ref, wo_ref, qin, kvin, n1_ref, gg, wo_all, qbuf, kvbuf, xg_ref, w_ref, qsem, ksem, fsem, gsem, osem, stage):
    pc = Place(nh, nb, hl)
    loads = [
        pltpu.make_async_copy(xg_hbm, xg_ref, stage.at[0]),
        pltpu.make_async_copy(w_hbm, w_ref, stage.at[1]),
    ]
    for cp in loads:
        cp.start()
    signal_plane_and_head(pc, nh, nb)
    rows = xg_ref.shape[1]
    lw = hl * DH
    loads[0].wait()
    for i in range(nh):
        n1_ref[i * rows : (i + 1) * rows, :] = norm_of(xg_ref[i].astype(F32))[0].astype(BF16)
    n1 = n1_ref[...]
    cos, sin = cos_ref[...], sin_ref[...]
    loads[1].wait()
    kk = jnp.dot(n1, w_ref[:, lw : 2 * lw], preferred_element_type=F32)
    vv = jnp.dot(n1, w_ref[:, 2 * lw :], preferred_element_type=F32)
    for p in range(hl // 2):
        k = turned(kk[:, p * 128 : (p + 1) * 128], cos, sin)
        v = vv[:, p * 128 : (p + 1) * 128]
        low = lanes_of(k) < DH
        even = jnp.where(low, k, lane_roll(v, DH)).astype(BF16)
        odd = jnp.where(low, lane_roll(k, DH), v).astype(BF16)
        for i in range(nh):
            kvbuf[2 * p, i] = even[i * rows : (i + 1) * rows]
            kvbuf[2 * p + 1, i] = odd[i * rows : (i + 1) * rows]
    wait_plane_and_head(nh, nb)
    core = pc.b % 2

    def keys_out(act):
        for l in range(hl):
            for u in range(pc.cb):
                routed(
                    pc,
                    kvbuf.at[l],
                    kvin.at[:, pc.b],
                    ksem.at[0, l * pc.cb + u],
                    ksem.at[1, pc.b // 2],
                    pc.x * 2 + core,
                    (2 * l + pc.c) * pc.cb + u,
                    act,
                )

    keys_out("start")
    qq = jnp.dot(n1, w_ref[:, :lw], preferred_element_type=F32)
    for p in range(hl // 2):
        q = turned(qq[:, p * 128 : (p + 1) * 128], cos, sin).T.astype(BF16)
        qbuf[2 * p] = q[:DH]
        qbuf[2 * p + 1] = q[DH:]
    queries_out(pc, qbuf, qin, qsem, "start")
    hg = HeadGather(nh, pc.h, pc.b, g_ref, gg, gsem)
    hg.start()
    spread = PairedSpread(nh, nb, pc.h, pc.b, lambda th: wo_ref, wo_all, osem, False)
    spread.start()

    def forward(k):
        at = kvin.at[:, 2 * k + pc.c]
        return remote(at, at, fsem.at[0, k], fsem.at[1, k], pc.sib, pc.b)

    @pl.loop(0, nb // 2)
    def _(k):
        wait_on(kvin.at[:, 2 * k + pc.c], ksem.at[1, k])
        forward(k).start()

    hg.pass_on()
    spread.pass_on()
    keys_out("wait_send")
    queries_out(pc, qbuf, qin, qsem, "wait_send")
    for zi in range(pc.nz):
        wait_on(qin.at[zi], qsem.at[1, zi])

    @pl.loop(0, nb // 2)
    def _(k):
        forward(k).wait()

    spread.finish()
    hg.finish()


def to_heads(xg, wq, cos, sin, g, wo, hl):
    nh, nb = dims()
    _, rows, width = xg.shape
    group = nh * rows
    cb = nb // (2 * hl)
    nz = nb // (2 * cb)
    dma = pltpu.SemaphoreType.DMA
    return comm_call(
        functools.partial(to_heads_body, nh, nb, hl),
        "to_heads",
        2,
        (
            jax.ShapeDtypeStruct((nz, DH, group), BF16),
            jax.ShapeDtypeStruct((nh, nb, rows, 2 * DH), BF16),
            jax.ShapeDtypeStruct((group, width), BF16),
            jax.ShapeDtypeStruct((nh, rows, width), BF16),
            jax.ShapeDtypeStruct((nb,) + wo.shape, BF16),
        ),
        [ANY, ANY, VM, VM, ANY, ANY],
        [ANY, ANY, VM, ANY, ANY],
        [
            pltpu.VMEM((hl, DH, group), BF16),
            pltpu.VMEM((hl, nh, rows, 2 * DH), BF16),
            pltpu.VMEM(xg.shape, BF16),
            pltpu.VMEM(wq.shape, BF16),
            dma((2, max(hl, nz))),
            dma((2, max(hl * cb, nb // 2))),
            dma((2, nb // 2)),
            HeadGather.sem_shape(nh),
            PairedSpread.sem_shape(nb // 2),
            dma((2,)),
        ],
        (xg, wq, cos, sin, g, wo),
        vmem=60 << 20,
    )


def query_tile(ref):
    return jnp.concatenate([ref[0], ref[1]], axis=1)


def allowed(block_at, first_ref, last_ref, lanes):
    at = block_at * KEY_BLOCK + lax.broadcasted_iota(jnp.int32, (KEY_BLOCK, lanes), 0)
    return jnp.logical_and(at >= first_ref[0], at < last_ref[0])


def attend_body(lo_ref, hi_ref, q_ref, kv_ref, first_ref, last_ref, o_ref, of_ref, lse_ref):
    tile = pl.program_id(0)
    q = query_tile(q_ref)
    lanes = q.shape[1]
    q_pad = jnp.concatenate([q, jnp.zeros_like(q)], axis=0)

    def step(j, carry):
        top, total, acc = carry
        kv = kv_ref[pl.ds(pl.multiple_of(j * KEY_BLOCK, KEY_BLOCK), KEY_BLOCK), :]
        s = jnp.dot(kv, q_pad, preferred_element_type=F32)
        s = jnp.where(allowed(j, first_ref, last_ref, lanes), s, MASK_FLOOR)
        new_top = jnp.maximum(top, jnp.max(s, axis=0, keepdims=True))
        p = jnp.exp2((s - new_top) * EXP_SCALE)
        alpha = jnp.exp2((top - new_top) * EXP_SCALE)
        total = total * alpha + jnp.sum(p, axis=0, keepdims=True)
        acc = acc * alpha + lax.dot_general(
            kv, p.astype(BF16), (((0,), (0,)), ((), ())), preferred_element_type=F32
        )
        return new_top, total, acc

    top, total, acc = lax.fori_loop(
        lo_ref[tile],
        hi_ref[tile],
        step,
        (
            jnp.full((1, lanes), MASK_FLOOR, F32),
            jnp.zeros((1, lanes), F32),
            jnp.zeros((2 * DH, lanes), F32),
        ),
    )
    o = acc[DH:] / total
    half = lanes // 2
    for i in range(2):
        part = o[:, i * half : (i + 1) * half]
        of_ref[i] = part
        o_ref[i] = part.astype(BF16)
    lse_ref[0] = top * EXP_SCALE + jnp.log2(total)


def attend_specs(kv_rows, rows, pairs):
    tile_spec = pl.BlockSpec((2, DH, rows), lambda i, *_: (i % pairs, 0, i // pairs))
    row_spec = pl.BlockSpec((1, 1, 2 * rows), lambda i, *_: (i, 0, 0))
    kv_spec = pl.BlockSpec((kv_rows, 2 * DH), lambda i, *_: (0, 0))
    return tile_spec, row_spec, kv_spec


def attend(q, kv, first, last, lo, hi, rows):
    nz, _, group = q.shape
    tiles = lo.shape[0]
    tile_spec, row_spec, kv_spec = attend_specs(kv.shape[0], rows, nz // 2)
    return pl.pallas_call(
        attend_body,
        grid_spec=pltpu.PrefetchScalarGridSpec(
            num_scalar_prefetch=2,
            grid=(tiles,),
            in_specs=[tile_spec, kv_spec, row_spec, row_spec],
            out_specs=[tile_spec, tile_spec, row_spec],
        ),
        out_shape=(
            jax.ShapeDtypeStruct(q.shape, BF16),
            jax.ShapeDtypeStruct(q.shape, F32),
            jax.ShapeDtypeStruct((tiles, 1, 2 * rows), F32),
        ),
        name="attend",
        compiler_params=pltpu.CompilerParams(vmem_limit_bytes=60 << 20),
    )(lo, hi, q, kv, first, last)


def attend_grad_body(lo_ref, hi_ref, q_ref, do_ref, of_ref, kv_ref, first_ref, last_ref, lse_ref, dq_ref, dkv_ref, acc_ref):
    tile = pl.program_id(0)

    @pl.when(tile == 0)
    def _():
        acc_ref[...] = jnp.zeros_like(acc_ref)

    q = query_tile(q_ref)
    do = query_tile(do_ref)
    lanes = q.shape[1]
    zero = jnp.zeros_like(q)
    both = jnp.concatenate(
        [jnp.concatenate([q, zero], axis=0), jnp.concatenate([zero, do], axis=0)], axis=1
    )
    delta = jnp.sum(do.astype(F32) * query_tile(of_ref), axis=0, keepdims=True)
    lse = lse_ref[0]

    def step(j, dq):
        at = pl.ds(pl.multiple_of(j * KEY_BLOCK, KEY_BLOCK), KEY_BLOCK)
        kv = kv_ref[at, :]
        sd = jnp.dot(kv, both, preferred_element_type=F32)
        s, dp = sd[:, :lanes], sd[:, lanes:]
        p = jnp.exp2(
            jnp.where(
                allowed(j, first_ref, last_ref, lanes), s * EXP_SCALE - lse, MASK_FLOOR
            )
        )
        ds = (p * (dp - delta)).astype(BF16)
        acc_ref[at, :] += lax.dot_general(
            jnp.concatenate([ds, p.astype(BF16)], axis=1),
            both,
            (((1,), (1,)), ((), ())),
            preferred_element_type=F32,
        )
        return dq + lax.dot_general(
            kv, ds, (((0,), (0,)), ((), ())), preferred_element_type=F32
        )

    dq = lax.fori_loop(lo_ref[tile], hi_ref[tile], step, jnp.zeros((2 * DH, lanes), F32))
    half = lanes // 2
    for i in range(2):
        dq_ref[i] = (dq[:DH, i * half : (i + 1) * half] * 0.125).astype(BF16)

    @pl.when(tile == pl.num_programs(0) - 1)
    def _():
        lane = lax.broadcasted_iota(jnp.int32, (1, 2 * DH), 1)
        dkv_ref[...] = (acc_ref[...] * jnp.where(lane < DH, 0.125, 1.0)).astype(BF16)


def attend_grad(q, do, of, kv, first, last, lse, lo, hi, rows):
    nz, _, group = q.shape
    tiles = lo.shape[0]
    tile_spec, row_spec, kv_spec = attend_specs(kv.shape[0], rows, nz // 2)
    return pl.pallas_call(
        attend_grad_body,
        grid_spec=pltpu.PrefetchScalarGridSpec(
            num_scalar_prefetch=2,
            grid=(tiles,),
            in_specs=[tile_spec, tile_spec, tile_spec, kv_spec, row_spec, row_spec, row_spec],
            out_specs=[tile_spec, kv_spec],
            scratch_shapes=[pltpu.VMEM(kv.shape, F32)],
        ),
        out_shape=(jax.ShapeDtypeStruct(q.shape, BF16), jax.ShapeDtypeStruct(kv.shape, BF16)),
        name="attend_grad",
        compiler_params=pltpu.CompilerParams(vmem_limit_bytes=60 << 20),
    )(lo, hi, q, do, of, kv, first, last, lse)


class HeadSum:
    def __init__(self, nh, h, b, part, near, far, out, sems):
        self.nx = nh // 2
        self.x, self.c = h // 2, h % 2
        self.h, self.part, self.near, self.far, self.out = h, part, near, far, out
        sib = self.x * 2 + 1 - self.c
        self.pairs = [
            remote(
                part.at[((self.x + k) % self.nx) * 2 + 1 - self.c],
                near.at[k],
                sems.at[0, k],
                sems.at[1, k],
                sib,
                b,
            )
            for k in range(self.nx)
        ]
        self.across = [
            remote(
                out.at[k],
                far.at[k],
                sems.at[2, k],
                sems.at[3, k],
                ((self.x + k) % self.nx) * 2 + self.c,
                b,
            )
            for k in range(1, self.nx)
        ]

    @staticmethod
    def sem_shape(nh):
        return pltpu.SemaphoreType.DMA((4, nh // 2))

    @staticmethod
    def buffers(nh, rows, width):
        return [pltpu.VMEM((nh // 2, rows, width), BF16)] * 3

    def start(self):
        for k in list(range(1, self.nx)) + [0]:
            self.pairs[k].start()

    def send(self):
        for k in range(1, self.nx):
            self.pairs[k].wait_recv()
            at = ((self.x + k) % self.nx) * 2 + self.c
            self.out[k] = (self.part[at].astype(F32) + self.near[k].astype(F32)).astype(BF16)
            self.across[k - 1].start()

    def total(self):
        self.pairs[0].wait_recv()
        total = self.part[self.h].astype(F32) + self.near[0].astype(F32)
        for k in range(1, self.nx):
            self.across[k - 1].wait_recv()
            total = total + self.far[k].astype(F32)
        return total

    def finish(self):
        for cp in self.pairs:
            cp.wait_send()
        for cp in self.across:
            cp.wait_send()


def norm_of(values):
    centre = values - jnp.mean(values, axis=-1, keepdims=True)
    scale = lax.rsqrt(jnp.mean(centre * centre, axis=-1, keepdims=True) + NORM_EPS)
    return centre * scale, scale


def norm_pull(grad, normed, scale):
    one = jnp.mean(grad, axis=-1, keepdims=True)
    two = jnp.mean(grad * normed, axis=-1, keepdims=True)
    return scale * (grad - one - normed * two)


CHUNKS = 2


def chunk_of(ref, j, axis):
    size = ref.shape[axis] // CHUNKS
    at = pl.ds(j * size, size)
    return ref.at[at] if axis == 0 else ref.at[:, at]


def head_sums(nh, h, b, part, bufs, sems):
    near, far, out = bufs
    return [
        HeadSum(
            nh,
            h,
            b,
            chunk_of(part, j, 1),
            chunk_of(near, j, 1),
            chunk_of(far, j, 1),
            chunk_of(out, j, 1),
            sems.at[j],
        )
        for j in range(CHUNKS)
    ]


def head_gathers(nh, h, b, src, dst, sems):
    return [
        HeadGather(nh, h, b, chunk_of(src, j, 0), chunk_of(dst, j, 1), sems.at[j])
        for j in range(CHUNKS)
    ]


def chunk_sems(nh):
    return pltpu.SemaphoreType.DMA((CHUNKS, 4, nh // 2))


def mid_body(nh, nb, hl, o_ref, wo_ref, x_ref, og, hid_ref, ng_ref, part, near, far, out, nbuf, osem, ssem, gsem):
    pc = Place(nh, nb, hl)
    h, b = pc.h, pc.b
    signal_plane_and_head(pc, nh, nb)
    wait_plane_and_head(nh, nb)
    rows, width = x_ref.shape
    queries_back(pc, o_ref, og, osem, "start")
    queries_back(pc, o_ref, og, osem, "wait_send")
    for l in range(hl):
        wait_on(og.at[l], osem.at[1, l])
    o = og[...].reshape(hl * DH, nh * rows)
    wo = wo_ref[...]
    for i in range(nh):
        part[i] = lax.dot_general(
            o[:, i * rows : (i + 1) * rows], wo, (((0,), (0,)), ((), ())), preferred_element_type=F32
        ).astype(BF16)
    hss = head_sums(nh, h, b, part, (near, far, out), ssem)
    hgs = head_gathers(nh, h, b, nbuf, ng_ref, gsem)
    for hs in hss:
        hs.start()
    for hs in hss:
        hs.send()
    size = rows // CHUNKS
    for j, (hs, hg) in enumerate(zip(hss, hgs)):
        at = pl.ds(j * size, size)
        hid = x_ref[at, :].astype(F32) + hs.total()
        hid_ref[at, :] = hid
        nbuf[at, :] = norm_of(hid)[0].astype(BF16)
        hg.start()
    for hg in hgs:
        hg.pass_on()
    for hs, hg in zip(hss, hgs):
        hs.finish()
        hg.finish()


def mid_exchange(ot, wo, x, hl):
    nh, nb = dims()
    rows, width = x.shape
    nz = ot.shape[0]
    return comm_call(
        functools.partial(mid_body, nh, nb, hl),
        "mid_exchange",
        3,
        (
            jax.ShapeDtypeStruct((hl,) + ot.shape[1:], BF16),
            jax.ShapeDtypeStruct(x.shape, F32),
            jax.ShapeDtypeStruct((nh, rows, width), BF16),
        ),
        [ANY, VM, VM],
        [VM, VM, VM],
        [pltpu.VMEM((nh, rows, width), BF16)]
        + HeadSum.buffers(nh, rows, width)
        + [
            pltpu.VMEM((rows, width), BF16),
            pltpu.SemaphoreType.DMA((2, max(hl, nz))),
            chunk_sems(nh),
            chunk_sems(nh),
        ],
        (ot, wo, x),
        vmem=60 << 20,
    )


def ffn_body(nh, nb, fl, split_rows, n_ref, g_ref, valid_ref, w_ref, y_ref, d_ref, ga_ref, gb_ref, gy, mm, dz):
    rows, width = n_ref.shape[1], n_ref.shape[2]
    group = nh * rows
    total, zc, off = ff_widths(fl)
    wide = total - off
    shift = 2 * fl - off
    step = 2 * rows
    lane = lax.broadcasted_iota(jnp.int32, (1, wide), 1)
    real = lane < fl

    @pl.loop(0, group // step)
    def _(r):
        at = pl.ds(pl.multiple_of(r * step, step), step)
        n = n_ref[pl.ds(r * 2, 2)].reshape(step, width)
        g = (g_ref[pl.ds(r * 2, 2)].reshape(step, width).astype(F32) * valid_ref[at, :]).astype(
            BF16
        )
        gy[at, :] = g
        z = jnp.dot(n, w_ref[:, :zc], preferred_element_type=F32)
        dm = lane_roll(jnp.dot(g, w_ref[:, off:], preferred_element_type=F32), -shift)
        gate, up = z[:, :wide], lane_roll(z, -fl)[:, :wide]
        cdf = 0.5 * (1.0 + lax.erf(gate * math.sqrt(0.5)))
        act = gate * cdf
        slope = cdf + gate * jnp.exp(-0.5 * gate * gate) * (1.0 / math.sqrt(2.0 * math.pi))
        m = lane_roll(jnp.where(real, act * up, 0.0), shift).astype(BF16)
        mm[at, :] = m
        d_gate = widen(jnp.where(real, dm * up * slope, 0.0), zc)
        d_up = lane_roll(widen(jnp.where(real, dm * act, 0.0), zc), fl)
        d = (d_gate + d_up).astype(BF16)
        dz[at, :] = d
        nt = (((1,), (1,)), ((), ()))
        dpart = lax.dot_general(d, w_ref[:, :zc], nt, preferred_element_type=F32)
        d_ref[pl.ds(r * 2, 2)] = dpart.astype(BF16).reshape(2, rows, width)
        ypart = lax.dot_general(m, w_ref[:, off:], nt, preferred_element_type=F32)
        y_ref[pl.ds(r * 2, 2)] = ypart.astype(BF16).reshape(2, rows, width)

    block = width // nh

    @pl.loop(0, nh)
    def _(i):
        cols = pl.ds(pl.multiple_of(i * block, block), block)
        tn = (((0,), (0,)), ((), ()))
        n = n_ref[:, :, cols].reshape(group, block)
        g_in = lax.dot_general(n, dz[...], tn, preferred_element_type=F32)
        g_down = lax.dot_general(gy[:, cols], mm[...], tn, preferred_element_type=F32)
        first = g_in[:, :off].astype(BF16)
        rest = jnp.concatenate(
            [g_in[:, off:] + g_down[:, : zc - off], g_down[:, zc - off :]], axis=1
        ).astype(BF16)
        if split_rows:
            ga_ref[:, i] = first.reshape(nb, block // nb, off)
            gb_ref[:, i] = rest.reshape(nb, block // nb, wide)
        else:
            ga_ref[pl.ds(i * block, block), :] = first
            gb_ref[pl.ds(i * block, block), :] = rest


def ffn(n2, g, valid, wm, fl, own_rows):
    nh, nb = dims()
    _, rows, width = n2.shape
    group = nh * rows
    total, zc, off = ff_widths(fl)
    split_rows = own_rows % 16 == 0
    lead = (nb, nh, own_rows) if split_rows else (width,)
    return pl.pallas_call(
        functools.partial(ffn_body, nh, nb, fl, split_rows),
        out_shape=(
            jax.ShapeDtypeStruct(n2.shape, BF16),
            jax.ShapeDtypeStruct(n2.shape, BF16),
            jax.ShapeDtypeStruct(lead + (off,), BF16),
            jax.ShapeDtypeStruct(lead + (total - off,), BF16),
        ),
        in_specs=[VM] * 4,
        out_specs=[VM] * 4,
        scratch_shapes=[
            pltpu.VMEM((group, width), BF16),
            pltpu.VMEM((group, total - off), BF16),
            pltpu.VMEM((group, zc), BF16),
        ],
        name="ffn",
        compiler_params=pltpu.CompilerParams(vmem_limit_bytes=60 << 20),
    )(n2, g, valid, wm)


def back_body(nh, nb, hl, dpart, ypart, hid_ref, g_ref, valid_ref, wo_ref, og_ref, gb_ref, y_ref, dh_ref, do_in, go_ref, gb_sum, n1, f1, o1, n2, f2, o2, dbuf, dg, dots, nearb, sumb, farb, s1, s2, gsem, qsem, pb, fb):
    pc = Place(nh, nb, hl)
    h, b = pc.h, pc.b
    signal_plane_and_head(pc, nh, nb)
    wait_plane_and_head(nh, nb)
    rows, width = hid_ref.shape
    hds = head_sums(nh, h, b, dpart, (n1, f1, o1), s1)
    hy = HeadSum(nh, h, b, ypart, n2, f2, o2, s2)
    hgs = head_gathers(nh, h, b, dbuf, dg, gsem)
    nk = nb // 2
    par, kb = b % 2, b // 2

    def pair_b(i):
        k = (kb + i) % nk
        return remote(
            gb_ref.at[k, 1 - par], nearb.at[k], pb.at[0, i], pb.at[1, i], h, b + 1 - 2 * par
        )

    def far_b(i):
        k = (kb + i) % nk
        return remote(sumb.at[k], farb.at[kb], fb.at[0, i], fb.at[1, i], h, 2 * k + par)

    def add_b(i):
        k = (kb + i) % nk
        pair_b(i).wait_recv()
        return (gb_ref[k, par].astype(F32) + nearb[k].astype(F32)).astype(BF16)

    def send_b(i):
        sumb[(kb + i) % nk] = add_b(i)
        far_b(i).start()

    for hd in hds:
        hd.start()

    @pl.loop(1, nk + 1)
    def _(i):
        pair_b(i % nk).start()

    for hd in hds:
        hd.send()
    size = rows // CHUNKS
    for j, (hd, hg) in enumerate(zip(hds, hgs)):
        at = pl.ds(j * size, size)
        normed, scale = norm_of(hid_ref[at, :])
        gy = g_ref[at, :].astype(F32) * valid_ref[at, :]
        dh = gy + norm_pull(hd.total(), normed, scale)
        dh_ref[at, :] = dh
        dbuf[at, :] = dh.astype(BF16)
        hg.start()
    hy.start()
    early = (nk - 1) // 2

    @pl.loop(1, 1 + early)
    def _(i):
        send_b(i)

    for hg in hgs:
        hg.pass_on()
    hy.send()
    for hd, hg in zip(hds, hgs):
        hd.finish()
        hg.finish()
    wo = wo_ref[...]
    lw = hl * DH
    nt = (((1,), (1,)), ((), ()))
    for i in range(nh):
        part = lax.dot_general(wo, dg[i], nt, preferred_element_type=F32).astype(BF16)
        dots[:, :, i * rows : (i + 1) * rows] = part.reshape(hl, DH, rows)
    queries_out(pc, dots, do_in, qsem, "start")
    og = og_ref[...].reshape(lw, nh * rows)
    go_ref[...] = jnp.dot(
        og, dg[...].reshape(nh * rows, width), preferred_element_type=F32
    ).astype(BF16)
    @pl.loop(1 + early, nk)
    def _(i):
        send_b(i)

    farb[kb] = add_b(0)
    y_ref[...] = valid_ref[...] * (hid_ref[...] + hy.total())
    hy.finish()

    @pl.loop(1, nk)
    def _(i):
        far_b(i).wait()

    @pl.loop(0, nk)
    def _(i):
        pair_b(i).wait_send()

    gb_sum[...] = jnp.sum(farb[...].astype(F32), axis=0).astype(BF16)
    queries_out(pc, dots, do_in, qsem, "wait_send")
    for zi in range(pc.nz):
        wait_on(do_in.at[zi], qsem.at[1, zi])


def back_exchange(dpart, ypart, hid, g, valid, wo, og, gb):
    nh, nb = dims()
    rows, width = hid.shape
    hl, _, group = og.shape
    nz = nb // (2 * (nb // (2 * hl)))
    return comm_call(
        functools.partial(back_body, nh, nb, hl),
        "back_exchange",
        4,
        (
            jax.ShapeDtypeStruct(hid.shape, F32),
            jax.ShapeDtypeStruct(hid.shape, F32),
            jax.ShapeDtypeStruct((nz, DH, group), BF16),
            jax.ShapeDtypeStruct((hl * DH, width), BF16),
            jax.ShapeDtypeStruct(gb.shape[2:], BF16),
        ),
        [VM] * 8,
        [VM, VM, ANY, VM, VM],
        HeadSum.buffers(nh, rows, width)
        + HeadSum.buffers(nh, rows, width)
        + [
            pltpu.VMEM((rows, width), BF16),
            pltpu.VMEM((nh, rows, width), BF16),
            pltpu.VMEM((hl, DH, group), BF16),
            pltpu.VMEM((nb // 2,) + gb.shape[2:], BF16),
            pltpu.VMEM((nb // 2,) + gb.shape[2:], BF16),
            pltpu.VMEM((nb // 2,) + gb.shape[2:], BF16),
            chunk_sems(nh),
            HeadSum.sem_shape(nh),
            chunk_sems(nh),
            pltpu.SemaphoreType.DMA((2, max(hl, nz))),
            pltpu.SemaphoreType.DMA((2, nb // 2)),
            pltpu.SemaphoreType.DMA((2, nb // 2)),
        ],
        (dpart, ypart, hid, g, valid, wo, og, gb),
        vmem=60 << 20,
    )


def grads_back_body(nh, nb, hl, dq_ref, dkv_ref, cos_ref, sin_ref, n1_ref, w_ref, gq_ref, dpart, got, sums, dq_out, dkv_out, dqkv, qsem, psem, ksem):
    pc = Place(nh, nb, hl)
    signal_plane(pc, nb)
    wait_plane(nb)
    rows = dkv_ref.shape[2]
    group = nh * rows
    width = n1_ref.shape[1]
    lw = hl * DH

    def pair(k):
        return remote(
            dkv_ref.at[:, 2 * k + 1 - pc.c], got.at[k], psem.at[0, k], psem.at[1, k], pc.sib, pc.b
        )

    def back(k, act):
        routed(
            pc,
            sums.at[k],
            dkv_out.at[pc.my_l, pc.u],
            ksem.at[0, k],
            ksem.at[1, pc.my_l * pc.cb + pc.u],
            pc.my_src_h,
            2 * k + pc.c,
            act,
        )

    half = nb // 2

    @pl.loop(0, half)
    def _(k):
        pair(k).start()

    queries_back(pc, dq_ref, dq_out, qsem, "start")

    @pl.loop(0, half)
    def _(k):
        pair(k).wait_recv()
        sums[k] = (dkv_ref[:, 2 * k + pc.c].astype(F32) + got[k].astype(F32)).astype(BF16)
        back(k, "start")

    @pl.loop(0, half)
    def _(k):
        pair(k).wait_send()
        back(k, "wait_send")

    queries_back(pc, dq_ref, dq_out, qsem, "wait_send")
    for l in range(hl):
        wait_on(dq_out.at[l], qsem.at[1, l])
    cos, sin = cos_ref[...], -sin_ref[...]
    for p in range(hl // 2):
        q = dq_out[2 * p : 2 * p + 2].reshape(2 * DH, group).astype(F32).T
        dqkv[:, p * 128 : (p + 1) * 128] = turned(q, cos, sin).astype(BF16)
    for l in range(hl):
        for u in range(pc.cb):
            wait_on(dkv_out.at[l, u], ksem.at[1, l * pc.cb + u])
    for p in range(hl // 2):
        even, odd = [
            jnp.sum(dkv_out[2 * p + i].astype(F32), axis=0).reshape(group, 2 * DH)
            for i in range(2)
        ]
        low = lanes_of(even) < DH
        k = jnp.where(low, even, lane_roll(odd, DH)).astype(BF16).astype(F32)
        v = jnp.where(low, lane_roll(even, DH), odd)
        dqkv[:, lw + p * 128 : lw + (p + 1) * 128] = turned(k, cos, sin).astype(BF16)
        dqkv[:, 2 * lw + p * 128 : 2 * lw + (p + 1) * 128] = v.astype(BF16)
    nt = (((1,), (1,)), ((), ()))
    tn = (((0,), (0,)), ((), ()))

    @pl.loop(0, nh)
    def _(i):
        cols = pl.ds(pl.multiple_of(i * (width // nh), width // nh), width // nh)
        gq_ref[cols, :] = lax.dot_general(
            n1_ref[:, cols], dqkv[...], tn, preferred_element_type=F32
        ).astype(BF16)
        at = pl.ds(pl.multiple_of(i * rows, rows), rows)
        dpart[i] = lax.dot_general(
            dqkv[at, :], w_ref[...], nt, preferred_element_type=F32
        ).astype(BF16)


def grads_back(dq, dkv, cos, sin, n1, wq, hl):
    nh, nb = dims()
    cb = nb // (2 * hl)
    nz = nb // (2 * cb)
    rows = dkv.shape[2]
    width = n1.shape[1]
    lw = hl * DH
    dma = pltpu.SemaphoreType.DMA
    return comm_call(
        functools.partial(grads_back_body, nh, nb, hl),
        "grads_back",
        5,
        (
            jax.ShapeDtypeStruct((width, 3 * lw), BF16),
            jax.ShapeDtypeStruct((nh, rows, width), BF16),
        ),
        [ANY] + [VM] * 5,
        [VM, VM],
        [
            pltpu.VMEM((nb // 2, nh, rows, 2 * DH), BF16),
            pltpu.VMEM((nb // 2, nh, rows, 2 * DH), BF16),
            pltpu.VMEM((hl,) + dq.shape[1:], BF16),
            pltpu.VMEM((hl, cb, nh, rows, 2 * DH), BF16),
            pltpu.VMEM((nh * rows, 3 * lw), BF16),
            dma((2, max(hl, nz))),
            dma((2, nb // 2)),
            dma((2, max(hl * cb, nb // 2))),
        ],
        (dq, dkv, cos, sin, n1, wq),
        vmem=60 << 20,
    )


def last_body(nh, nb, dpart, gq_ref, go_ref, gma_ref, gmb_ref, dn_ref, farq, faro, gma_all, gmb_all, near, far, out, nearq, sumq, nearo, sumo, ssem, pq, fq, po, fo, msem):
    h, b = me()
    signal_all(nh, nb, h, b)
    wait_all(nh, nb)
    nk = nb // 2
    y, kb = b % 2, b // 2
    other = b + 1 - 2 * y

    def pair_q(i):
        k = (kb + i) % nk
        return remote(gq_ref.at[:, k, 1 - y], nearq.at[k], pq.at[0, i], pq.at[1, i], h, other)

    pair_o = remote(go_ref.at[:, 1 - y], nearo, po.at[0], po.at[1], h, other)

    def far_q(i, j):
        k, th = (kb + i) % nk, (h + j) % nh
        slot = i * nh + j
        return remote(
            sumq.at[k, th], farq.at[h, kb], fq.at[0, slot], fq.at[1, slot], th, 2 * k + y
        )

    def far_o(i):
        k = (kb + i) % nk
        return remote(sumo.at[k], faro.at[kb], fo.at[0, i], fo.at[1, i], h, 2 * k + y)

    @pl.loop(1, nk + 1)
    def _(i):
        pair_q(i % nk).start()

    hs = HeadSum(nh, h, b, dpart, near, far, out, ssem)
    hs.start()
    pair_o.start()
    moves = []
    for n, (ref, dst) in enumerate(((gma_ref, gma_all), (gmb_ref, gmb_all))):
        for i in range(1, nh):
            th = (h + i) % nh
            moves.append(remote(ref.at[th], dst.at[h], msem.at[0, n, i], msem.at[1, n, i], th, b))
        moves.append(pltpu.make_async_copy(ref.at[h], dst.at[h], msem.at[0, n, 0]))
    for cp in moves:
        cp.start()
    hs.send()

    @pl.loop(1, nk)
    def _(i):
        k = (kb + i) % nk
        pair_q(i).wait_recv()
        sumq[k] = (gq_ref[:, k, y].astype(F32) + nearq[k].astype(F32)).astype(BF16)
        for j in range(nh):
            far_q(i, j).start()

    pair_q(0).wait_recv()
    sumq[kb] = (gq_ref[:, kb, y].astype(F32) + nearq[kb].astype(F32)).astype(BF16)
    for j in range(1, nh):
        far_q(0, j).start()
    farq[h, kb] = sumq[kb, h]
    pair_o.wait_recv()
    sumo[...] = (go_ref[:, y].astype(F32) + nearo[...].astype(F32)).astype(BF16)

    @pl.loop(1, nk)
    def _(i):
        far_o(i).start()

    faro[kb] = sumo[kb]
    dn_ref[...] = hs.total()
    hs.finish()
    for cp in moves:
        cp.wait()

    @pl.loop(1, nk)
    def _(i):
        for j in range(nh):
            far_q(i, j).wait()

    for j in range(1, nh):
        far_q(0, j).wait()

    @pl.loop(0, nk)
    def _(i):
        pair_q(i).wait_send()

    @pl.loop(1, nk)
    def _(i):
        far_o(i).wait()

    pair_o.wait_send()


def last_exchange(dpart, gq, go, gma, gmb):
    nh, nb = dims()
    _, rows, width = dpart.shape
    own_rows, cols = gq.shape[3:]
    nk = nb // 2
    dma = pltpu.SemaphoreType.DMA
    return comm_call(
        functools.partial(last_body, nh, nb),
        "last_exchange",
        6,
        (
            jax.ShapeDtypeStruct((rows, width), F32),
            jax.ShapeDtypeStruct((nh, nk, own_rows, cols), BF16),
            jax.ShapeDtypeStruct((nk, own_rows, width), BF16),
            jax.ShapeDtypeStruct(gma.shape, BF16),
            jax.ShapeDtypeStruct(gmb.shape, BF16),
        ),
        [VM] * 3 + [ANY] * 2,
        [VM] * 3 + [ANY] * 2,
        HeadSum.buffers(nh, rows, width)
        + [pltpu.VMEM((nk, nh, own_rows, cols), BF16)] * 2
        + [pltpu.VMEM((nk, own_rows, width), BF16)] * 2
        + [
            HeadSum.sem_shape(nh),
            dma((2, nk)),
            dma((2, nh * nk)),
            dma((2,)),
            dma((2, nk)),
            dma((2, 2, nh)),
        ],
        (dpart, gq, go, gma, gmb),
        vmem=60 << 20,
    )


def finish_body(nh, lw, fl, dn_ref, x_ref, dh_ref, y_in, farq, faro, gma, gmb, wq_ref, win_ref, ga_ref, gf_ref,
                y_ref, dx_ref, lna_ref, dq_ref, do_ref, lnm_ref, din_ref, dwd_ref):
    y_ref[...] = y_in[...]
    normed, scale = norm_of(x_ref[...].astype(F32))
    dx_ref[...] = dh_ref[...] + norm_pull(dn_ref[...], normed, scale)
    do_ref[...] = jnp.sum(faro[...].astype(F32), axis=0)
    width = nh * lw
    gain = ga_ref[...]
    rowsum = 0.0
    for i in range(nh):
        g = jnp.sum(farq[i].astype(F32), axis=0)
        for c in range(3):
            at = c * width + i * lw
            piece = g[:, c * lw : (c + 1) * lw]
            dq_ref[:, at : at + lw] = piece * gain
            rowsum = rowsum + jnp.sum(
                piece * wq_ref[:, at : at + lw].astype(F32), axis=1, keepdims=True
            )
    lna_ref[...] = rowsum
    ff = nh * fl
    total, _, _ = ff_widths(fl)
    tiles = lambda v: (v + 127) // 128 * 128
    gate_up, down = 0.0, 0.0
    for i in range(nh):
        piece = jnp.concatenate([gma[i].astype(F32), gmb[i].astype(F32)], axis=1)
        lane = lanes_of(piece)
        gate = widen(jnp.where(lane < fl, piece, 0.0), tiles(2 * ff))
        up = jnp.where(jnp.logical_and(lane >= fl, lane < 2 * fl), piece, 0.0)
        up = widen(up, tiles(2 * ff))
        gate_up = gate_up + lane_roll(gate, i * fl) + lane_roll(up, ff - fl + i * fl)
        dn = jnp.where(jnp.logical_and(lane >= 2 * fl, lane < 3 * fl), piece, 0.0)
        down = down + lane_roll(widen(dn, max(total, tiles(ff))), i * fl - 2 * fl)
    gate_up = gate_up[:, : 2 * ff]
    dwd_ref[...] = down[:, :ff]
    din_ref[...] = gate_up * gf_ref[...]
    lnm_ref[...] = jnp.sum(gate_up * win_ref[...].astype(F32), axis=1, keepdims=True)


def finish(dn, x, dh, y, farq, faro, gma, gmb, w_qkv, w_in, gain_attn, gain_mlp, fl):
    nh, _ = dims()
    rows, width = x.shape
    own_rows = w_qkv.shape[0]
    ff = nh * fl
    f32 = lambda *shape: jax.ShapeDtypeStruct(shape, F32)
    return pl.pallas_call(
        functools.partial(finish_body, nh, width // nh, fl),
        out_shape=(
            f32(rows, width),
            f32(rows, width),
            f32(own_rows, 1),
            f32(own_rows, 3 * width),
            f32(own_rows, width),
            f32(own_rows, 1),
            f32(own_rows, 2 * ff),
            f32(own_rows, ff),
        ),
        in_specs=[VM] * 12,
        out_specs=[VM] * 8,
        name="finish",
        compiler_params=pltpu.CompilerParams(vmem_limit_bytes=60 << 20),
    )(dn, x, dh, y, farq, faro, gma, gmb, w_qkv, w_in, gain_attn, gain_mlp)


def spans(rows_at, lengths):
    ends = jnp.cumsum(lengths)
    total = ends[-1]
    starts = ends - lengths
    inside = jnp.logical_and(rows_at[..., None] >= starts, rows_at[..., None] < ends)
    first = jnp.sum(jnp.where(inside, starts, 0), axis=-1)
    last = jnp.sum(jnp.where(inside, ends, 0), axis=-1)
    pad = rows_at >= total
    return jnp.where(pad, total, first), last, pad


def shards(layer_input, out_grad, lengths, ln_attn, w_qkv, w_attn_out, ln_mlp, w_in, w_mlp_out):
    nh, nb = dims()
    h, b = me()
    rows, width = layer_input.shape
    heads = width // DH
    hl = heads // nh
    lw = hl * DH
    group = nh * rows
    slots = nh * nb * rows
    own_rows = w_qkv.shape[0]
    ff = w_mlp_out.shape[0]
    fl = ff // nh
    total = ff_widths(fl)[0]
    cb = nb // (2 * hl)
    qs = 2 * cb
    nz = nb // qs

    gain_attn = ln_attn.astype(F32)[:, None]
    gain_mlp = ln_mlp.astype(F32)[:, None]
    xg, wm_h, wq = first_exchange(
        layer_input, w_qkv, gain_attn, w_in, gain_mlp, w_mlp_out.T, fl
    )
    wm = lax.all_gather(wm_h, "blk", axis=1, tiled=True).reshape(width, total)
    wq = wq.reshape(width, 3 * lw)

    row = lax.iota(jnp.int32, rows)
    group_at = ((lax.iota(jnp.int32, nh) * nb + b)[:, None] * rows + row).reshape(group)
    first, _, pad = spans(group_at, lengths)
    position = (group_at - first).astype(F32)
    half = DH // 2
    lane = lax.iota(jnp.int32, 2 * DH)
    inv_freq = jnp.power(ROPE_BASE, -2.0 * (lane % half).astype(F32) / DH)
    angles = position[:, None] * inv_freq[None, :]
    sign = jnp.where(lane % DH < half, -1.0, 1.0)
    cos, sin = jnp.cos(angles), jnp.sin(angles) * sign
    valid_group = jnp.where(pad, 0.0, 1.0)[:, None]
    own_at = (h * nb + b) * rows + row
    valid = jnp.where(spans(own_at, lengths)[2], 0.0, 1.0)[:, None]

    split = (b % cb) * 2 + h % 2
    tile_block = (
        lax.iota(jnp.int32, nh)[:, None, None] * nb
        + (lax.iota(jnp.int32, nz // 2)[None, :, None] * 2 + lax.iota(jnp.int32, 2)) * qs
        + split
    )
    tiles = nh * nz // 2
    query_at = (tile_block[..., None] * rows + row).reshape(tiles, 1, 2 * rows)
    q_first, q_last, q_pad = spans(query_at, lengths)
    q_last = jnp.where(q_pad, slots, q_last)
    lo = q_first[:, 0, 0] // KEY_BLOCK
    hi = (q_last[:, 0, -1] + KEY_BLOCK - 1) // KEY_BLOCK

    qin, kvin, n1, gg, wo = to_heads(xg, wq, cos, sin, out_grad, w_attn_out, hl)
    wo = wo.reshape(lw, width)
    kv_all = kvin.reshape(slots, 2 * DH)
    ot, of, lse = attend(qin, kv_all, q_first, q_last, lo, hi, rows)
    og, hid, n2 = mid_exchange(ot, wo, layer_input, hl)
    ypart, dpart, gma, gmb = ffn(n2, gg, valid_group, wm, fl, own_rows)
    if gma.ndim == 4:
        gma = lax.psum_scatter(gma, "blk", scatter_dimension=0, tiled=True)
        gmb = gmb.reshape((nb // 2, 2) + gmb.shape[1:])
    else:
        gma = gma.reshape(nh, nb * own_rows, gma.shape[1])
        gma = lax.psum_scatter(gma, "blk", scatter_dimension=1, tiled=True)
        gmb = gmb.reshape(nh, nb // 2, 2, own_rows, gmb.shape[1]).transpose(1, 2, 0, 3, 4)
    gma = gma.reshape(nh, own_rows, gma.shape[-1])
    y_out, dh, do_in, go, gmb = back_exchange(
        dpart, ypart, hid, out_grad, valid, wo, og, gmb
    )
    dq, dkv = attend_grad(qin, do_in, of, kv_all, q_first, q_last, lse, lo, hi, rows)
    gq, dpart1 = grads_back(dq, dkv.reshape(nh, nb, rows, 2 * DH), cos, sin, n1, wq, hl)
    dn, farq, faro, gma, gmb = last_exchange(
        dpart1,
        gq.reshape(nh, nb // 2, 2, own_rows, 3 * lw),
        go.reshape(nb // 2, 2, own_rows, width),
        gma,
        gmb,
    )
    y_out, dx, d_ln_attn, d_wqkv, d_wout, d_ln_mlp, d_win, d_wd = finish(
        dn, layer_input, dh, y_out, farq, faro, gma, gmb, w_qkv, w_in, gain_attn, gain_mlp, fl
    )
    return (
        y_out,
        dx,
        d_ln_attn.reshape(own_rows),
        d_wqkv,
        d_wout,
        d_ln_mlp.reshape(own_rows),
        d_win,
        d_wd.T,
    )


def solution(mesh):
    both = ("head", "blk")
    row_split = P(both, None)
    return jax.shard_map(
        shards,
        mesh=mesh,
        in_specs=(
            row_split,
            row_split,
            P(),
            P(both),
            row_split,
            row_split,
            P(both),
            row_split,
            P(None, both),
        ),
        out_specs=(
            row_split,
            row_split,
            P(both),
            row_split,
            row_split,
            P(both),
            row_split,
            P(None, both),
        ),
        check_vma=False,
    )
```

time: 386 us -> 337 us (0.87)
  local copies, waits for them, and re-layouts: 35.5 us -> 2.91 us
  matrix products: 29.8 us -> 0 us
  Pallas kernels: 286 us -> 310 us
  other arithmetic: 21.1 us -> 11.2 us
    dot_general x14 -> x0, matrix products: 29.8 us -> none  [dot(): lax.dot_general(a, b, (((ca,), (cb,)), ((), ())), preferred_element_type=...]
    pallas_call x0 -> x2, Pallas kernels: none -> 19.4 us  [the longest x1 15 us: ffn(): pl.pallas_call(functools.partial(ffn_body, nh, nb, fl, split_rows), out_s...]
    unnamed x78 -> x6, local copies, waits for them, and re-layouts: 10.9 us -> 0.01 us
    reshape x11 -> x0, local copies, waits for them, and re-layouts: 7.76 us -> none  [the longest x3 1.94 us: shards(): win_own = win_own.reshape(nh, own_rows, 2 * fl)]
    pallas_call x8 -> x6, Pallas kernels: 247 us -> 255 us  [comm_call(): pl.pallas_call(body, out_shape=out_shape, in_specs=in_specs, out_specs=ou...]
    concatenate x1 -> x0, local copies, waits for them, and re-layouts: 6.52 us -> none  [shards(): jnp.concatenate([g_in, g_down], axis=1).reshape(nh, nb * own_rows, 3 * fl)]
    dot_general x4 -> x0, local copies, waits for them, and re-layouts: 6.04 us -> none  [dot(): lax.dot_general(a, b, (((ca,), (cb,)), ((), ())), preferred_element_type=...]
    convert_element_type x9 -> x0, other arithmetic: 5.76 us -> none  [the longest x1 3.01 us: shards(): (gg.reshape(group, width).astype(F32) * valid_group[:, None]).astype(BF16)]
  transfers between devices with their start and end apart: 2 -> 2, of which waited for: 0 -> 0; matrix products, arithmetic and copies ran while one was open for 10% -> 3% of each run, Pallas kernels for 47% -> 63%
where the time goes in v2:
time: 337 us; the launch traced here: 339 us
  Pallas kernels  310 us (92%)
  between operations  14.2 us (4%)
  other arithmetic  11.2 us (3%)
    pallas_call x6, Pallas kernels, comm_call(): pl.pallas_call(body, out_shape=out_shape, in_specs=in_specs, out_specs=ou...  255 us
    pallas_call x1, Pallas kernels, attend_grad(): pl.pallas_call(attend_grad_body, grid_spec=pltpu.PrefetchScalarGridSpec(n...  18.5 us
    pallas_call x1, Pallas kernels, attend(): pl.pallas_call(attend_body, grid_spec=pltpu.PrefetchScalarGridSpec(num_sc...  17.4 us
    pallas_call x1, Pallas kernels, ffn(): pl.pallas_call(functools.partial(ffn_body, nh, nb, fl, split_rows), out_s...  15 us
  transfers between devices with their start and end apart: 2, of which 0 were waited for; matrix products, arithmetic and copies ran while one was open for 3% of the time, Pallas kernels for 63%

profile of v2, /device:TPU:0, one launch (start us, length us, event | category | flops | bytes accessed | tf_op | source)
XLA Modules:
  0.0 338.5 jit_solution(2676679238020070033)
XLA Ops:
  7.2 0.7 bitcast_convert_fusion.1
  7.9 0.7 copy.26.ga_ref
  8.6 0.7 bitcast_convert_fusion
  9.2 0.7 copy.27.gf_ref
  9.9 39.0 %first_exchange.1 = (bf16[4,128,1024]{2,1,0:T(8,128)(2,1)}, bf16[4,32,2048]{2,1,0:T(8,128)(2,1)}, bf16[32,32,768]{2,1,0:T(8,128)(2,1)}) custom-call(bf16[128,1024]{1,0:T(8,128)(2,1)} %x_ref.5, bf16[32,3072]{1,0:T(8,128)(2,1)} %wq_ref.3, f32[32,1]{1,0:T(8,128)} %copy.26.ga_ref, bf16[32,5248]{1,0:T(8,128)(2,1)} %win_ref.1, f32[32,1]{1,0:T(8,128)} %copy.27.gf_ref, ...), custom_call_target="tpu_custom_call" | custom-call | tf_op jit(solution)/shard_map/first_exchange/pallas_call | solution.py:35
  49.0 0.2 reduce-window.4
  49.1 0.6 slice.12
  49.7 0.7 fusion.5
  50.5 0.9 copy.28.valid_ref
  51.3 0.1 fusion.4
  51.4 0.1 select_reduce_fusion.2
  51.5 0.7 subtract_convert_fusion
  52.2 1.8 fusion
  54.0 49.8 %to_heads.1 = (bf16[4,64,512]{2,1,0:T(8,128)(2,1)}, bf16[4,8,128,128]{3,2,1,0:T(8,128)(2,1)}, bf16[512,1024]{1,0:T(8,128)(2,1)}, bf16[4,128,1024]{2,1,0:T(8,128)(2,1)}, bf16[8,32,1024]{2,1,0:T(8,128)(2,1)}) custom-call(bf16[4,128,1024]{2,1,0:T(8,128)(2,1)} %get-tuple-element.48.xg_hbm, bf16[1024,768]{1,0:T(8,128)(2,1)} %bitcast.33, ...), custom_call_target="tpu_custom_call" | custom-call | tf_op jit(solution)/shard_map/to_heads/pallas_call | solution.py:35
  103.9 0.1 add_multiply_fusion
  104.0 0.1 add.189
  104.1 0.1 select_reduce_fusion
  104.1 0.7 compare_select_fusion
  104.8 0.4 slice_reduce_fusion
  105.2 0.5 and_select_fusion.2.hi_ref
  105.8 0.5 and_select_fusion.3.lo_ref
  106.3 17.4 %attend.1 = (bf16[4,64,512]{2,1,0:T(8,128)(2,1)}, f32[4,64,512]{2,1,0:T(8,128)}, f32[8,1,256]{2,1,0:T(1,128)}) custom-call(s32[8]{0:T(128)} %and_select_fusion.3.lo_ref, s32[8]{0:T(128)} %and_select_fusion.2.hi_ref, bf16[4,64,512]{2,1,0:T(8,128)(2,1)} %get-tuple-element.50.q_ref, bf16[4096,128]{1,0:T(8,128)(2,1)} %bitcast.36, s32[8,1,256]{2,1,0:T(1,128)} %copy-done.1, ...), custom_call_target="tpu_custom_call" | custom-call | tf_op jit(solution)/shard_map/attend/pallas_call | solution.py:572
  123.6 33.8 %mid_exchange.1 = (bf16[4,64,512]{2,1,0:T(8,128)(2,1)}, f32[128,1024]{1,0:T(8,128)}, bf16[4,128,1024]{2,1,0:T(8,128)(2,1)}) custom-call(bf16[4,64,512]{2,1,0:T(8,128)(2,1)} %get-tuple-element.52.o_ref, bf16[256,1024]{1,0:T(8,128)(2,1)} %bitcast.38, bf16[128,1024]{1,0:T(8,128)(2,1)} %x_ref.5), custom_call_target="tpu_custom_call" | custom-call | tf_op jit(solution)/shard_map/mid_exchange/pallas_call | solution.py:35
  157.5 15.0 %ffn.1 = (bf16[4,128,1024]{2,1,0:T(8,128)(2,1)}, bf16[4,128,1024]{2,1,0:T(8,128)(2,1)}, bf16[8,4,32,1280]{3,2,1,0:T(8,128)(2,1)}, bf16[8,4,32,768]{3,2,1,0:T(8,128)(2,1)}) custom-call(bf16[4,128,1024]{2,1,0:T(8,128)(2,1)} %get-tuple-element.54.n_ref, bf16[4,128,1024]{2,1,0:T(8,128)(2,1)} %get-tuple-element.55.g_ref, f32[512,1]{1,0:T(8,128)} %copy.28.valid_ref, ...), custom_call_target="tpu_custom_call" | custom-call | tf_op jit(solution)/shard_map/ffn/pallas_call | solution.py:898
  172.5 1.3 fusion.1.valid_ref
  173.8 55.5 %back_exchange.1 = (f32[128,1024]{1,0:T(8,128)}, f32[128,1024]{1,0:T(8,128)}, bf16[4,64,512]{2,1,0:T(8,128)(2,1)}, bf16[256,1024]{1,0:T(8,128)(2,1)}, bf16[4,32,768]{2,1,0:T(8,128)(2,1)}) custom-call(bf16[4,128,1024]{2,1,0:T(8,128)(2,1)} %get-tuple-element.57.dpart, bf16[4,128,1024]{2,1,0:T(8,128)(2,1)} %get-tuple-element.58.ypart, ...), custom_call_target="tpu_custom_call" | custom-call | tf_op jit(solution)/shard_map/back_exchange/pallas_call | solution.py:35
  229.3 18.5 %attend_grad.1 = (bf16[4,64,512]{2,1,0:T(8,128)(2,1)}, bf16[4096,128]{1,0:T(8,128)(2,1)}) custom-call(s32[8]{0:T(128)} %and_select_fusion.3.lo_ref, s32[8]{0:T(128)} %and_select_fusion.2.hi_ref, bf16[4,64,512]{2,1,0:T(8,128)(2,1)} %get-tuple-element.50.q_ref, bf16[4,64,512]{2,1,0:T(8,128)(2,1)} %get-tuple-element.62.do_ref, ...), custom_call_target="tpu_custom_call" | custom-call | tf_op jit(solution)/shard_map/attend_grad/pallas_call | solution.py:643
  247.9 36.8 %grads_back.1 = (bf16[1024,768]{1,0:T(8,128)(2,1)}, bf16[4,128,1024]{2,1,0:T(8,128)(2,1)}) custom-call(bf16[4,64,512]{2,1,0:T(8,128)(2,1)} %get-tuple-element.65.dq_ref, bf16[4,8,128,128]{3,2,1,0:T(8,128)(2,1)} %bitcast.42, f32[512,128]{1,0:T(8,128)} %get-tuple-element.93.cos_ref, f32[512,128]{1,0:T(8,128)} %get-tuple-element.92.sin_ref, ...), custom_call_target="tpu_custom_call" | custom-call | tf_op jit(solution)/shard_map/grads_back/pallas_call | solution.py:35
  284.7 40.0 %last_exchange.1 = (f32[128,1024]{1,0:T(8,128)}, bf16[4,4,32,768]{3,2,1,0:T(8,128)(2,1)}, bf16[4,32,1024]{2,1,0:T(8,128)(2,1)}, bf16[4,32,1280]{2,1,0:T(8,128)(2,1)}, bf16[4,32,768]{2,1,0:T(8,128)(2,1)}) custom-call(bf16[4,128,1024]{2,1,0:T(8,128)(2,1)} %get-tuple-element.68.dpart, bf16[4,4,2,32,768]{4,3,2,1,0:T(8,128)(2,1)} %bitcast.40, ...), custom_call_target="tpu_custom_call" | custom-call | tf_op jit(solution)/shard_map/last_exchange/pallas_call | solution.py:35
  324.6 4.4 %finish.1 = (f32[128,1024]{1,0:T(8,128)}, f32[128,1024]{1,0:T(8,128)}, f32[32,1]{1,0:T(8,128)}, f32[32,3072]{1,0:T(8,128)}, f32[32,1024]{1,0:T(8,128)}, /*index=...) custom-call(f32[128,1024]{1,0:T(8,128)} %get-tuple-element.73.dn_ref, bf16[128,1024]{1,0:T(8,128)(2,1)} %x_ref.5, ...), custom_call_target="tpu_custom_call" | custom-call | tf_op jit(solution)/shard_map/finish/pallas_call | solution.py:1331
  329.0 1.3 reduce.4
  330.4 1.3 reduce.5
  (20 shorter events, 0.3 us)
Async XLA Ops:
  7.2 41.8 %copy-start.2 = (s32[4]{0:T(128)S(1)}, s32[4]{0:T(128)}, u32[]{:S(2)}) copy-start(s32[4]{0:T(128)} %param.11) | copy-start | bytes 52
  7.2 150.3 %all-gather.2.cloned.1.call-start = ((), (), s32[]{:S(2)}) async-start(), calls=%async_computation.1 | async-start | bytes 4718592 | tf_op jit(solution)/shard_map/all_gather | solution.py:1383
  48.9 235.8 %reduce-scatter.2.cloned.1.call-start = ((), (), s32[]{:S(2)}) async-start(), calls=%async_computation.2 | async-start | bytes 2949120 | tf_op jit(solution)/shard_map/reduce_scatter | solution.py:1420
  104.8 1.5 copy-start
  104.8 1.5 copy-start.1
Sparse Core Ops, SparseCore 0:
  49.0 96.9 all-gather.1
  172.6 104.3 reduce-scatter.1

commit v3 on v2

v3 whole, which is shorter than its diff:
```python
import functools
import math

import jax
import jax.numpy as jnp
from jax import lax
from jax.experimental import pallas as pl
from jax.experimental.pallas import tpu as pltpu
from jax.sharding import PartitionSpec as P

DH = 64
ROPE_BASE = 160000.0
NORM_EPS = 1e-05
MASK_FLOOR = -1e30
KEY_BLOCK = 512
GRAD_CUT = 1280
EXP_SCALE = 0.125 * math.log2(math.e)
BF16 = jnp.bfloat16
F32 = jnp.float32
MESH_ID = pl.DeviceIdType.MESH
ANY = pl.BlockSpec(memory_space=pl.ANY)
VM = pl.BlockSpec(memory_space=pltpu.VMEM)
SM = pl.BlockSpec(memory_space=pltpu.SMEM)


def dims():
    nh = lax.axis_size("head")
    nb = lax.axis_size("blk")
    return nh, nb


def me():
    return lax.axis_index("head"), lax.axis_index("blk")


def comm_call(body, name, cid, out_shape, in_specs, out_specs, scratch, args, vmem=None):
    return pl.pallas_call(
        body,
        out_shape=out_shape,
        in_specs=in_specs,
        out_specs=out_specs,
        scratch_shapes=scratch,
        name=name,
        compiler_params=pltpu.CompilerParams(
            collective_id=cid, has_side_effects=True, vmem_limit_bytes=vmem
        ),
    )(*args)


def remote(src, dst, send, recv, h, b):
    return pltpu.make_async_remote_copy(
        src_ref=src,
        dst_ref=dst,
        send_sem=send,
        recv_sem=recv,
        device_id=(h, b),
        device_id_type=MESH_ID,
    )


def signal(h, b):
    pl.semaphore_signal(
        pltpu.get_barrier_semaphore(), inc=1, device_id=(h, b), device_id_type=MESH_ID
    )


def signal_head(nh, h, b):
    for i in range(1, nh):
        signal((h + i) % nh, b)


def wait_head(nh):
    pl.semaphore_wait(pltpu.get_barrier_semaphore(), nh - 1)


def signal_all(nh, nb, h, b):
    @pl.loop(1, nh * nb)
    def _(i):
        signal((h + i // nb) % nh, (b + i % nb) % nb)


def wait_all(nh, nb):
    pl.semaphore_wait(pltpu.get_barrier_semaphore(), nh * nb - 1)


class HeadGather:
    def __init__(self, nh, h, b, src, dst, sems):
        self.nh, self.h, self.b, self.dst, self.sems = nh, h, b, dst, sems
        nx = nh // 2
        self.nx = nx
        x, c = h // 2, h % 2
        sib = x * 2 + 1 - c
        self.sib = sib
        self.across = []
        for k in range(1, nx):
            self.across.append(
                remote(src, dst.at[h], sems.at[0, k], sems.at[1, k], ((x + k) % nx) * 2 + c, b)
            )
        self.near = remote(src, dst.at[h], sems.at[0, 0], sems.at[1, 0], sib, b)
        self.local = pltpu.make_async_copy(src, dst.at[h], sems.at[2, 0])
        self.forward = []
        for k in range(1, nx):
            got = ((x + nx - k) % nx) * 2 + c
            self.forward.append(
                remote(dst.at[got], dst.at[got], sems.at[2, k], sems.at[3, k], sib, b)
            )

    @staticmethod
    def sem_shape(nh):
        return pltpu.SemaphoreType.DMA((4, nh // 2))

    def start(self):
        for cp in self.across:
            cp.start()
        self.near.start()
        self.local.start()

    def pass_on(self):
        for cp, fw in zip(self.across, self.forward):
            cp.wait_recv()
            fw.start()

    def finish(self):
        for cp in self.across:
            cp.wait_send()
        self.near.wait()
        self.local.wait()
        for fw in self.forward:
            fw.wait()


def lane_roll(values, shift):
    return pltpu.roll(values, shift % values.shape[1], 1)


def lanes_of(values):
    return lax.broadcasted_iota(jnp.int32, (1, values.shape[1]), 1)


def widen(values, width):
    extra = width - values.shape[1]
    if extra <= 0:
        return values[:, :width]
    return jnp.concatenate([values, jnp.zeros((values.shape[0], extra), values.dtype)], axis=1)


def column(row):
    n = row.shape[1]
    same = lax.broadcasted_iota(jnp.int32, (n, n), 0) == lax.broadcasted_iota(jnp.int32, (n, n), 1)
    return jnp.sum(jnp.where(same, row, 0.0), axis=1, keepdims=True)


def as_row(col):
    n = col.shape[0]
    same = lax.broadcasted_iota(jnp.int32, (n, n), 0) == lax.broadcasted_iota(jnp.int32, (n, n), 1)
    return jnp.sum(jnp.where(same, col, 0.0), axis=0, keepdims=True)


def sequence_ends(len_ref):
    ends, total = [], 0
    for i in range(len_ref.shape[0]):
        total = total + len_ref[i]
        ends.append(total)
    return ends


def segment_first(slot, ends):
    first = jnp.zeros_like(slot)
    for end in ends:
        first = jnp.where(slot >= end, end, first)
    return first


def segment_end(slot, ends, slots):
    last = jnp.zeros_like(slot) + slots
    for end in reversed(ends):
        last = jnp.where(slot < end, end, last)
    return last


def half_pick(low_src, high_src, low_at, high_at):
    low = low_src if low_at == 0 else lane_roll(low_src, DH)
    high = high_src if high_at == 1 else lane_roll(high_src, DH)
    return jnp.where(lanes_of(low) < DH, low, high)


def ff_widths(fl):
    up = lambda v: (v + 127) // 128 * 128
    return up(3 * fl), up(2 * fl), 2 * fl // 128 * 128


class LineGather:
    def __init__(self, pc, src, place, sems):
        self.pc, self.src, self.place, self.sems = pc, src, place, sems

    @staticmethod
    def sem_shape(nz):
        return pltpu.SemaphoreType.DMA((5, nz))

    def origin(self, t, up):
        return self.pc.zi - t if up else self.pc.zi + t

    def move(self, t, up):
        pc = self.pc
        at = self.place(self.origin(t, up))
        n = 0 if up else 2
        return remote(
            self.src if t == 0 else at,
            at,
            self.sems.at[n, t],
            self.sems.at[n + 1, t],
            pc.h,
            pc.b + pc.qs if up else pc.b - pc.qs,
        )

    def sends(self, t, up):
        zi, nz = self.pc.zi, self.pc.nz
        if up:
            return jnp.logical_and(zi - t >= 0, zi + 1 < nz)
        return jnp.logical_and(zi + t < nz, zi - 1 >= 0)

    def local(self):
        return pltpu.make_async_copy(self.src, self.place(self.pc.zi), self.sems.at[4, 0])

    def start(self):
        for up in (True, False):

            @pl.when(self.sends(0, up))
            def _():
                self.move(0, up).start()

        self.local().start()

    def step(self, t, arrived=None):
        low = self.pc.zi < self.pc.nz // 2
        self.take(t, False, jnp.logical_not(low), arrived)
        self.take(t, True, True, arrived)
        self.take(t, False, low, arrived)

    def take(self, t, up, now, arrived):
        zi, nz = self.pc.zi, self.pc.nz
        origin = self.origin(t, up)
        here = jnp.logical_and(now, origin >= 0 if up else origin < nz)

        @pl.when(here)
        def _():
            wait_on(self.place(origin), self.sems.at[1 if up else 3, t - 1])

        if t < nz - 1:

            @pl.when(jnp.logical_and(now, self.sends(t, up)))
            def _():
                self.move(t, up).start()

        if arrived is not None:

            @pl.when(here)
            def _():
                arrived(origin)

    def finish(self):
        self.local().wait()
        for t in range(self.pc.nz - 1):
            for up in (True, False):

                @pl.when(self.sends(t, up))
                def _():
                    self.move(t, up).wait_send()


class BlkGather:
    def __init__(self, pc, src, out, sems, ssem):
        self.pc, self.out, self.ssem, self.src = pc, out, ssem, src
        self.line = LineGather(pc, src, lambda zi: out.at[:, zi, pc.s], sems)

    @staticmethod
    def sem_shapes(nz, qs):
        return [LineGather.sem_shape(nz), pltpu.SemaphoreType.DMA((2, nz, qs))]

    def side(self, zi, ds, own=False):
        pc = self.pc
        ref = self.out.at[:, zi, pc.s]
        return remote(
            self.src if own else ref,
            ref,
            self.ssem.at[0, zi, ds],
            self.ssem.at[1, zi, ds],
            pc.h,
            pc.zi * pc.qs + (pc.s + ds) % pc.qs,
        )

    def spread(self, zi, own=False):
        for ds in range(1, self.pc.qs):
            self.side(zi, ds, own).start()

    def start(self):
        self.line.start()
        self.spread(self.pc.zi, True)

    def step(self, t):
        self.line.step(t, self.spread)

    def finish(self):
        self.line.finish()

        @pl.loop(0, self.pc.nz)
        def _(zi):
            for ds in range(1, self.pc.qs):
                self.side(zi, ds).wait()


class LineSum:
    def __init__(self, pc, term, sent, got, sems):
        self.pc, self.term, self.sent, self.got, self.sems = pc, term, sent, got, sems

    @staticmethod
    def scratch(nz, shape):
        return [
            pltpu.VMEM((2, nz) + shape, BF16),
            pltpu.VMEM((2, nz) + shape, BF16),
            pltpu.SemaphoreType.DMA((4, nz)),
        ]

    def move(self, d, up):
        pc = self.pc
        n = 0 if up else 1
        return remote(
            self.sent.at[n, d],
            self.got.at[n, d],
            self.sems.at[2 * n, d],
            self.sems.at[2 * n + 1, d],
            pc.h,
            pc.b + pc.qs if up else pc.b - pc.qs,
        )

    def takes(self, up):
        return self.pc.zi > 0 if up else self.pc.zi < self.pc.nz - 1

    def lead(self, j):
        self.step(j, False)

    def follow(self, j):
        self.step(j, True)

    def step(self, j, taking):
        low = self.pc.zi < self.pc.nz // 2
        if taking:
            self.one(j, False, jnp.logical_not(low), True)
            self.one(j, True, True, True)
            self.one(j, False, low, True)
        else:
            self.one(j, True, True, False)
            self.one(j, False, True, False)

    def one(self, j, up, now, taking):
        zi, nz = self.pc.zi, self.pc.nz
        d = nz - 1 - j if up else j
        n = 0 if up else 1
        takes = self.takes(up)
        far = jnp.logical_and(now, zi < d if up else zi > d)

        @pl.when(jnp.logical_and(far, takes if taking else jnp.logical_not(takes)))
        def _():
            if taking:
                wait_on(self.got.at[n, d], self.sems.at[2 * n + 1, d])
                self.sent[n, d] = (self.term(d) + self.got[n, d].astype(F32)).astype(BF16)
            else:
                self.sent[n, d] = self.term(d).astype(BF16)
            self.move(d, up).start()

    def total(self, total_ref):
        zi = self.pc.zi
        total_ref[...] = self.term(zi)
        for up in (True, False):
            n = 0 if up else 1

            @pl.when(self.takes(up))
            def _():
                wait_on(self.got.at[n, zi], self.sems.at[2 * n + 1, zi])
                total_ref[...] += self.got[n, zi].astype(F32)

    def finish(self):
        zi, nz = self.pc.zi, self.pc.nz
        for j in range(nz - 1):
            for up in (True, False):
                d = nz - 1 - j if up else j

                @pl.when(zi < d if up else zi > d)
                def _():
                    self.move(d, up).wait_send()


class StretchSum:
    def __init__(self, pc, part, got, sems):
        self.pc, self.part, self.got, self.sems = pc, part, got, sems

    @staticmethod
    def scratch(nz, shape):
        return [pltpu.VMEM((nz,) + shape, BF16), pltpu.SemaphoreType.DMA((2, nz))]

    def move(self, i):
        pc = self.pc
        to = (pc.zi + i) % pc.nz
        return remote(
            self.part.at[to],
            self.got.at[pc.zi],
            self.sems.at[0, i],
            self.sems.at[1, i],
            pc.h,
            to * pc.qs + pc.s,
        )

    def start(self):
        for i in range(1, self.pc.nz):
            self.move(i).start()

    def total(self):
        pc = self.pc
        total = self.part[pc.zi].astype(F32)
        for i in range(1, pc.nz):
            self.move(i).wait_recv()
            total = total + self.got[(pc.zi + pc.nz - i) % pc.nz].astype(F32)
        return total

    def finish(self):
        for i in range(1, self.pc.nz):
            self.move(i).wait_send()


class PlaneWeights:
    def __init__(self, pc, pack, out, sems, ksem):
        self.pc, self.pack, self.out, self.sems, self.ksem = pc, pack, out, sems, ksem

    @staticmethod
    def sem_shapes(nh, nz, qs):
        dma = pltpu.SemaphoreType.DMA
        return [dma((2, nz)), dma((4, nh // 2 * qs))]

    def along(self, i):
        pc = self.pc
        to = (pc.zi + i) % pc.nz
        return remote(
            self.pack.at[to],
            self.out.at[pc.h, pc.zi, pc.s],
            self.sems.at[0, i],
            self.sems.at[1, i],
            pc.h,
            to * pc.qs + pc.s,
        )

    def local(self):
        pc = self.pc
        return pltpu.make_async_copy(
            self.pack.at[pc.zi], self.out.at[pc.h, pc.zi, pc.s], self.sems.at[0, 0]
        )

    def place(self, i, sign):
        pc = self.pc
        nx = pc.nh // 2
        dx, ds = i // pc.qs, i % pc.qs
        if sign < 0:
            dx, ds = nx - dx, pc.qs - ds
        return ((pc.x + dx) % nx) * 2 + pc.c, (pc.s + ds) % pc.qs

    def across(self, i):
        pc = self.pc
        th, ts = self.place(i, 1)
        ref = self.out.at[pc.h, :, pc.s]
        return remote(
            ref, ref, self.ksem.at[0, i], self.ksem.at[1, i], th, pc.zi * pc.qs + ts
        )

    def near(self, i):
        pc = self.pc
        gh, gs = self.place(i, -1)
        ref = self.out.at[gh, :, gs]
        return remote(ref, ref, self.ksem.at[2, i], self.ksem.at[3, i], pc.sib, pc.b)

    def start(self):
        for i in range(1, self.pc.nz):
            self.along(i).start()
        self.local().start()

    def spread(self):
        pc = self.pc
        self.local().wait()
        for i in range(1, pc.nz):
            self.along(i).wait_recv()

        @pl.loop(1, pc.nh // 2 * pc.qs)
        def _(i):
            self.across(i).start()

        self.near(0).start()

    def pass_on(self):
        @pl.loop(1, self.pc.nh // 2 * self.pc.qs)
        def _(i):
            self.across(i).wait_recv()
            self.near(i).start()

    def finish(self):
        for i in range(1, self.pc.nz):
            self.along(i).wait_send()

        @pl.loop(1, self.pc.nh // 2 * self.pc.qs)
        def _(i):
            self.across(i).wait_send()

        @pl.loop(0, self.pc.nh // 2 * self.pc.qs)
        def _(i):
            self.near(i).wait()


def first_body(nh, nb, hl, fl, len_ref, x_ref, wq_ref, ga_ref, win_hbm, gf_ref, wd_hbm, g_ref, n1_all, wma, wmb, wq_all, gg, cos_ref, sin_ref, own_n, pack, wmp, win_ref, wd_ref, lsem, wsem, ksem, gsem, msem, stage):
    pc = Place(nh, nb, hl)
    h, b = pc.h, pc.b
    loads = [
        pltpu.make_async_copy(win_hbm, win_ref, stage.at[0]),
        pltpu.make_async_copy(wd_hbm, wd_ref, stage.at[1]),
    ]
    for cp in loads:
        cp.start()
    signal_all(nh, nb, h, b)
    width = x_ref.shape[1]
    lw = width // pc.nz
    gain = column(ga_ref[...].astype(F32))
    for c in range(3):
        w = wq_ref[:, c * width : (c + 1) * width].astype(F32) * gain
        tile = lambda l, i: w[:, l * pc.nz * DH + i // 2 * 128 : l * pc.nz * DH + i // 2 * 128 + 128]
        for i in range(pc.nz):
            for p in range(nh // 2):
                both = half_pick(tile(2 * p, i), tile(2 * p + 1, i), i % 2, i % 2)
                at = c * lw + p * 128
                pack[i, :, at : at + 128] = both.astype(BF16)
    own_n[...] = norm_of(x_ref[...].astype(F32))[0].astype(BF16)
    wait_all(nh, nb)
    weights = PlaneWeights(pc, pack, wq_all, wsem, ksem)
    line = LineGather(pc, own_n, lambda zi: n1_all.at[zi], lsem)
    gather = HeadGather(nh, h, b, g_ref, gg, gsem)
    weights.start()
    line.start()
    gather.start()
    for cp in loads:
        cp.wait()
    total, _, off = ff_widths(fl)
    ff = nh * fl
    win = win_ref[...].astype(F32) * column(gf_ref[...].astype(F32))
    wd = widen(wd_ref[...].astype(F32), total if total > ff else (ff + 127) // 128 * 128)
    lane = lax.broadcasted_iota(jnp.int32, (1, total), 1)
    for i in range(nh):
        gate = widen(lane_roll(win, -i * fl), total)
        up = widen(lane_roll(win, fl - ff - i * fl), total)
        down = widen(lane_roll(wd, 2 * fl - i * fl), total)
        piece = jnp.where(
            lane < fl,
            gate,
            jnp.where(lane < 2 * fl, up, jnp.where(lane < 3 * fl, down, 0.0)),
        )
        wmp[i] = piece.astype(BF16)
    copies = []
    for n, (dst, cols) in enumerate(((wma, pl.ds(0, off)), (wmb, pl.ds(off, total - off)))):
        for i in range(1, nh):
            th = (h + i) % nh
            src = wmp.at[th, :, cols]
            copies.append(remote(src, dst.at[h], msem.at[0, n, i], msem.at[1, n, i], th, b))
        copies.append(pltpu.make_async_copy(wmp.at[h, :, cols], dst.at[h], msem.at[0, n, 0]))
    weights.spread()
    for cp in copies:
        cp.start()
    ends = sequence_ends(len_ref)
    rows = x_ref.shape[0]
    lane = lax.broadcasted_iota(jnp.int32, (1, 2 * DH), 1)
    power = (lane % (DH // 2)).astype(F32) * (-2.0 / DH)
    inv_freq = jnp.exp2(power * math.log2(ROPE_BASE))
    sign = jnp.where(lane % DH < DH // 2, -1.0, 1.0)
    line.step(1)
    for i in range(pc.nz):
        slot = (h * nb + i * pc.qs + pc.s) * rows + lax.broadcasted_iota(jnp.int32, (rows, 1), 0)
        angle = (slot - segment_first(slot, ends)).astype(F32) * inv_freq
        cos_ref[i * rows : (i + 1) * rows, :] = jnp.cos(angle)
        sin_ref[i * rows : (i + 1) * rows, :] = jnp.sin(angle) * sign
    gather.pass_on()
    for t in range(2, pc.nz):
        line.step(t)
    weights.pass_on()
    for cp in copies:
        cp.wait()
    weights.finish()
    line.finish()
    gather.finish()


def first_exchange(lengths, x, w_qkv, gain_attn, w_in, gain_mlp, wd_t, g, hl, fl):
    nh, nb = dims()
    rows, width = x.shape
    nz, qs = hl, nb // hl
    lw = width // nz
    own_rows = w_in.shape[0]
    total, _, off = ff_widths(fl)
    dma = pltpu.SemaphoreType.DMA
    return comm_call(
        functools.partial(first_body, nh, nb, hl, fl),
        "first_exchange",
        0,
        (
            jax.ShapeDtypeStruct((nz, rows, width), BF16),
            jax.ShapeDtypeStruct((nh, own_rows, off), BF16),
            jax.ShapeDtypeStruct((nh, own_rows, total - off), BF16),
            jax.ShapeDtypeStruct((nh, nz, qs, own_rows, 3 * lw), BF16),
            jax.ShapeDtypeStruct((nh, rows, width), BF16),
            jax.ShapeDtypeStruct((nz * rows, 2 * DH), F32),
            jax.ShapeDtypeStruct((nz * rows, 2 * DH), F32),
        ),
        [SM, VM, VM, VM, ANY, VM, ANY, ANY],
        [ANY] * 5 + [VM] * 2,
        [
            pltpu.VMEM((rows, width), BF16),
            pltpu.VMEM((nz, own_rows, 3 * lw), BF16),
            pltpu.VMEM((nh, own_rows, total), BF16),
            pltpu.VMEM(w_in.shape, BF16),
            pltpu.VMEM(wd_t.shape, BF16),
            LineGather.sem_shape(nz),
        ]
        + PlaneWeights.sem_shapes(nh, nz, qs)
        + [
            HeadGather.sem_shape(nh),
            dma((2, 2, nh)),
            dma((2,)),
        ],
        (lengths, x, w_qkv, gain_attn, w_in, gain_mlp, wd_t, g),
        vmem=60 << 20,
    )


class Place:
    def __init__(self, nh, nb, hl):
        h, b = me()
        self.nh, self.nb, self.h, self.b = nh, nb, h, b
        self.x, self.c = h // 2, h % 2
        self.nz = hl
        self.qs = nb // hl
        self.cb = self.qs // 2
        self.sib = self.x * 2 + 1 - self.c
        self.zi, self.s = b // self.qs, b % self.qs
        self.head = self.x * 2 + self.s // self.cb
        self.u = self.s % self.cb
        self.from_s = self.u * 2 + self.c

    def attends(self, zi, l, core, u):
        return (l // 2) * 2 + core, zi * self.qs + (l % 2) * self.cb + u


def routed(pc, src, dst, send, recv, th, tb, act):
    mine = jnp.logical_and(th == pc.h, tb == pc.b)

    @pl.when(mine)
    def _():
        if act == "start":
            pltpu.make_async_copy(src, dst, recv).start()

    @pl.when(jnp.logical_not(mine))
    def _():
        cp = remote(src, dst, send, recv, th, tb)
        if act == "start":
            cp.start()
        else:
            cp.wait_send()


def wait_on(ref, sem):
    pltpu.make_async_copy(ref, ref, sem).wait()


def stretch_lanes(ref, zi, rows):
    return ref.at[:, :, pl.ds(pl.multiple_of(zi * rows, rows), rows)]


def outputs_back(pc, o_ref, og, osem, act):
    rows = og.shape[3]
    for zi in range(pc.nz):
        routed(
            pc,
            stretch_lanes(o_ref, zi, rows),
            og.at[pc.zi],
            osem.at[0, zi],
            osem.at[1, pc.zi],
            pc.head,
            zi * pc.qs + pc.from_s,
            act,
        )


def grads_out(pc, dots, do_in, qsem, act):
    rows = dots.shape[3]
    for zi in range(pc.nz):
        th, tb = pc.attends(zi, pc.h, pc.s % 2, pc.s // 2)
        routed(
            pc,
            dots.at[zi],
            stretch_lanes(do_in, pc.zi, rows),
            qsem.at[0, zi],
            qsem.at[1, pc.zi],
            th,
            tb,
            act,
        )


def halves_swapped(tile):
    lane = lanes_of(tile)
    return jnp.where(lane % DH < DH // 2, lane_roll(tile, -(DH // 2)), lane_roll(tile, DH // 2))


def turned(tile, cos, sin):
    return tile * cos + halves_swapped(tile) * sin


def to_heads_body(nh, nb, hl, n1_hbm, w_hbm, cos_ref, sin_ref, wo_ref, qin, kvin, wo_all, qbuf, kvbuf, n1_ref, w_ref, qsem, ksem, fsem, osem, osem2, stage):
    pc = Place(nh, nb, hl)
    loads = [
        pltpu.make_async_copy(n1_hbm, n1_ref, stage.at[0]),
        pltpu.make_async_copy(w_hbm, w_ref, stage.at[1]),
    ]
    for cp in loads:
        cp.start()
    signal_all(nh, nb, pc.h, pc.b)
    rows = kvbuf.shape[2]
    lw = nh * DH
    for cp in loads:
        cp.wait()
    n1 = n1_ref[...]
    cos, sin = cos_ref[...], sin_ref[...]
    kk = jnp.dot(n1, w_ref[:, lw : 2 * lw], preferred_element_type=F32)
    vv = jnp.dot(n1, w_ref[:, 2 * lw :], preferred_element_type=F32)
    for p in range(nh // 2):
        k = turned(kk[:, p * 128 : (p + 1) * 128], cos, sin)
        v = vv[:, p * 128 : (p + 1) * 128]
        low = lanes_of(k) < DH
        even = jnp.where(low, k, lane_roll(v, DH)).astype(BF16)
        odd = jnp.where(low, lane_roll(k, DH), v).astype(BF16)
        for i in range(pc.nz):
            kvbuf[2 * p, i] = even[i * rows : (i + 1) * rows]
            kvbuf[2 * p + 1, i] = odd[i * rows : (i + 1) * rows]
    wait_all(nh, nb)

    def keys_out(act):
        for l in range(nh):
            for u in range(pc.cb):
                th, tb = pc.attends(pc.zi, l, pc.s % 2, u)
                routed(
                    pc,
                    kvbuf.at[l],
                    kvin.at[pc.h, :, pc.s],
                    ksem.at[0, l * pc.cb + u],
                    ksem.at[1, pc.h * pc.cb + pc.s // 2],
                    th,
                    tb,
                    act,
                )

    def queries_out(act):
        for l in range(nh):
            th, tb = pc.attends(pc.zi, l, pc.s % 2, pc.s // 2)
            routed(
                pc, qbuf.at[l], qin.at[pc.h], qsem.at[0, l], qsem.at[1, pc.h], th, tb, act
            )

    spread = BlkGather(pc, wo_ref, wo_all, osem, osem2)
    keys_out("start")
    spread.start()
    qq = jnp.dot(n1, w_ref[:, :lw], preferred_element_type=F32)
    for p in range(nh // 2):
        q = turned(qq[:, p * 128 : (p + 1) * 128], cos, sin).T.astype(BF16)
        qbuf[2 * p] = q[:DH]
        qbuf[2 * p + 1] = q[DH:]
    queries_out("start")
    count = nh * pc.cb

    def forward(i):
        at = kvin.at[i // pc.cb, :, 2 * (i % pc.cb) + pc.c]
        return remote(at, at, fsem.at[0, i], fsem.at[1, i], pc.sib, pc.b)

    @pl.loop(0, count)
    def _(i):
        wait_on(kvin.at[i // pc.cb, :, 2 * (i % pc.cb) + pc.c], ksem.at[1, i])
        forward(i).start()

    for t in range(1, pc.nz):
        spread.step(t)
    keys_out("wait_send")
    queries_out("wait_send")
    for i in range(nh):
        wait_on(qin.at[i], qsem.at[1, i])

    @pl.loop(0, count)
    def _(i):
        forward(i).wait()

    spread.finish()


def to_heads(n1, wq, cos, sin, wo, hl):
    nh, nb = dims()
    group, width = n1.shape
    nz, qs = hl, nb // hl
    cb = qs // 2
    rows = group // nz
    dma = pltpu.SemaphoreType.DMA
    return comm_call(
        functools.partial(to_heads_body, nh, nb, hl),
        "to_heads",
        1,
        (
            jax.ShapeDtypeStruct((nh, DH, group), BF16),
            jax.ShapeDtypeStruct((nh, nz, qs, rows, 2 * DH), BF16),
            jax.ShapeDtypeStruct((1, nz, qs) + wo.shape[1:], BF16),
        ),
        [ANY, ANY, VM, VM, ANY],
        [ANY, ANY, ANY],
        [
            pltpu.VMEM((nh, DH, group), BF16),
            pltpu.VMEM((nh, nz, rows, 2 * DH), BF16),
            pltpu.VMEM(n1.shape, BF16),
            pltpu.VMEM(wq.shape, BF16),
            dma((2, nh)),
            dma((2, nh * cb)),
            dma((2, nh * cb)),
        ]
        + BlkGather.sem_shapes(nz, qs)
        + [dma((2,))],
        (n1, wq, cos, sin, wo),
        vmem=60 << 20,
    )


class Queries:
    def __init__(self, nh, nb, hl, len_ref, lanes, slots):
        pc = Place(nh, nb, hl)
        tile = pl.program_id(0)
        rows = lanes // 2
        each = pc.nz // 2
        ends = sequence_ends(len_ref)
        base = (tile // each) * nb + (tile % each) * 2 * pc.qs + pc.from_s
        lane = lax.broadcasted_iota(jnp.int32, (1, lanes), 1)
        slot = (base + jnp.where(lane < rows, 0, pc.qs)) * rows + lane % rows
        self.first = segment_first(slot, ends)
        self.last = segment_end(slot, ends, slots)
        self.lo = segment_first(base * rows, ends) // KEY_BLOCK
        far = (base + pc.qs) * rows + rows - 1
        self.hi = (segment_end(far, ends, slots) + KEY_BLOCK - 1) // KEY_BLOCK
        self.lanes = lanes

    def allowed(self, block_at):
        at = block_at * KEY_BLOCK + lax.broadcasted_iota(jnp.int32, (KEY_BLOCK, self.lanes), 0)
        return jnp.logical_and(at >= self.first, at < self.last)


def attend_body(nh, nb, hl, len_ref, q_ref, kv_ref, o_ref, of_ref, lse_ref):
    q = q_ref[0]
    lanes = q.shape[1]
    at = Queries(nh, nb, hl, len_ref, lanes, kv_ref.shape[0])
    q_pad = jnp.concatenate([q, jnp.zeros_like(q)], axis=0)

    def step(j, carry):
        top, total, acc = carry
        kv = kv_ref[pl.ds(pl.multiple_of(j * KEY_BLOCK, KEY_BLOCK), KEY_BLOCK), :]
        s = jnp.dot(kv, q_pad, preferred_element_type=F32)
        s = jnp.where(at.allowed(j), s, MASK_FLOOR)
        new_top = jnp.maximum(top, jnp.max(s, axis=0, keepdims=True))
        p = jnp.exp2((s - new_top) * EXP_SCALE)
        alpha = jnp.exp2((top - new_top) * EXP_SCALE)
        total = total * alpha + jnp.sum(p, axis=0, keepdims=True)
        acc = acc * alpha + lax.dot_general(
            kv, p.astype(BF16), (((0,), (0,)), ((), ())), preferred_element_type=F32
        )
        return new_top, total, acc

    top, total, acc = lax.fori_loop(
        at.lo,
        at.hi,
        step,
        (
            jnp.full((1, lanes), MASK_FLOOR, F32),
            jnp.zeros((1, lanes), F32),
            jnp.zeros((2 * DH, lanes), F32),
        ),
    )
    o = acc[DH:] / total
    of_ref[0] = o
    o_ref[0] = o.astype(BF16)
    lse_ref[0] = top * EXP_SCALE + jnp.log2(total)


def attend_specs(kv_rows, lanes, tiles_each):
    tile_spec = pl.BlockSpec((1, DH, lanes), lambda i, *_: (i // tiles_each, 0, i % tiles_each))
    row_spec = pl.BlockSpec((1, 1, lanes), lambda i, *_: (i, 0, 0))
    kv_spec = pl.BlockSpec((kv_rows, 2 * DH), lambda i, *_: (0, 0))
    return tile_spec, row_spec, kv_spec


def attend(lengths, q, kv, lanes, hl):
    nh, nb = dims()
    each = q.shape[2] // lanes
    tiles = q.shape[0] * each
    tile_spec, row_spec, kv_spec = attend_specs(kv.shape[0], lanes, each)
    return pl.pallas_call(
        functools.partial(attend_body, nh, nb, hl),
        grid_spec=pltpu.PrefetchScalarGridSpec(
            num_scalar_prefetch=1,
            grid=(tiles,),
            in_specs=[tile_spec, kv_spec],
            out_specs=[tile_spec, tile_spec, row_spec],
        ),
        out_shape=(
            jax.ShapeDtypeStruct(q.shape, BF16),
            jax.ShapeDtypeStruct(q.shape, F32),
            jax.ShapeDtypeStruct((tiles, 1, lanes), F32),
        ),
        name="attend",
        compiler_params=pltpu.CompilerParams(vmem_limit_bytes=60 << 20),
    )(lengths, q, kv)


def attend_grad_body(nh, nb, hl, len_ref, q_ref, do_ref, of_ref, kv_ref, lse_ref, dq_ref, dkv_ref, acc_ref):
    tile = pl.program_id(0)

    @pl.when(tile == 0)
    def _():
        acc_ref[...] = jnp.zeros_like(acc_ref)

    q = q_ref[0]
    do = do_ref[0]
    lanes = q.shape[1]
    place = Queries(nh, nb, hl, len_ref, lanes, kv_ref.shape[0])
    zero = jnp.zeros_like(q)
    both = jnp.concatenate(
        [jnp.concatenate([q, zero], axis=0), jnp.concatenate([zero, do], axis=0)], axis=1
    )
    delta = jnp.sum(do.astype(F32) * of_ref[0], axis=0, keepdims=True)
    lse = lse_ref[0]

    def step(j, dq):
        at = pl.ds(pl.multiple_of(j * KEY_BLOCK, KEY_BLOCK), KEY_BLOCK)
        kv = kv_ref[at, :]
        sd = jnp.dot(kv, both, preferred_element_type=F32)
        s, dp = sd[:, :lanes], sd[:, lanes:]
        p = jnp.exp2(
            jnp.where(place.allowed(j), s * EXP_SCALE - lse, MASK_FLOOR)
        )
        ds = (p * (dp - delta)).astype(BF16)
        acc_ref[at, :] += lax.dot_general(
            jnp.concatenate([ds, p.astype(BF16)], axis=1),
            both,
            (((1,), (1,)), ((), ())),
            preferred_element_type=F32,
        )
        return dq + lax.dot_general(
            kv, ds, (((0,), (0,)), ((), ())), preferred_element_type=F32
        )

    dq = lax.fori_loop(place.lo, place.hi, step, jnp.zeros((2 * DH, lanes), F32))
    dq_ref[0] = (dq[:DH] * 0.125).astype(BF16)

    @pl.when(tile == pl.num_programs(0) - 1)
    def _():
        lane = lax.broadcasted_iota(jnp.int32, (1, 2 * DH), 1)
        dkv_ref[...] = (acc_ref[...] * jnp.where(lane < DH, 0.125, 1.0)).astype(BF16)


def attend_grad(lengths, q, do, of, kv, lse, hl):
    nh, nb = dims()
    tiles, _, lanes = lse.shape
    tile_spec, row_spec, kv_spec = attend_specs(kv.shape[0], lanes, tiles // q.shape[0])
    return pl.pallas_call(
        functools.partial(attend_grad_body, nh, nb, hl),
        grid_spec=pltpu.PrefetchScalarGridSpec(
            num_scalar_prefetch=1,
            grid=(tiles,),
            in_specs=[tile_spec, tile_spec, tile_spec, kv_spec, row_spec],
            out_specs=[tile_spec, kv_spec],
            scratch_shapes=[pltpu.VMEM(kv.shape, F32)],
        ),
        out_shape=(jax.ShapeDtypeStruct(q.shape, BF16), jax.ShapeDtypeStruct(kv.shape, BF16)),
        name="attend_grad",
        compiler_params=pltpu.CompilerParams(vmem_limit_bytes=60 << 20),
    )(lengths, q, do, of, kv, lse)


class HeadSum:
    def __init__(self, nh, h, b, part, near, far, out, sems):
        self.nx = nh // 2
        self.x, self.c = h // 2, h % 2
        self.h, self.part, self.near, self.far, self.out = h, part, near, far, out
        sib = self.x * 2 + 1 - self.c
        self.pairs = [
            remote(
                part.at[((self.x + k) % self.nx) * 2 + 1 - self.c],
                near.at[k],
                sems.at[0, k],
                sems.at[1, k],
                sib,
                b,
            )
            for k in range(self.nx)
        ]
        self.across = [
            remote(
                out.at[k],
                far.at[k],
                sems.at[2, k],
                sems.at[3, k],
                ((self.x + k) % self.nx) * 2 + self.c,
                b,
            )
            for k in range(1, self.nx)
        ]

    @staticmethod
    def sem_shape(nh):
        return pltpu.SemaphoreType.DMA((4, nh // 2))

    @staticmethod
    def buffers(nh, rows, width):
        return [pltpu.VMEM((nh // 2, rows, width), BF16)] * 3

    def start(self):
        for k in list(range(1, self.nx)) + [0]:
            self.pairs[k].start()

    def send(self):
        for k in range(1, self.nx):
            self.pairs[k].wait_recv()
            at = ((self.x + k) % self.nx) * 2 + self.c
            self.out[k] = (self.part[at].astype(F32) + self.near[k].astype(F32)).astype(BF16)
            self.across[k - 1].start()

    def total(self):
        self.pairs[0].wait_recv()
        total = self.part[self.h].astype(F32) + self.near[0].astype(F32)
        for k in range(1, self.nx):
            self.across[k - 1].wait_recv()
            total = total + self.far[k].astype(F32)
        return total

    def finish(self):
        for cp in self.pairs:
            cp.wait_send()
        for cp in self.across:
            cp.wait_send()


def norm_of(values):
    centre = values - jnp.mean(values, axis=-1, keepdims=True)
    scale = lax.rsqrt(jnp.mean(centre * centre, axis=-1, keepdims=True) + NORM_EPS)
    return centre * scale, scale


def norm_pull(grad, normed, scale):
    one = jnp.mean(grad, axis=-1, keepdims=True)
    two = jnp.mean(grad * normed, axis=-1, keepdims=True)
    return scale * (grad - one - normed * two)


CHUNKS = 2


def chunk_of(ref, j, axis):
    size = ref.shape[axis] // CHUNKS
    at = pl.ds(j * size, size)
    return ref.at[at] if axis == 0 else ref.at[:, at]


def head_sums(nh, h, b, part, bufs, sems):
    near, far, out = bufs
    return [
        HeadSum(
            nh,
            h,
            b,
            chunk_of(part, j, 1),
            chunk_of(near, j, 1),
            chunk_of(far, j, 1),
            chunk_of(out, j, 1),
            sems.at[j],
        )
        for j in range(CHUNKS)
    ]


def head_gathers(nh, h, b, src, dst, sems):
    return [
        HeadGather(nh, h, b, chunk_of(src, j, 0), chunk_of(dst, j, 1), sems.at[j])
        for j in range(CHUNKS)
    ]


def chunk_sems(nh):
    return pltpu.SemaphoreType.DMA((CHUNKS, 4, nh // 2))


def mid_body(nh, nb, hl, o_ref, wo_ref, x_ref, wmb_ref, og, hid_ref, ng_ref, wmb_all, part, near, far, out, nbuf, osem, ssem, gsem, wsem, wsem2):
    pc = Place(nh, nb, hl)
    h, b = pc.h, pc.b
    signal_all(nh, nb, h, b)
    wait_all(nh, nb)
    rows, width = x_ref.shape
    outputs_back(pc, o_ref, og, osem, "start")
    spread = BlkGather(pc, wmb_ref, wmb_all, wsem, wsem2)
    spread.start()
    outputs_back(pc, o_ref, og, osem, "wait_send")
    for zi in range(pc.nz):
        wait_on(og.at[zi], osem.at[1, zi])
    wo = wo_ref[...]
    for i in range(nh):
        part[i] = lax.dot_general(
            og[:, i].reshape(pc.nz * DH, rows),
            wo,
            (((0,), (0,)), ((), ())),
            preferred_element_type=F32,
        ).astype(BF16)
    hss = head_sums(nh, h, b, part, (near, far, out), ssem)
    hgs = head_gathers(nh, h, b, nbuf, ng_ref, gsem)
    for hs in hss:
        hs.start()
    spread.step(1)
    for hs in hss:
        hs.send()
    size = rows // CHUNKS
    for j, (hs, hg) in enumerate(zip(hss, hgs)):
        at = pl.ds(j * size, size)
        hid = x_ref[at, :].astype(F32) + hs.total()
        hid_ref[at, :] = hid
        nbuf[at, :] = norm_of(hid)[0].astype(BF16)
        hg.start()
    spread.step(2)
    for hg in hgs:
        hg.pass_on()
    for t in range(3, pc.nz):
        spread.step(t)
    for hs, hg in zip(hss, hgs):
        hs.finish()
        hg.finish()
    spread.finish()


def mid_exchange(ot, wo, x, wmb, hl):
    nh, nb = dims()
    rows, width = x.shape
    nz = hl
    return comm_call(
        functools.partial(mid_body, nh, nb, hl),
        "mid_exchange",
        2,
        (
            jax.ShapeDtypeStruct((nz, nh, DH, rows), BF16),
            jax.ShapeDtypeStruct(x.shape, F32),
            jax.ShapeDtypeStruct((nh, rows, width), BF16),
            jax.ShapeDtypeStruct((nh, nz, nb // nz) + wmb.shape[1:], BF16),
        ),
        [ANY, VM, VM, ANY],
        [VM, VM, VM, ANY],
        [pltpu.VMEM((nh, rows, width), BF16)]
        + HeadSum.buffers(nh, rows, width)
        + [
            pltpu.VMEM((rows, width), BF16),
            pltpu.SemaphoreType.DMA((2, nz)),
            chunk_sems(nh),
            chunk_sems(nh),
        ]
        + BlkGather.sem_shapes(nz, nb // nz),
        (ot, wo, x, wmb),
        vmem=60 << 20,
    )


def ffn_body(nh, nb, fl, split_rows, cut, len_ref, n_hbm, g_hbm, wa_hbm, wb_hbm, y_hbm, d_hbm, ga_hbm, gb_hbm, n_ref, g_ref, w_ref, y_ref, d_ref, ga_ref, gb_ref, gy, mm, dz, stage, drain):
    rows, width = n_ref.shape[1], n_ref.shape[2]
    group = nh * rows
    total, zc, off = ff_widths(fl)
    wide = total - off
    shift = 2 * fl - off
    step = 2 * rows
    lane = lax.broadcasted_iota(jnp.int32, (1, wide), 1)
    real = lane < fl
    valid = sequence_ends(len_ref)[-1]
    blk = lax.axis_index("blk")
    loads = [
        pltpu.make_async_copy(n_hbm, n_ref, stage.at[0]),
        pltpu.make_async_copy(wa_hbm, w_ref.at[:, pl.ds(0, off)], stage.at[1]),
        pltpu.make_async_copy(wb_hbm, w_ref.at[:, pl.ds(off, wide)], stage.at[2]),
        pltpu.make_async_copy(g_hbm, g_ref, stage.at[3]),
    ]
    for cp in loads:
        cp.start()
    for cp in loads:
        cp.wait()

    def out_rows(r):
        at = pl.ds(r * 2, 2)
        return [
            pltpu.make_async_copy(d_ref.at[at], d_hbm.at[at], drain.at[0, r]),
            pltpu.make_async_copy(y_ref.at[at], y_hbm.at[at], drain.at[1, r]),
        ]

    @pl.loop(0, group // step)
    def _(r):
        at = pl.ds(pl.multiple_of(r * step, step), step)
        n = n_ref[pl.ds(r * 2, 2)].reshape(step, width)
        row = lax.broadcasted_iota(jnp.int32, (step, 1), 0)
        slot = ((r * 2 + row // rows) * nb + blk) * rows + row % rows
        g = g_ref[pl.ds(r * 2, 2)].reshape(step, width)
        g = jnp.where(slot < valid, g.astype(F32), 0.0).astype(BF16)
        gy[at, :] = g
        z = jnp.dot(n, w_ref[:, :zc], preferred_element_type=F32)
        dm = lane_roll(jnp.dot(g, w_ref[:, off:], preferred_element_type=F32), -shift)
        gate, up = z[:, :wide], lane_roll(z, -fl)[:, :wide]
        cdf = 0.5 * (1.0 + lax.erf(gate * math.sqrt(0.5)))
        act = gate * cdf
        slope = cdf + gate * jnp.exp(-0.5 * gate * gate) * (1.0 / math.sqrt(2.0 * math.pi))
        m = lane_roll(jnp.where(real, act * up, 0.0), shift).astype(BF16)
        mm[at, :] = m
        d_gate = widen(jnp.where(real, dm * up * slope, 0.0), zc)
        d_up = lane_roll(widen(jnp.where(real, dm * act, 0.0), zc), fl)
        d = (d_gate + d_up).astype(BF16)
        dz[at, :] = d
        nt = (((1,), (1,)), ((), ()))
        dpart = lax.dot_general(d, w_ref[:, :zc], nt, preferred_element_type=F32)
        d_ref[pl.ds(r * 2, 2)] = dpart.astype(BF16).reshape(2, rows, width)
        ypart = lax.dot_general(m, w_ref[:, off:], nt, preferred_element_type=F32)
        y_ref[pl.ds(r * 2, 2)] = ypart.astype(BF16).reshape(2, rows, width)
        for cp in out_rows(r):
            cp.start()

    block = width // nh

    def out_block(i):
        at = (slice(None), i) if split_rows else (pl.ds(i * block, block),)
        return [
            pltpu.make_async_copy(ga_ref.at[i], ga_hbm.at[at], drain.at[2, i]),
            pltpu.make_async_copy(gb_ref.at[i], gb_hbm.at[at], drain.at[3, i]),
        ]

    @pl.loop(0, nh)
    def _(i):
        cols = pl.ds(pl.multiple_of(i * block, block), block)
        tn = (((0,), (0,)), ((), ()))
        n = n_ref[:, :, cols].reshape(group, block)
        g_in = lax.dot_general(n, dz[...], tn, preferred_element_type=F32)
        g_down = lax.dot_general(gy[:, cols], mm[...], tn, preferred_element_type=F32)
        both = jnp.concatenate(
            [g_in[:, :off], g_in[:, off:] + g_down[:, : zc - off], g_down[:, zc - off :]], axis=1
        ).astype(BF16)
        for ref, part in ((ga_ref, both[:, :cut]), (gb_ref, both[:, cut:])):
            if split_rows:
                part = part.reshape(nb, block // nb, part.shape[1])
            ref[i] = part
        for cp in out_block(i):
            cp.start()

    @pl.loop(0, nh)
    def _(i):
        for cp in out_block(i):
            cp.wait()

    @pl.loop(0, group // step)
    def _(r):
        for cp in out_rows(r):
            cp.wait()


def ffn(lengths, n2, g, wma, wmb, fl, own_rows, cut):
    nh, nb = dims()
    _, rows, width = n2.shape
    group = nh * rows
    total, zc, off = ff_widths(fl)
    split_rows = own_rows % 16 == 0
    lead = (nb, nh, own_rows) if split_rows else (width,)
    held = (nh, nb, own_rows) if split_rows else (nh, width // nh)
    return pl.pallas_call(
        functools.partial(ffn_body, nh, nb, fl, split_rows, cut),
        out_shape=(
            jax.ShapeDtypeStruct(n2.shape, BF16),
            jax.ShapeDtypeStruct(n2.shape, BF16),
            jax.ShapeDtypeStruct(lead + (cut,), BF16),
            jax.ShapeDtypeStruct(lead + (total - cut,), BF16),
        ),
        in_specs=[SM, ANY, ANY, ANY, ANY],
        out_specs=[ANY] * 4,
        scratch_shapes=[
            pltpu.VMEM(n2.shape, BF16),
            pltpu.VMEM(n2.shape, BF16),
            pltpu.VMEM((width, total), BF16),
            pltpu.VMEM(n2.shape, BF16),
            pltpu.VMEM(n2.shape, BF16),
            pltpu.VMEM(held + (cut,), BF16),
            pltpu.VMEM(held + (total - cut,), BF16),
            pltpu.VMEM((group, width), BF16),
            pltpu.VMEM((group, total - off), BF16),
            pltpu.VMEM((group, zc), BF16),
            pltpu.SemaphoreType.DMA((4,)),
            pltpu.SemaphoreType.DMA((4, nh)),
        ],
        name="ffn",
        compiler_params=pltpu.CompilerParams(vmem_limit_bytes=60 << 20),
    )(lengths, n2, g, wma, wmb)


def back_body(nh, nb, hl, len_ref, dpart, ypart, hid_ref, g_ref, wo_ref, og_ref, gb_hbm, y_ref, dh_ref, do_in, go_ref, gb_out, n1, f1, o1, n2, f2, o2, dbuf, dg, dots, gb_ref, nearb, s1, s2, gsem, qsem, pb, stage):
    pc = Place(nh, nb, hl)
    h, b = pc.h, pc.b
    mine = pltpu.make_async_copy(gb_hbm.at[:, pc.s], gb_ref, stage)
    mine.start()
    signal_all(nh, nb, h, b)
    wait_all(nh, nb)
    pairs = [
        remote(
            gb_hbm.at[:, (pc.s + ds) % pc.qs],
            nearb.at[ds - 1],
            pb.at[0, ds],
            pb.at[1, ds],
            h,
            pc.zi * pc.qs + (pc.s + ds) % pc.qs,
        )
        for ds in range(1, pc.qs)
    ]
    rows, width = hid_ref.shape
    slot = (h * nb + b) * rows + lax.broadcasted_iota(jnp.int32, (rows, 1), 0)
    valid = slot < sequence_ends(len_ref)[-1]
    hds = head_sums(nh, h, b, dpart, (n1, f1, o1), s1)
    hy = HeadSum(nh, h, b, ypart, n2, f2, o2, s2)
    hgs = head_gathers(nh, h, b, dbuf, dg, gsem)
    for hd in hds:
        hd.start()
    for cp in pairs:
        cp.start()
    for hd in hds:
        hd.send()
    size = rows // CHUNKS
    for j, (hd, hg) in enumerate(zip(hds, hgs)):
        at = pl.ds(j * size, size)
        normed, scale = norm_of(hid_ref[at, :])
        gy = jnp.where(valid[j * size : (j + 1) * size], g_ref[at, :].astype(F32), 0.0)
        dh = gy + norm_pull(hd.total(), normed, scale)
        dh_ref[at, :] = dh
        dbuf[at, :] = dh.astype(BF16)
        hg.start()
    hy.start()
    for hg in hgs:
        hg.pass_on()
    hy.send()
    for hd, hg in zip(hds, hgs):
        hd.finish()
        hg.finish()
    wo = wo_ref[...]
    nt = (((1,), (1,)), ((), ()))
    for i in range(nh):
        part = lax.dot_general(wo, dg[i], nt, preferred_element_type=F32).astype(BF16)
        dots[:, i] = part.reshape(pc.nz, DH, rows)
    grads_out(pc, dots, do_in, qsem, "start")
    total = 0.0
    for i in range(nh):
        total = total + jnp.dot(
            og_ref[:, i].reshape(pc.nz * DH, rows), dg[i], preferred_element_type=F32
        )
    go_ref[...] = total.astype(BF16)
    y_ref[...] = jnp.where(valid, hid_ref[...] + hy.total(), 0.0)
    hy.finish()
    mine.wait()
    for cp in pairs:
        cp.wait()

    @pl.loop(0, pc.nz)
    def _(d):
        others = jnp.sum(nearb[:, d].astype(F32), axis=0)
        gb_out[d] = (gb_ref[d].astype(F32) + others).astype(BF16)

    grads_out(pc, dots, do_in, qsem, "wait_send")
    for zi in range(pc.nz):
        wait_on(stretch_lanes(do_in, zi, rows), qsem.at[1, zi])


def back_exchange(lengths, dpart, ypart, hid, g, wo, og, gb):
    nh, nb = dims()
    rows, width = hid.shape
    nz = hl = og.shape[0]
    return comm_call(
        functools.partial(back_body, nh, nb, hl),
        "back_exchange",
        3,
        (
            jax.ShapeDtypeStruct(hid.shape, F32),
            jax.ShapeDtypeStruct(hid.shape, F32),
            jax.ShapeDtypeStruct((nh, DH, nz * rows), BF16),
            jax.ShapeDtypeStruct((nz * DH, width), BF16),
            jax.ShapeDtypeStruct(gb.shape[:1] + gb.shape[2:], BF16),
        ),
        [SM] + [VM] * 6 + [ANY],
        [VM, VM, ANY, VM, VM],
        HeadSum.buffers(nh, rows, width)
        + HeadSum.buffers(nh, rows, width)
        + [
            pltpu.VMEM((rows, width), BF16),
            pltpu.VMEM((nh, rows, width), BF16),
            pltpu.VMEM(og.shape, BF16),
            pltpu.VMEM(gb.shape[:1] + gb.shape[2:], BF16),
            pltpu.VMEM((gb.shape[1] - 1, nz) + gb.shape[2:], BF16),
            chunk_sems(nh),
            HeadSum.sem_shape(nh),
            chunk_sems(nh),
            pltpu.SemaphoreType.DMA((2, nz)),
            pltpu.SemaphoreType.DMA((2, gb.shape[1])),
            pltpu.SemaphoreType.DMA,
        ],
        (lengths, dpart, ypart, hid, g, wo, og, gb),
        vmem=60 << 20,
    )


def grads_back_body(nh, nb, hl, dq_ref, dkv_ref, cos_ref, sin_ref, n1_hbm, w_hbm, go_ref, gb_ref, gq_ref, dpart, do_ref, gb_sum, got, sums, dq_out, dkv_out, dqkv, n1_ref, w_ref, nearo, sumo, goto, lsem, gotb, bsem, qsem, psem, ksem, stage, po):
    pc = Place(nh, nb, hl)
    loads = [
        pltpu.make_async_copy(n1_hbm, n1_ref, stage.at[0]),
        pltpu.make_async_copy(w_hbm, w_ref, stage.at[1]),
    ]
    for cp in loads:
        cp.start()
    signal_all(nh, nb, pc.h, pc.b)
    wait_all(nh, nb)
    rows = dkv_ref.shape[3]
    group = pc.nz * rows
    width = n1_ref.shape[1]
    lw = nh * DH
    count = nh * pc.cb

    def pair(k):
        src = dkv_ref.at[k // pc.cb, :, 2 * (k % pc.cb) + 1 - pc.c]
        return remote(src, got.at[k], psem.at[0, k], psem.at[1, k], pc.sib, pc.b)

    def back(k, act):
        routed(
            pc,
            sums.at[k],
            dkv_out.at[pc.head, pc.u],
            ksem.at[0, k],
            ksem.at[1, pc.head * pc.cb + pc.u],
            k // pc.cb,
            pc.zi * pc.qs + 2 * (k % pc.cb) + pc.c,
            act,
        )

    def queries_back(act):
        for i in range(nh):
            routed(
                pc,
                dq_ref.at[i],
                dq_out.at[pc.head],
                qsem.at[0, i],
                qsem.at[1, pc.head],
                i,
                pc.zi * pc.qs + pc.from_s,
                act,
            )

    pairs_o = [
        remote(
            go_ref.at[:, (pc.s + ds) % pc.qs],
            nearo.at[ds - 1],
            po.at[0, ds],
            po.at[1, ds],
            pc.h,
            pc.zi * pc.qs + (pc.s + ds) % pc.qs,
        )
        for ds in range(1, pc.qs)
    ]
    along_o = StretchSum(pc, sumo, goto, lsem)
    along_b = StretchSum(pc, gb_ref, gotb, bsem)

    @pl.loop(0, count)
    def _(k):
        pair(k).start()

    queries_back("start")
    for cp in pairs_o:
        cp.start()
    along_b.start()

    @pl.loop(0, count)
    def _(k):
        pair(k).wait_recv()
        mine = dkv_ref[k // pc.cb, :, 2 * (k % pc.cb) + pc.c]
        sums[k] = (mine.astype(F32) + got[k].astype(F32)).astype(BF16)
        back(k, "start")

    for cp in pairs_o:
        cp.wait_recv()
    sumo[...] = (go_ref[:, pc.s].astype(F32) + jnp.sum(nearo[...].astype(F32), axis=0)).astype(BF16)
    along_o.start()
    cos, sin = cos_ref[...], -sin_ref[...]
    for l in range(nh):
        wait_on(dq_out.at[l], qsem.at[1, l])
    for p in range(nh // 2):
        q = dq_out[2 * p : 2 * p + 2].reshape(2 * DH, group).astype(F32).T
        dqkv[:, p * 128 : (p + 1) * 128] = turned(q, cos, sin).astype(BF16)
    for l in range(nh):
        for u in range(pc.cb):
            wait_on(dkv_out.at[l, u], ksem.at[1, l * pc.cb + u])
    for p in range(nh // 2):
        even, odd = [
            jnp.sum(dkv_out[2 * p + i].astype(F32), axis=0).reshape(group, 2 * DH)
            for i in range(2)
        ]
        low = lanes_of(even) < DH
        k = jnp.where(low, even, lane_roll(odd, DH)).astype(BF16).astype(F32)
        v = jnp.where(low, lane_roll(even, DH), odd)
        dqkv[:, lw + p * 128 : lw + (p + 1) * 128] = turned(k, cos, sin).astype(BF16)
        dqkv[:, 2 * lw + p * 128 : 2 * lw + (p + 1) * 128] = v.astype(BF16)
    nt = (((1,), (1,)), ((), ()))
    tn = (((0,), (0,)), ((), ()))
    for cp in loads:
        cp.wait()

    @pl.loop(0, nh)
    def _(i):
        cols = pl.ds(pl.multiple_of(i * (width // nh), width // nh), width // nh)
        gq_ref[cols, :] = lax.dot_general(
            n1_ref[:, cols], dqkv[...], tn, preferred_element_type=F32
        ).astype(BF16)

    @pl.loop(0, pc.nz)
    def _(i):
        at = pl.ds(pl.multiple_of(i * rows, rows), rows)
        dpart[i] = lax.dot_general(
            dqkv[at, :], w_ref[...], nt, preferred_element_type=F32
        ).astype(BF16)

    @pl.loop(0, count)
    def _(k):
        pair(k).wait_send()
        back(k, "wait_send")

    queries_back("wait_send")
    do_ref[...] = along_o.total()
    gb_sum[...] = along_b.total().astype(BF16)
    along_o.finish()
    along_b.finish()
    for cp in pairs_o:
        cp.wait_send()


def grads_back(dq, dkv, cos, sin, n1, wq, go, gb, hl):
    nh, nb = dims()
    nz, qs = hl, nb // hl
    cb = qs // 2
    rows = dkv.shape[3]
    width = n1.shape[1]
    lw = nh * DH
    dma = pltpu.SemaphoreType.DMA
    return comm_call(
        functools.partial(grads_back_body, nh, nb, hl),
        "grads_back",
        4,
        (
            jax.ShapeDtypeStruct((width, 3 * lw), BF16),
            jax.ShapeDtypeStruct((nz, rows, width), BF16),
            jax.ShapeDtypeStruct(go.shape[2:], F32),
            jax.ShapeDtypeStruct(gb.shape[1:], BF16),
        ),
        [ANY, VM, VM, VM, ANY, ANY, VM, VM],
        [VM] * 4,
        [
            pltpu.VMEM((nh * cb, nz, rows, 2 * DH), BF16),
            pltpu.VMEM((nh * cb, nz, rows, 2 * DH), BF16),
            pltpu.VMEM(dq.shape, BF16),
            pltpu.VMEM((nh, cb, nz, rows, 2 * DH), BF16),
            pltpu.VMEM((nz * rows, 3 * lw), BF16),
            pltpu.VMEM(n1.shape, BF16),
            pltpu.VMEM(wq.shape, BF16),
            pltpu.VMEM((qs - 1, nz) + go.shape[2:], BF16),
            pltpu.VMEM((nz,) + go.shape[2:], BF16),
        ]
        + StretchSum.scratch(nz, go.shape[2:])
        + StretchSum.scratch(nz, gb.shape[1:])
        + [
            dma((2, nh)),
            dma((2, nh * cb)),
            dma((2, nh * cb)),
            dma((2,)),
            dma((2, qs)),
        ],
        (dq, dkv, cos, sin, n1, wq, go, gb),
        vmem=60 << 20,
    )


def last_body(nh, nb, hl, dpart, gq_ref, gma_ref, gmb_ref, dn_ref, quarters, gma_all, gmb_all, nearq, sumq, farq, totq, sentz, gotz, zsem, pq, fq, cq, msem):
    pc = Place(nh, nb, hl)
    h, b = pc.h, pc.b
    signal_all(nh, nb, h, b)
    wait_all(nh, nb)
    nx, nz, qs = nh // 2, pc.nz, pc.qs
    def pair_q(k):
        return remote(
            gq_ref.at[2 * k + 1 - pc.c], nearq.at[k], pq.at[0, k], pq.at[1, k], pc.sib, b
        )

    line = LineSum(pc, lambda d: dpart[d].astype(F32), sentz, gotz, zsem)

    def plane_q(i):
        tx, ts = (pc.x + i // qs) % nx, (pc.s + i % qs) % qs
        return remote(
            sumq.at[tx, :, ts],
            farq.at[pc.x, pc.s],
            fq.at[0, i],
            fq.at[1, i],
            tx * 2 + pc.c,
            pc.zi * qs + ts,
        )

    def quarter(i):
        to = (pc.zi + i) % nz
        return remote(
            totq.at[to], quarters.at[pc.zi], cq.at[0, i], cq.at[1, i], h, to * qs + pc.s
        )

    for k in range(nx):
        pair_q(k).start()
    line.lead(0)
    moves = []
    for n, (ref, dst) in enumerate(((gma_ref, gma_all), (gmb_ref, gmb_all))):
        for i in range(1, nh):
            th = (h + i) % nh
            moves.append(remote(ref.at[th], dst.at[h], msem.at[0, n, i], msem.at[1, n, i], th, b))
        moves.append(pltpu.make_async_copy(ref.at[h], dst.at[h], msem.at[0, n, 0]))
    for k in range(nx):
        pair_q(k).wait_recv()
        sumq[k] = (gq_ref[2 * k + pc.c].astype(F32) + nearq[k].astype(F32)).astype(BF16)

    @pl.loop(1, nx * qs)
    def _(i):
        plane_q(i).start()

    farq[pc.x, pc.s] = sumq[pc.x, :, pc.s]
    for cp in moves:
        cp.start()
    line.follow(0)
    line.lead(1)

    @pl.loop(1, nx * qs)
    def _(i):
        plane_q(i).wait_recv()

    totq[...] = jnp.sum(
        farq[...].astype(F32).reshape((nx * qs,) + totq.shape), axis=0
    ).astype(BF16)
    for i in range(1, nz):
        quarter(i).start()
    quarters[pc.zi] = totq[pc.zi]
    for j in range(1, nz - 1):
        line.follow(j)
        if j + 1 < nz - 1:
            line.lead(j + 1)
    line.total(dn_ref)
    line.finish()
    for i in range(1, nz):
        quarter(i).wait()
    for cp in moves:
        cp.wait()
    for k in range(nx):
        pair_q(k).wait_send()

    @pl.loop(1, nx * qs)
    def _(i):
        plane_q(i).wait_send()


def last_exchange(dpart, gq, gma, gmb):
    nh, nb = dims()
    nz, rows, width = dpart.shape
    qs = nb // nz
    own_rows, cols = gq.shape[3:]
    nx = nh // 2
    dma = pltpu.SemaphoreType.DMA
    return comm_call(
        functools.partial(last_body, nh, nb, nz),
        "last_exchange",
        5,
        (
            jax.ShapeDtypeStruct((rows, width), F32),
            jax.ShapeDtypeStruct((nz, own_rows, cols), BF16),
            jax.ShapeDtypeStruct(gma.shape, BF16),
            jax.ShapeDtypeStruct(gmb.shape, BF16),
        ),
        [VM] * 2 + [ANY] * 2,
        [VM] * 2 + [ANY] * 2,
        [
            pltpu.VMEM((nx, nz, qs, own_rows, cols), BF16),
            pltpu.VMEM((nx, nz, qs, own_rows, cols), BF16),
            pltpu.VMEM((nx, qs, nz, own_rows, cols), BF16),
            pltpu.VMEM((nz, own_rows, cols), BF16),
        ]
        + LineSum.scratch(nz, (rows, width))
        + [
            dma((2, nx)),
            dma((2, nx * qs)),
            dma((2, nz)),
            dma((2, 2, nh)),
        ],
        (dpart, gq, gma, gmb),
        vmem=60 << 20,
    )


def finish_body(nh, fl, dn_ref, x_ref, dh_ref, y_in, quarters, do_in, gma, gmb, wq_ref, win_ref, ga_ref, gf_ref,
                y_ref, dx_ref, lna_ref, dq_ref, do_ref, lnm_ref, din_ref, dwd_ref):
    y_ref[...] = y_in[...]
    do_ref[...] = do_in[...]
    normed, scale = norm_of(x_ref[...].astype(F32))
    dx_ref[...] = dh_ref[...] + norm_pull(dn_ref[...], normed, scale)
    width = x_ref.shape[1]
    gain = column(ga_ref[...].astype(F32))
    nz = quarters.shape[0]
    rowsum = 0.0
    for c in range(3):
        for l in range(nh):
            src = (c * nh * DH + l // 2 * 128) // 128 * 128
            for p in range(nz // 2):
                tiles = [quarters[2 * p + i, :, src : src + 128].astype(F32) for i in range(2)]
                piece = half_pick(tiles[0], tiles[1], l % 2, l % 2)
                at = c * width + l * nz * DH + p * 128
                dq_ref[:, at : at + 128] = piece * gain
                rowsum = rowsum + jnp.sum(
                    piece * wq_ref[:, at : at + 128].astype(F32), axis=1, keepdims=True
                )
    lna_ref[...] = as_row(rowsum)
    ff = nh * fl
    total, _, _ = ff_widths(fl)
    tiles = lambda v: (v + 127) // 128 * 128
    gate_up, down = 0.0, 0.0
    for i in range(nh):
        piece = jnp.concatenate([gma[i].astype(F32), gmb[i].astype(F32)], axis=1)
        lane = lanes_of(piece)
        gate = widen(jnp.where(lane < fl, piece, 0.0), tiles(2 * ff))
        up = jnp.where(jnp.logical_and(lane >= fl, lane < 2 * fl), piece, 0.0)
        up = widen(up, tiles(2 * ff))
        gate_up = gate_up + lane_roll(gate, i * fl) + lane_roll(up, ff - fl + i * fl)
        dn = jnp.where(jnp.logical_and(lane >= 2 * fl, lane < 3 * fl), piece, 0.0)
        down = down + lane_roll(widen(dn, max(total, tiles(ff))), i * fl - 2 * fl)
    gate_up = gate_up[:, : 2 * ff]
    dwd_ref[...] = down[:, :ff]
    din_ref[...] = gate_up * column(gf_ref[...].astype(F32))
    lnm_ref[...] = as_row(jnp.sum(gate_up * win_ref[...].astype(F32), axis=1, keepdims=True))


def finish(dn, x, dh, y, quarters, d_wout, gma, gmb, w_qkv, w_in, gain_attn, gain_mlp, fl):
    nh, _ = dims()
    rows, width = x.shape
    own_rows = w_qkv.shape[0]
    ff = nh * fl
    f32 = lambda *shape: jax.ShapeDtypeStruct(shape, F32)
    return pl.pallas_call(
        functools.partial(finish_body, nh, fl),
        out_shape=(
            f32(rows, width),
            f32(rows, width),
            f32(1, own_rows),
            f32(own_rows, 3 * width),
            f32(own_rows, width),
            f32(1, own_rows),
            f32(own_rows, 2 * ff),
            f32(own_rows, ff),
        ),
        in_specs=[VM] * 12,
        out_specs=[VM] * 8,
        name="finish",
        compiler_params=pltpu.CompilerParams(vmem_limit_bytes=60 << 20),
    )(dn, x, dh, y, quarters, d_wout, gma, gmb, w_qkv, w_in, gain_attn, gain_mlp)


def shards(layer_input, out_grad, lengths, ln_attn, w_qkv, w_attn_out, ln_mlp, w_in, w_mlp_out):
    nh, nb = dims()
    h, b = me()
    rows, width = layer_input.shape
    heads = width // DH
    hl = heads // nh
    group = nh * rows
    slots = nh * nb * rows
    own_rows = w_qkv.shape[0]
    ff = w_mlp_out.shape[0]
    fl = ff // nh
    nz, qs = hl, nb // hl
    lw = nh * DH

    gain_attn = ln_attn.reshape(1, own_rows)
    gain_mlp = ln_mlp.reshape(1, own_rows)
    n1, wma, wmb, wq, gg, cos, sin = first_exchange(
        lengths, layer_input, w_qkv, gain_attn, w_in, gain_mlp, w_mlp_out.T, out_grad, hl, fl
    )
    wma = lax.all_gather(wma, "blk", axis=1, tiled=True).reshape(width, -1)
    wq = wq.reshape(width, 3 * lw)
    n1 = n1.reshape(group, width)
    qin, kvin, wo = to_heads(n1, wq, cos, sin, w_attn_out[None], hl)
    wo = wo.reshape(nz * DH, width)
    kv_all = kvin.reshape(slots, 2 * DH)
    ot, of, lse = attend(lengths, qin, kv_all, 2 * rows, hl)
    og, hid, n2, wmb = mid_exchange(ot, wo, layer_input, wmb, hl)
    wmb = wmb.reshape(width, -1)
    ypart, dpart, gma, gmb = ffn(lengths, n2, gg, wma, wmb, fl, own_rows, GRAD_CUT)
    if gma.ndim == 4:
        gma = lax.psum_scatter(gma, "blk", scatter_dimension=0, tiled=True)
        gmb = gmb.reshape((nz, qs) + gmb.shape[1:])
    else:
        gma = gma.reshape(nh, nb * own_rows, gma.shape[1])
        gma = lax.psum_scatter(gma, "blk", scatter_dimension=1, tiled=True)
        gmb = gmb.reshape(nh, nz, qs, own_rows, gmb.shape[1]).transpose(1, 2, 0, 3, 4)
    gma = gma.reshape(nh, own_rows, gma.shape[-1])
    y_out, dh, do_in, go, gmb = back_exchange(
        lengths, dpart, ypart, hid, out_grad, wo, og, gmb
    )
    dq, dkv = attend_grad(lengths, qin, do_in, of, kv_all, lse, hl)
    go = go.reshape(nz, qs, own_rows, width)
    gq, dpart1, d_wout, gmb = grads_back(
        dq, dkv.reshape(kvin.shape), cos, sin, n1, wq, go, gmb, hl
    )
    dn, quarters, gma, gmb = last_exchange(
        dpart1, gq.reshape(nh, nz, qs, own_rows, 3 * lw), gma, gmb
    )
    y_out, dx, d_ln_attn, d_wqkv, d_wout, d_ln_mlp, d_win, d_wd = finish(
        dn,
        layer_input,
        dh,
        y_out,
        quarters,
        d_wout,
        gma,
        gmb,
        w_qkv,
        w_in,
        gain_attn,
        gain_mlp,
        fl,
    )
    return (
        y_out,
        dx,
        d_ln_attn.reshape(own_rows),
        d_wqkv,
        d_wout,
        d_ln_mlp.reshape(own_rows),
        d_win,
        d_wd.T,
    )


def solution(mesh):
    both = ("head", "blk")
    row_split = P(both, None)
    return jax.shard_map(
        shards,
        mesh=mesh,
        in_specs=(
            row_split,
            row_split,
            P(),
            P(both),
            row_split,
            row_split,
            P(both),
            row_split,
            P(None, both),
        ),
        out_specs=(
            row_split,
            row_split,
            P(both),
            row_split,
            row_split,
            P(both),
            row_split,
            P(None, both),
        ),
        check_vma=False,
    )
```

time: 337 us -> 289 us (0.86); the launches traced: 339 us -> 285 us
  Pallas kernels: 310 us -> 271 us
  other arithmetic: 11.2 us -> 0 us
    pallas_call x6, Pallas kernels: 255 us -> 218 us  [comm_call(): pl.pallas_call(body, out_shape=out_shape, in_specs=in_specs, out_specs=ou...]
    select_n x6 -> x0, other arithmetic: 3.71 us -> none  [the longest x1 1.29 us: shards(): valid = jnp.where(spans(own_at, lengths)[2], 0.0, 1.0)[:, None]]
  transfers between devices with their start and end apart: 2 -> 2, of which waited for: 0 -> 0; matrix products, arithmetic and copies ran while one was open for 3% -> 0% of each run, Pallas kernels for 63% -> 64%
where the time goes in v3:
time: 289 us; the launch traced here: 285 us
  Pallas kernels  271 us (94%)
  between operations  14.1 us (5%)
    pallas_call x6, Pallas kernels, comm_call(): pl.pallas_call(body, out_shape=out_shape, in_specs=in_specs, out_specs=ou...  218 us
    pallas_call x1, Pallas kernels, attend_grad(): pl.pallas_call(functools.partial(attend_grad_body, nh, nb, hl), grid_spec...  16.8 us
    pallas_call x1, Pallas kernels, attend(): pl.pallas_call(functools.partial(attend_body, nh, nb, hl), grid_spec=pltp...  15.9 us
    pallas_call x1, Pallas kernels, ffn(): pl.pallas_call(functools.partial(ffn_body, nh, nb, fl, split_rows, cut),...  14.6 us
    pallas_call x1, Pallas kernels, finish(): pl.pallas_call(functools.partial(finish_body, nh, fl), out_shape=(f32(row...  5.8 us
  transfers between devices with their start and end apart: 2, of which 0 were waited for; matrix products, arithmetic and copies ran while one was open for 0% of the time, Pallas kernels for 64%

profile of v3, /device:TPU:0, one launch (start us, length us, event | category | flops | bytes accessed | tf_op | source)
XLA Modules:
  0.0 285.2 jit_solution(18334632132404332006)
XLA Ops:
  7.2 0.0 all-gather.2.cloned.1.call-start
  7.2 36.5 %first_exchange.1 = (bf16[4,128,1024]{2,1,0:T(8,128)(2,1)}, bf16[4,32,1280]{2,1,0:T(8,128)(2,1)}, bf16[4,32,768]{2,1,0:T(8,128)(2,1)}, bf16[4,4,2,32,768]{4,3,2,...) custom-call(s32[4]{0:T(128)} %len_ref.9, bf16[128,1024]{1,0:T(8,128)(2,1)} %x_ref.5, ...), custom_call_target="tpu_custom_call" | custom-call | tf_op jit(solution)/shard_map/first_exchange/pallas_call | solution.py:37
  43.8 0.0 all-gather.2.cloned.1.call-update
  43.8 0.2 reduce-scatter.2.cloned.1.call-start
  44.0 25.3 %to_heads.1 = (bf16[4,64,512]{2,1,0:T(8,128)(2,1)}, bf16[4,4,2,128,128]{4,3,2,1,0:T(8,128)(2,1)}, bf16[1,4,2,32,1024]{4,3,2,1,0:T(8,128)(2,1)}) custom-call(bf16[512,1024]{1,0:T(8,128)(2,1)} %bitcast.22, bf16[1024,768]{1,0:T(8,128)(2,1)} %bitcast.18, f32[512,128]{1,0:T(8,128)} %get-tuple-element.54.cos_ref, f32[512,128]{1,0:T(8,128)} %get-tuple-element.55.sin_ref, ...), custom_call_target="tpu_custom_call" | custom-call | tf_op jit(solution)/shard_map/to_heads/pallas_call | solution.py:37
  69.3 15.9 %attend.1 = (bf16[4,64,512]{2,1,0:T(8,128)(2,1)}, f32[4,64,512]{2,1,0:T(8,128)}, f32[8,1,256]{2,1,0:T(1,128)}) custom-call(s32[4]{0:T(128)} %len_ref.9, bf16[4,64,512]{2,1,0:T(8,128)(2,1)} %get-tuple-element.56.q_ref, bf16[4096,128]{1,0:T(8,128)(2,1)} %bitcast.20), custom_call_target="tpu_custom_call" | custom-call | tf_op jit(solution)/shard_map/attend/pallas_call | solution.py:907
  85.2 47.8 %mid_exchange.1 = (bf16[4,4,64,128]{3,2,1,0:T(8,128)(2,1)}, f32[128,1024]{1,0:T(8,128)}, bf16[4,128,1024]{2,1,0:T(8,128)(2,1)}, bf16[4,4,2,32,768]{4,3,2,1,0:T(8,128)(2,1)}) custom-call(bf16[4,64,512]{2,1,0:T(8,128)(2,1)} %get-tuple-element.58.o_ref, bf16[256,1024]{1,0:T(8,128)(2,1)} %bitcast.25, bf16[128,1024]{1,0:T(8,128)(2,1)} %x_ref.5, ...), custom_call_target="tpu_custom_call" | custom-call | tf_op jit(solution)/shard_map/mid_exchange/pallas_call | solution.py:37
  133.0 0.0 all-gather.2.cloned.1.call-done
  133.0 14.6 %ffn.1 = (bf16[4,128,1024]{2,1,0:T(8,128)(2,1)}, bf16[4,128,1024]{2,1,0:T(8,128)(2,1)}, bf16[8,4,32,1280]{3,2,1,0:T(8,128)(2,1)}, bf16[8,4,32,768]{3,2,1,0:T(8,128)(2,1)}) custom-call(s32[4]{0:T(128)} %len_ref.9, bf16[4,128,1024]{2,1,0:T(8,128)(2,1)} %get-tuple-element.61.n_hbm, bf16[4,128,1024]{2,1,0:T(8,128)(2,1)} %get-tuple-element.62.g_hbm, ...), custom_call_target="tpu_custom_call" | custom-call | tf_op jit(solution)/shard_map/ffn/pallas_call | solution.py:1280
  147.6 0.0 reduce-scatter.2.cloned.1.call-update
  147.6 34.6 %back_exchange.1 = (f32[128,1024]{1,0:T(8,128)}, f32[128,1024]{1,0:T(8,128)}, bf16[4,64,512]{2,1,0:T(8,128)(2,1)}, bf16[256,1024]{1,0:T(8,128)(2,1)}, bf16[4,4,32,768]{3,2,1,0:T(8,128)(2,1)}) custom-call(s32[4]{0:T(128)} %len_ref.9, bf16[4,128,1024]{2,1,0:T(8,128)(2,1)} %get-tuple-element.65.dpart, bf16[4,128,1024]{2,1,0:T(8,128)(2,1)} %get-tuple-element.66.ypart, ...), custom_call_target="tpu_custom_call" | custom-call | tf_op jit(solution)/shard_map/back_exchange/pallas_call | solution.py:37
  182.2 16.8 %attend_grad.1 = (bf16[4,64,512]{2,1,0:T(8,128)(2,1)}, bf16[4096,128]{1,0:T(8,128)(2,1)}) custom-call(s32[4]{0:T(128)} %len_ref.9, bf16[4,64,512]{2,1,0:T(8,128)(2,1)} %get-tuple-element.56.q_ref, bf16[4,64,512]{2,1,0:T(8,128)(2,1)} %get-tuple-element.70.do_ref, f32[4,64,512]{2,1,0:T(8,128)} %get-tuple-element.71.of_ref, bf16[4096,128]{1,0:T(8,128)(2,1)} %bitcast.21, ...), custom_call_target="tpu_custom_call" | custom-call | tf_op jit(solution)/shard_map/attend_grad/pallas_call | solution.py:975
  199.0 42.8 %grads_back.1 = (bf16[1024,768]{1,0:T(8,128)(2,1)}, bf16[4,128,1024]{2,1,0:T(8,128)(2,1)}, f32[32,1024]{1,0:T(8,128)}, bf16[4,32,768]{2,1,0:T(8,128)(2,1)}) custom-call(bf16[4,64,512]{2,1,0:T(8,128)(2,1)} %get-tuple-element.73.dq_ref, bf16[4,4,2,128,128]{4,3,2,1,0:T(8,128)(2,1)} %bitcast.30, f32[512,128]{1,0:T(8,128)} %get-tuple-element.54.cos_ref, ...), custom_call_target="tpu_custom_call" | custom-call | tf_op jit(solution)/shard_map/grads_back/pallas_call | solution.py:37
  241.8 0.0 reduce-scatter.2.cloned.1.call-done
  241.8 30.7 %last_exchange.1 = (f32[128,1024]{1,0:T(8,128)}, bf16[4,32,768]{2,1,0:T(8,128)(2,1)}, bf16[4,32,1280]{2,1,0:T(8,128)(2,1)}, bf16[4,32,768]{2,1,0:T(8,128)(2,1)}) custom-call(bf16[4,128,1024]{2,1,0:T(8,128)(2,1)} %get-tuple-element.77.dpart, bf16[4,4,2,32,768]{4,3,2,1,0:T(8,128)(2,1)} %bitcast.27, bf16[4,32,1280]{2,1,0:T(8,128)(2,1)} %bitcast.32, ...), custom_call_target="tpu_custom_call" | custom-call | tf_op jit(solution)/shard_map/last_exchange/pallas_call | solution.py:37
  272.5 5.8 %finish.1 = (f32[128,1024]{1,0:T(8,128)}, f32[128,1024]{1,0:T(8,128)}, f32[1,32]{1,0:T(1,128)}, f32[32,3072]{1,0:T(8,128)}, f32[32,1024]{1,0:T(8,128)}, /*index=...) custom-call(f32[128,1024]{1,0:T(8,128)} %get-tuple-element.81.dn_ref, bf16[128,1024]{1,0:T(8,128)(2,1)} %x_ref.5, ...), custom_call_target="tpu_custom_call" | custom-call | tf_op jit(solution)/shard_map/finish/pallas_call | solution.py:1761
Async XLA Ops:
  7.2 125.8 %all-gather.2.cloned.1.call-start = ((), (), s32[]{:S(2)}) async-start(), calls=%async_computation.1 | async-start | bytes 2949120 | tf_op jit(solution)/shard_map/all_gather | solution.py:1799
  43.8 198.0 %reduce-scatter.2.cloned.1.call-start = ((), (), s32[]{:S(2)}) async-start(), calls=%async_computation.2 | async-start | bytes 2949120 | tf_op jit(solution)/shard_map/reduce_scatter | solution.py:1810
Sparse Core Ops, SparseCore 0:
  43.9 67.3 all-gather.1
  147.8 89.0 reduce-scatter.1

commit v4 on v3

--- a/solution.py
+++ b/solution.py
@@ -12,8 +12,9 @@
 ROPE_BASE = 160000.0
 NORM_EPS = 1e-05
 MASK_FLOOR = -1e30
-KEY_BLOCK = 512
-GRAD_CUT = 1280
+GRAD_CUT = 1536
+FF_BLOCKS = 2
+WEIGHT_CUTS = (768, 1024)
 EXP_SCALE = 0.125 * math.log2(math.e)
 BF16 = jnp.bfloat16
 F32 = jnp.float32
@@ -33,13 +34,51 @@
     return lax.axis_index("head"), lax.axis_index("blk")
 
 
-def comm_call(body, name, cid, out_shape, in_specs, out_specs, scratch, args, vmem=None):
+class Staged:
+    def __init__(self, loads, drains):
+        self.loads, self.drains = loads, drains
+
+    def need(self, *which):
+        for i in which:
+            self.loads[i].wait()
+
+    def put(self, *which):
+        for i in which:
+            self.drains[i].start()
+
+
+def comm_call(body, name, cid, out_shape, in_specs, out_specs, scratch, args, vmem=None, late=(), early=()):
+    n_in, n_out, n_late, n_early = len(args), len(out_shape), len(late), len(early)
+    in_specs = [ANY if i in late else spec for i, spec in enumerate(in_specs)]
+    out_specs = [ANY if i in early else spec for i, spec in enumerate(out_specs)]
+    held = [pltpu.VMEM(args[i].shape, args[i].dtype) for i in late]
+    held += [pltpu.VMEM(out_shape[i].shape, out_shape[i].dtype) for i in early]
+    held.append(pltpu.SemaphoreType.DMA((max(n_late + n_early, 1),)))
+
+    def staged_body(*refs):
+        ins, outs = list(refs[:n_in]), list(refs[n_in : n_in + n_out])
+        bufs = refs[n_in + n_out : n_in + n_out + n_late + n_early]
+        sems = refs[n_in + n_out + n_late + n_early]
+        rest = refs[n_in + n_out + n_late + n_early + 1 :]
+        loads, drains = {}, {}
+        for k, i in enumerate(late):
+            loads[i] = pltpu.make_async_copy(ins[i], bufs[k], sems.at[k])
+            loads[i].start()
+            ins[i] = bufs[k]
+        for k, i in enumerate(early):
+            k += n_late
+            drains[i] = pltpu.make_async_copy(bufs[k], outs[i], sems.at[k])
+            outs[i] = bufs[k]
+        body(Staged(loads, drains), *ins, *outs, *rest)
+        for cp in drains.values():
+            cp.wait()
+
     return pl.pallas_call(
-        body,
+        staged_body,
         out_shape=out_shape,
         in_specs=in_specs,
         out_specs=out_specs,
-        scratch_shapes=scratch,
+        scratch_shapes=held + list(scratch),
         name=name,
         compiler_params=pltpu.CompilerParams(
             collective_id=cid, has_side_effects=True, vmem_limit_bytes=vmem
@@ -62,25 +101,6 @@
     pl.semaphore_signal(
         pltpu.get_barrier_semaphore(), inc=1, device_id=(h, b), device_id_type=MESH_ID
     )
-
-
-def signal_head(nh, h, b):
-    for i in range(1, nh):
-        signal((h + i) % nh, b)
-
-
-def wait_head(nh):
-    pl.semaphore_wait(pltpu.get_barrier_semaphore(), nh - 1)
-
-
-def signal_all(nh, nb, h, b):
-    @pl.loop(1, nh * nb)
-    def _(i):
-        signal((h + i // nb) % nh, (b + i % nb) % nb)
-
-
-def wait_all(nh, nb):
-    pl.semaphore_wait(pltpu.get_barrier_semaphore(), nh * nb - 1)
 
 
 class HeadGather:
@@ -144,6 +164,11 @@
     return jnp.concatenate([values, jnp.zeros((values.shape[0], extra), values.dtype)], axis=1)
 
 
+def weight_parts(total):
+    marks = (0,) + WEIGHT_CUTS + (total,)
+    return list(zip(marks[:-1], marks[1:]))
+
+
 def column(row):
     n = row.shape[1]
     same = lax.broadcasted_iota(jnp.int32, (n, n), 0) == lax.broadcasted_iota(jnp.int32, (n, n), 1)
@@ -512,7 +537,7 @@
             self.near(i).wait()
 
 
-def first_body(nh, nb, hl, fl, len_ref, x_ref, wq_ref, ga_ref, win_hbm, gf_ref, wd_hbm, g_ref, n1_all, wma, wmb, wq_all, gg, cos_ref, sin_ref, own_n, pack, wmp, win_ref, wd_ref, lsem, wsem, ksem, gsem, msem, stage):
+def first_body(nh, nb, hl, fl, io, len_ref, x_ref, wq_ref, ga_ref, win_hbm, gf_ref, wd_hbm, g_ref, n1_all, wma, wmb, wmc, wq_all, gg, cos_ref, sin_ref, own_n, pack, wmp, win_ref, wd_ref, lsem, wsem, ksem, gsem, msem, stage):
     pc = Place(nh, nb, hl)
     h, b = pc.h, pc.b
     loads = [
@@ -521,10 +546,11 @@
     ]
     for cp in loads:
         cp.start()
-    signal_all(nh, nb, h, b)
+    signal_near(pc)
     width = x_ref.shape[1]
     lw = width // pc.nz
     gain = column(ga_ref[...].astype(F32))
+    io.need(2)
     for c in range(3):
         w = wq_ref[:, c * width : (c + 1) * width].astype(F32) * gain
         tile = lambda l, i: w[:, l * pc.nz * DH + i // 2 * 128 : l * pc.nz * DH + i // 2 * 128 + 128]
@@ -533,8 +559,9 @@
                 both = half_pick(tile(2 * p, i), tile(2 * p + 1, i), i % 2, i % 2)
                 at = c * lw + p * 128
                 pack[i, :, at : at + 128] = both.astype(BF16)
+    io.need(1)
     own_n[...] = norm_of(x_ref[...].astype(F32))[0].astype(BF16)
-    wait_all(nh, nb)
+    wait_near(pc)
     weights = PlaneWeights(pc, pack, wq_all, wsem, ksem)
     line = LineGather(pc, own_n, lambda zi: n1_all.at[zi], lsem)
     gather = HeadGather(nh, h, b, g_ref, gg, gsem)
@@ -543,7 +570,7 @@
     gather.start()
     for cp in loads:
         cp.wait()
-    total, _, off = ff_widths(fl)
+    total = ff_widths(fl)[0]
     ff = nh * fl
     win = win_ref[...].astype(F32) * column(gf_ref[...].astype(F32))
     wd = widen(wd_ref[...].astype(F32), total if total > ff else (ff + 127) // 128 * 128)
@@ -559,7 +586,8 @@
         )
         wmp[i] = piece.astype(BF16)
     copies = []
-    for n, (dst, cols) in enumerate(((wma, pl.ds(0, off)), (wmb, pl.ds(off, total - off)))):
+    for n, (dst, (begin, end)) in enumerate(zip((wma, wmb, wmc), weight_parts(total))):
+        cols = pl.ds(begin, end - begin)
         for i in range(1, nh):
             th = (h + i) % nh
             src = wmp.at[th, :, cols]
@@ -580,6 +608,7 @@
         angle = (slot - segment_first(slot, ends)).astype(F32) * inv_freq
         cos_ref[i * rows : (i + 1) * rows, :] = jnp.cos(angle)
         sin_ref[i * rows : (i + 1) * rows, :] = jnp.sin(angle) * sign
+    io.put(6, 7)
     gather.pass_on()
     for t in range(2, pc.nz):
         line.step(t)
@@ -597,7 +626,7 @@
     nz, qs = hl, nb // hl
     lw = width // nz
     own_rows = w_in.shape[0]
-    total, _, off = ff_widths(fl)
+    total = ff_widths(fl)[0]
     dma = pltpu.SemaphoreType.DMA
     return comm_call(
         functools.partial(first_body, nh, nb, hl, fl),
@@ -605,15 +634,17 @@
         0,
         (
             jax.ShapeDtypeStruct((nz, rows, width), BF16),
-            jax.ShapeDtypeStruct((nh, own_rows, off), BF16),
-            jax.ShapeDtypeStruct((nh, own_rows, total - off), BF16),
+            *[
+                jax.ShapeDtypeStruct((nh, own_rows, end - begin), BF16)
+                for begin, end in weight_parts(total)
+            ],
             jax.ShapeDtypeStruct((nh, nz, qs, own_rows, 3 * lw), BF16),
             jax.ShapeDtypeStruct((nh, rows, width), BF16),
             jax.ShapeDtypeStruct((nz * rows, 2 * DH), F32),
             jax.ShapeDtypeStruct((nz * rows, 2 * DH), F32),
         ),
         [SM, VM, VM, VM, ANY, VM, ANY, ANY],
-        [ANY] * 5 + [VM] * 2,
+        [ANY] * 6 + [VM] * 2,
         [
             pltpu.VMEM((rows, width), BF16),
             pltpu.VMEM((nz, own_rows, 3 * lw), BF16),
@@ -625,11 +656,13 @@
         + PlaneWeights.sem_shapes(nh, nz, qs)
         + [
             HeadGather.sem_shape(nh),
-            dma((2, 2, nh)),
+            dma((2, 3, nh)),
             dma((2,)),
         ],
         (lengths, x, w_qkv, gain_attn, w_in, gain_mlp, wd_t, g),
         vmem=60 << 20,
+        late=(2, 1),
+        early=(6, 7),
     )
 
 
@@ -651,6 +684,29 @@
         return (l // 2) * 2 + core, zi * self.qs + (l % 2) * self.cb + u
 
 
+def signal_near(pc):
+    here = pc.nh * pc.qs
+
+    @pl.loop(1, here)
+    def _(i):
+        signal((pc.h + i // pc.qs) % pc.nh, pc.zi * pc.qs + (pc.s + i % pc.qs) % pc.qs)
+
+    @pl.loop(1, pc.nz)
+    def _(i):
+        signal(pc.h, (pc.zi + i) % pc.nz * pc.qs + pc.s)
+
+
+def wait_near(pc, more=0):
+    pl.semaphore_wait(pltpu.get_barrier_semaphore(), pc.nh * pc.qs + pc.nz - 2 + more)
+
+
+def enter_with(pc, source):
+    signal_near(pc)
+    for i in range(1, pc.nz):
+        signal(*source((pc.zi + i) % pc.nz))
+    wait_near(pc, pc.nz - 1)
+
+
 def routed(pc, src, dst, send, recv, th, tb, act):
     mine = jnp.logical_and(th == pc.h, tb == pc.b)
 
@@ -716,7 +772,7 @@
     return tile * cos + halves_swapped(tile) * sin
 
 
-def to_heads_body(nh, nb, hl, n1_hbm, w_hbm, cos_ref, sin_ref, wo_ref, qin, kvin, wo_all, qbuf, kvbuf, n1_ref, w_ref, qsem, ksem, fsem, osem, osem2, stage):
+def to_heads_body(nh, nb, hl, io, n1_hbm, w_hbm, cos_ref, sin_ref, wo_ref, wmb_ref, qin, kvin, wo_all, wmb_all, qbuf, kvbuf, n1_ref, w_ref, qsem, ksem, fsem, osem, osem2, bsem, bsem2, stage):
     pc = Place(nh, nb, hl)
     loads = [
         pltpu.make_async_copy(n1_hbm, n1_ref, stage.at[0]),
@@ -724,12 +780,13 @@
     ]
     for cp in loads:
         cp.start()
-    signal_all(nh, nb, pc.h, pc.b)
+    signal_near(pc)
     rows = kvbuf.shape[2]
     lw = nh * DH
     for cp in loads:
         cp.wait()
     n1 = n1_ref[...]
+    io.need(2, 3)
     cos, sin = cos_ref[...], sin_ref[...]
     kk = jnp.dot(n1, w_ref[:, lw : 2 * lw], preferred_element_type=F32)
     vv = jnp.dot(n1, w_ref[:, 2 * lw :], preferred_element_type=F32)
@@ -742,7 +799,7 @@
         for i in range(pc.nz):
             kvbuf[2 * p, i] = even[i * rows : (i + 1) * rows]
             kvbuf[2 * p + 1, i] = odd[i * rows : (i + 1) * rows]
-    wait_all(nh, nb)
+    wait_near(pc)
 
     def keys_out(act):
         for l in range(nh):
@@ -767,8 +824,10 @@
             )
 
     spread = BlkGather(pc, wo_ref, wo_all, osem, osem2)
+    spread_b = BlkGather(pc, wmb_ref, wmb_all, bsem, bsem2)
     keys_out("start")
     spread.start()
+    spread_b.start()
     qq = jnp.dot(n1, w_ref[:, :lw], preferred_element_type=F32)
     for p in range(nh // 2):
         q = turned(qq[:, p * 128 : (p + 1) * 128], cos, sin).T.astype(BF16)
@@ -788,6 +847,7 @@
 
     for t in range(1, pc.nz):
         spread.step(t)
+        spread_b.step(t)
     keys_out("wait_send")
     queries_out("wait_send")
     for i in range(nh):
@@ -798,9 +858,10 @@
         forward(i).wait()
 
     spread.finish()
-
-
-def to_heads(n1, wq, cos, sin, wo, hl):
+    spread_b.finish()
+
+
+def to_heads(n1, wq, cos, sin, wo, wmb, hl):
     nh, nb = dims()
     group, width = n1.shape
     nz, qs = hl, nb // hl
@@ -815,9 +876,10 @@
             jax.ShapeDtypeStruct((nh, DH, group), BF16),
             jax.ShapeDtypeStruct((nh, nz, qs, rows, 2 * DH), BF16),
             jax.ShapeDtypeStruct((1, nz, qs) + wo.shape[1:], BF16),
+            jax.ShapeDtypeStruct((nh, nz, qs) + wmb.shape[1:], BF16),
         ),
-        [ANY, ANY, VM, VM, ANY],
-        [ANY, ANY, ANY],
+        [ANY, ANY, VM, VM, ANY, ANY],
+        [ANY] * 4,
         [
             pltpu.VMEM((nh, DH, group), BF16),
             pltpu.VMEM((nh, nz, rows, 2 * DH), BF16),
@@ -827,65 +889,73 @@
             dma((2, nh * cb)),
             dma((2, nh * cb)),
         ]
-        + BlkGather.sem_shapes(nz, qs)
+        + BlkGather.sem_shapes(nz, qs) * 2
         + [dma((2,))],
-        (n1, wq, cos, sin, wo),
+        (n1, wq, cos, sin, wo, wmb),
         vmem=60 << 20,
+        late=(2, 3),
     )
 
 
 class Queries:
-    def __init__(self, nh, nb, hl, len_ref, lanes, slots):
+    def __init__(self, nh, nb, hl, len_ref, lanes, slots, size):
         pc = Place(nh, nb, hl)
         tile = pl.program_id(0)
-        rows = lanes // 2
-        each = pc.nz // 2
+        rows = slots // (nh * nb)
+        count = lanes // rows
+        each = pc.nz // count
         ends = sequence_ends(len_ref)
-        base = (tile // each) * nb + (tile % each) * 2 * pc.qs + pc.from_s
+        base = (tile // each) * nb + (tile % each) * count * pc.qs + pc.from_s
         lane = lax.broadcasted_iota(jnp.int32, (1, lanes), 1)
-        slot = (base + jnp.where(lane < rows, 0, pc.qs)) * rows + lane % rows
+        slot = (base + lane // rows * pc.qs) * rows + lane % rows
         self.first = segment_first(slot, ends)
         self.last = segment_end(slot, ends, slots)
-        self.lo = segment_first(base * rows, ends) // KEY_BLOCK
-        far = (base + pc.qs) * rows + rows - 1
-        self.hi = (segment_end(far, ends, slots) + KEY_BLOCK - 1) // KEY_BLOCK
+        near = base * rows
+        far = (base + (count - 1) * pc.qs) * rows + rows - 1
+        self.size = size
+        self.lo = segment_first(near, ends) // size
+        self.hi = (segment_end(far, ends, slots) + size - 1) // size
+        self.open = jnp.minimum((segment_first(far, ends) + size - 1) // size, self.hi)
+        self.close = jnp.maximum(segment_end(near, ends, slots) // size, self.open)
         self.lanes = lanes
 
     def allowed(self, block_at):
-        at = block_at * KEY_BLOCK + lax.broadcasted_iota(jnp.int32, (KEY_BLOCK, self.lanes), 0)
+        at = block_at * self.size + lax.broadcasted_iota(jnp.int32, (self.size, self.lanes), 0)
         return jnp.logical_and(at >= self.first, at < self.last)
 
-
-def attend_body(nh, nb, hl, len_ref, q_ref, kv_ref, o_ref, of_ref, lse_ref):
+    def walk(self, step, carry):
+        masked = lambda j, kept: step(j, kept, True)
+        carry = lax.fori_loop(self.lo, self.open, masked, carry)
+        carry = lax.fori_loop(self.open, self.close, lambda j, kept: step(j, kept, False), carry)
+        return lax.fori_loop(self.close, self.hi, masked, carry)
+
+
+def attend_body(nh, nb, hl, size, len_ref, q_ref, kv_ref, o_ref, of_ref, lse_ref):
     q = q_ref[0]
     lanes = q.shape[1]
-    at = Queries(nh, nb, hl, len_ref, lanes, kv_ref.shape[0])
+    at = Queries(nh, nb, hl, len_ref, lanes, kv_ref.shape[0], size)
     q_pad = jnp.concatenate([q, jnp.zeros_like(q)], axis=0)
-
-    def step(j, carry):
-        top, total, acc = carry
-        kv = kv_ref[pl.ds(pl.multiple_of(j * KEY_BLOCK, KEY_BLOCK), KEY_BLOCK), :]
+    is_key = lax.broadcasted_iota(jnp.int32, (1, 2 * DH), 1) < DH
+
+    def step(j, carry, masked):
+        top, acc = carry
+        kv = kv_ref[pl.ds(pl.multiple_of(j * size, size), size), :]
         s = jnp.dot(kv, q_pad, preferred_element_type=F32)
-        s = jnp.where(at.allowed(j), s, MASK_FLOOR)
+        if masked:
+            s = jnp.where(at.allowed(j), s, MASK_FLOOR)
         new_top = jnp.maximum(top, jnp.max(s, axis=0, keepdims=True))
-        p = jnp.exp2((s - new_top) * EXP_SCALE)
+        p = jnp.exp2((s - new_top) * EXP_SCALE).astype(BF16)
         alpha = jnp.exp2((top - new_top) * EXP_SCALE)
-        total = total * alpha + jnp.sum(p, axis=0, keepdims=True)
+        ones_values = jnp.where(is_key, jnp.ones_like(kv), kv)
         acc = acc * alpha + lax.dot_general(
-            kv, p.astype(BF16), (((0,), (0,)), ((), ())), preferred_element_type=F32
-        )
-        return new_top, total, acc
-
-    top, total, acc = lax.fori_loop(
-        at.lo,
-        at.hi,
-        step,
-        (
-            jnp.full((1, lanes), MASK_FLOOR, F32),
-            jnp.zeros((1, lanes), F32),
-            jnp.zeros((2 * DH, lanes), F32),
-        ),
+            ones_values, p, (((0,), (0,)), ((), ())), preferred_element_type=F32
+        )
+        return new_top, acc
+
+    top, acc = at.walk(
+        step, (jnp.full((1, lanes), MASK_FLOOR, F32), jnp.zeros((2 * DH, lanes), F32))
     )
+    total = acc[:1]
     o = acc[DH:] / total
     of_ref[0] = o
     o_ref[0] = o.astype(BF16)
@@ -899,13 +969,13 @@
     return tile_spec, row_spec, kv_spec
 
 
-def attend(lengths, q, kv, lanes, hl):
+def attend(lengths, q, kv, lanes, size, hl):
     nh, nb = dims()
     each = q.shape[2] // lanes
     tiles = q.shape[0] * each
     tile_spec, row_spec, kv_spec = attend_specs(kv.shape[0], lanes, each)
     return pl.pallas_call(
-        functools.partial(attend_body, nh, nb, hl),
+        functools.partial(attend_body, nh, nb, hl, size),
         grid_spec=pltpu.PrefetchScalarGridSpec(
             num_scalar_prefetch=1,
             grid=(tiles,),
@@ -922,7 +992,7 @@
     )(lengths, q, kv)
 
 
-def attend_grad_body(nh, nb, hl, len_ref, q_ref, do_ref, of_ref, kv_ref, lse_ref, dq_ref, dkv_ref, acc_ref):
+def attend_grad_body(nh, nb, hl, size, len_ref, q_ref, do_ref, of_ref, kv_ref, lse_ref, dq_ref, dkv_ref, acc_ref):
     tile = pl.program_id(0)
 
     @pl.when(tile == 0)
@@ -932,7 +1002,7 @@
     q = q_ref[0]
     do = do_ref[0]
     lanes = q.shape[1]
-    place = Queries(nh, nb, hl, len_ref, lanes, kv_ref.shape[0])
+    place = Queries(nh, nb, hl, len_ref, lanes, kv_ref.shape[0], size)
     zero = jnp.zeros_like(q)
     both = jnp.concatenate(
         [jnp.concatenate([q, zero], axis=0), jnp.concatenate([zero, do], axis=0)], axis=1
@@ -940,14 +1010,15 @@
     delta = jnp.sum(do.astype(F32) * of_ref[0], axis=0, keepdims=True)
     lse = lse_ref[0]
 
-    def step(j, dq):
-        at = pl.ds(pl.multiple_of(j * KEY_BLOCK, KEY_BLOCK), KEY_BLOCK)
+    def step(j, dq, masked):
+        at = pl.ds(pl.multiple_of(j * size, size), size)
         kv = kv_ref[at, :]
         sd = jnp.dot(kv, both, preferred_element_type=F32)
         s, dp = sd[:, :lanes], sd[:, lanes:]
-        p = jnp.exp2(
-            jnp.where(place.allowed(j), s * EXP_SCALE - lse, MASK_FLOOR)
-        )
+        power = s * EXP_SCALE - lse
+        if masked:
+            power = jnp.where(place.allowed(j), power, MASK_FLOOR)
+        p = jnp.exp2(power)
         ds = (p * (dp - delta)).astype(BF16)
         acc_ref[at, :] += lax.dot_general(
             jnp.concatenate([ds, p.astype(BF16)], axis=1),
@@ -959,7 +1030,7 @@
             kv, ds, (((0,), (0,)), ((), ())), preferred_element_type=F32
         )
 
-    dq = lax.fori_loop(place.lo, place.hi, step, jnp.zeros((2 * DH, lanes), F32))
+    dq = place.walk(step, jnp.zeros((2 * DH, lanes), F32))
     dq_ref[0] = (dq[:DH] * 0.125).astype(BF16)
 
     @pl.when(tile == pl.num_programs(0) - 1)
@@ -968,12 +1039,13 @@
         dkv_ref[...] = (acc_ref[...] * jnp.where(lane < DH, 0.125, 1.0)).astype(BF16)
 
 
-def attend_grad(lengths, q, do, of, kv, lse, hl):
+def attend_grad(lengths, q, do, of, kv, lse, lanes, size, hl):
     nh, nb = dims()
-    tiles, _, lanes = lse.shape
+    tiles = lse.size // lanes
+    lse = lse.reshape(tiles, 1, lanes)
     tile_spec, row_spec, kv_spec = attend_specs(kv.shape[0], lanes, tiles // q.shape[0])
     return pl.pallas_call(
-        functools.partial(attend_grad_body, nh, nb, hl),
+        functools.partial(attend_grad_body, nh, nb, hl, size),
         grid_spec=pltpu.PrefetchScalarGridSpec(
             num_scalar_prefetch=1,
             grid=(tiles,),
@@ -1099,11 +1171,10 @@
     return pltpu.SemaphoreType.DMA((CHUNKS, 4, nh // 2))
 
 
-def mid_body(nh, nb, hl, o_ref, wo_ref, x_ref, wmb_ref, og, hid_ref, ng_ref, wmb_all, part, near, far, out, nbuf, osem, ssem, gsem, wsem, wsem2):
+def mid_body(nh, nb, hl, io, o_ref, wo_ref, x_ref, wmb_ref, og, hid_ref, ng_ref, wmb_all, part, near, far, out, nbuf, osem, ssem, gsem, wsem, wsem2):
     pc = Place(nh, nb, hl)
     h, b = pc.h, pc.b
-    signal_all(nh, nb, h, b)
-    wait_all(nh, nb)
+    enter_with(pc, lambda zi: pc.attends(zi, h, pc.s % 2, pc.s // 2))
     rows, width = x_ref.shape
     outputs_back(pc, o_ref, og, osem, "start")
     spread = BlkGather(pc, wmb_ref, wmb_all, wsem, wsem2)
@@ -1111,6 +1182,8 @@
     outputs_back(pc, o_ref, og, osem, "wait_send")
     for zi in range(pc.nz):
         wait_on(og.at[zi], osem.at[1, zi])
+    io.put(0)
+    io.need(1)
     wo = wo_ref[...]
     for i in range(nh):
         part[i] = lax.dot_general(
@@ -1127,12 +1200,14 @@
     for hs in hss:
         hs.send()
     size = rows // CHUNKS
+    io.need(2)
     for j, (hs, hg) in enumerate(zip(hss, hgs)):
         at = pl.ds(j * size, size)
         hid = x_ref[at, :].astype(F32) + hs.total()
         hid_ref[at, :] = hid
         nbuf[at, :] = norm_of(hid)[0].astype(BF16)
         hg.start()
+    io.put(1)
     spread.step(2)
     for hg in hgs:
         hg.pass_on()
@@ -1158,8 +1233,8 @@
             jax.ShapeDtypeStruct((nh, rows, width), BF16),
             jax.ShapeDtypeStruct((nh, nz, nb // nz) + wmb.shape[1:], BF16),
         ),
-        [ANY, VM, VM, ANY],
-        [VM, VM, VM, ANY],
+        [ANY] * 4,
+        [ANY] * 4,
         [pltpu.VMEM((nh, rows, width), BF16)]
         + HeadSum.buffers(nh, rows, width)
         + [
@@ -1171,33 +1246,36 @@
         + BlkGather.sem_shapes(nz, nb // nz),
         (ot, wo, x, wmb),
         vmem=60 << 20,
+        late=(1, 2),
+        early=(0, 1),
     )
 
 
-def ffn_body(nh, nb, fl, split_rows, cut, len_ref, n_hbm, g_hbm, wa_hbm, wb_hbm, y_hbm, d_hbm, ga_hbm, gb_hbm, n_ref, g_ref, w_ref, y_ref, d_ref, ga_ref, gb_ref, gy, mm, dz, stage, drain):
+def ffn_body(nh, nb, fl, split_rows, cut, len_ref, n_hbm, g_hbm, wa_hbm, wb_hbm, wc_hbm, y_hbm, d_hbm, ga_hbm, gb_hbm, n_ref, g_ref, w_ref, y_ref, d_ref, ga_ref, gb_ref, gy, mm, dz, stage, drain):
     rows, width = n_ref.shape[1], n_ref.shape[2]
     group = nh * rows
     total, zc, off = ff_widths(fl)
     wide = total - off
     shift = 2 * fl - off
-    step = 2 * rows
+    step = FF_BLOCKS * rows
     lane = lax.broadcasted_iota(jnp.int32, (1, wide), 1)
     real = lane < fl
     valid = sequence_ends(len_ref)[-1]
     blk = lax.axis_index("blk")
     loads = [
         pltpu.make_async_copy(n_hbm, n_ref, stage.at[0]),
-        pltpu.make_async_copy(wa_hbm, w_ref.at[:, pl.ds(0, off)], stage.at[1]),
-        pltpu.make_async_copy(wb_hbm, w_ref.at[:, pl.ds(off, wide)], stage.at[2]),
-        pltpu.make_async_copy(g_hbm, g_ref, stage.at[3]),
+        pltpu.make_async_copy(g_hbm, g_ref, stage.at[1]),
     ]
+    for n, (w, (begin, end)) in enumerate(zip((wa_hbm, wb_hbm, wc_hbm), weight_parts(total))):
+        dst = w_ref.at[:, pl.ds(begin, end - begin)]
+        loads.append(pltpu.make_async_copy(w, dst, stage.at[2 + n]))
     for cp in loads:
         cp.start()
     for cp in loads:
         cp.wait()
 
     def out_rows(r):
-        at = pl.ds(r * 2, 2)
+        at = pl.ds(r * FF_BLOCKS, FF_BLOCKS)
         return [
             pltpu.make_async_copy(d_ref.at[at], d_hbm.at[at], drain.at[0, r]),
             pltpu.make_async_copy(y_ref.at[at], y_hbm.at[at], drain.at[1, r]),
@@ -1206,10 +1284,10 @@
     @pl.loop(0, group // step)
     def _(r):
         at = pl.ds(pl.multiple_of(r * step, step), step)
-        n = n_ref[pl.ds(r * 2, 2)].reshape(step, width)
+        n = n_ref[pl.ds(r * FF_BLOCKS, FF_BLOCKS)].reshape(step, width)
         row = lax.broadcasted_iota(jnp.int32, (step, 1), 0)
-        slot = ((r * 2 + row // rows) * nb + blk) * rows + row % rows
-        g = g_ref[pl.ds(r * 2, 2)].reshape(step, width)
+        slot = ((r * FF_BLOCKS + row // rows) * nb + blk) * rows + row % rows
+        g = g_ref[pl.ds(r * FF_BLOCKS, FF_BLOCKS)].reshape(step, width)
         g = jnp.where(slot < valid, g.astype(F32), 0.0).astype(BF16)
         gy[at, :] = g
         z = jnp.dot(n, w_ref[:, :zc], preferred_element_type=F32)
@@ -1226,9 +1304,9 @@
         dz[at, :] = d
         nt = (((1,), (1,)), ((), ()))
         dpart = lax.dot_general(d, w_ref[:, :zc], nt, preferred_element_type=F32)
-        d_ref[pl.ds(r * 2, 2)] = dpart.astype(BF16).reshape(2, rows, width)
+        d_ref[pl.ds(r * FF_BLOCKS, FF_BLOCKS)] = dpart.astype(BF16).reshape(FF_BLOCKS, rows, width)
         ypart = lax.dot_general(m, w_ref[:, off:], nt, preferred_element_type=F32)
-        y_ref[pl.ds(r * 2, 2)] = ypart.astype(BF16).reshape(2, rows, width)
+        y_ref[pl.ds(r * FF_BLOCKS, FF_BLOCKS)] = ypart.astype(BF16).reshape(FF_BLOCKS, rows, width)
         for cp in out_rows(r):
             cp.start()
 
@@ -1269,7 +1347,7 @@
             cp.wait()
 
 
-def ffn(lengths, n2, g, wma, wmb, fl, own_rows, cut):
+def ffn(lengths, n2, g, weights, fl, own_rows, cut):
     nh, nb = dims()
     _, rows, width = n2.shape
     group = nh * rows
@@ -1285,7 +1363,7 @@
             jax.ShapeDtypeStruct(lead + (cut,), BF16),
             jax.ShapeDtypeStruct(lead + (total - cut,), BF16),
         ),
-        in_specs=[SM, ANY, ANY, ANY, ANY],
+        in_specs=[SM] + [ANY] * 5,
         out_specs=[ANY] * 4,
         scratch_shapes=[
             pltpu.VMEM(n2.shape, BF16),
@@ -1298,21 +1376,20 @@
             pltpu.VMEM((group, width), BF16),
             pltpu.VMEM((group, total - off), BF16),
             pltpu.VMEM((group, zc), BF16),
-            pltpu.SemaphoreType.DMA((4,)),
+            pltpu.SemaphoreType.DMA((5,)),
             pltpu.SemaphoreType.DMA((4, nh)),
         ],
         name="ffn",
         compiler_params=pltpu.CompilerParams(vmem_limit_bytes=60 << 20),
-    )(lengths, n2, g, wma, wmb)
-
-
-def back_body(nh, nb, hl, len_ref, dpart, ypart, hid_ref, g_ref, wo_ref, og_ref, gb_hbm, y_ref, dh_ref, do_in, go_ref, gb_out, n1, f1, o1, n2, f2, o2, dbuf, dg, dots, gb_ref, nearb, s1, s2, gsem, qsem, pb, stage):
+    )(lengths, n2, g, *weights)
+
+
+def back_body(nh, nb, hl, io, len_ref, dpart, ypart, hid_ref, g_ref, wo_ref, og_ref, gb_hbm, y_ref, dh_ref, do_in, go_ref, gb_out, n1, f1, o1, n2, f2, o2, dbuf, dg, dots, gb_ref, nearb, s1, s2, gsem, qsem, pb, stage):
     pc = Place(nh, nb, hl)
     h, b = pc.h, pc.b
     mine = pltpu.make_async_copy(gb_hbm.at[:, pc.s], gb_ref, stage)
     mine.start()
-    signal_all(nh, nb, h, b)
-    wait_all(nh, nb)
+    enter_with(pc, lambda zi: (pc.head, zi * pc.qs + pc.from_s))
     pairs = [
         remote(
             gb_hbm.at[:, (pc.s + ds) % pc.qs],
@@ -1330,6 +1407,7 @@
     hds = head_sums(nh, h, b, dpart, (n1, f1, o1), s1)
     hy = HeadSum(nh, h, b, ypart, n2, f2, o2, s2)
     hgs = head_gathers(nh, h, b, dbuf, dg, gsem)
+    io.need(1)
     for hd in hds:
         hd.start()
     for cp in pairs:
@@ -1337,6 +1415,7 @@
     for hd in hds:
         hd.send()
     size = rows // CHUNKS
+    io.need(3, 4)
     for j, (hd, hg) in enumerate(zip(hds, hgs)):
         at = pl.ds(j * size, size)
         normed, scale = norm_of(hid_ref[at, :])
@@ -1345,6 +1424,8 @@
         dh_ref[at, :] = dh
         dbuf[at, :] = dh.astype(BF16)
         hg.start()
+    io.put(1)
+    io.need(2)
     hy.start()
     for hg in hgs:
         hg.pass_on()
@@ -1352,6 +1433,7 @@
     for hd, hg in zip(hds, hgs):
         hd.finish()
         hg.finish()
+    io.need(5)
     wo = wo_ref[...]
     nt = (((1,), (1,)), ((), ()))
     for i in range(nh):
@@ -1359,12 +1441,15 @@
         dots[:, i] = part.reshape(pc.nz, DH, rows)
     grads_out(pc, dots, do_in, qsem, "start")
     total = 0.0
+    io.need(6)
     for i in range(nh):
         total = total + jnp.dot(
             og_ref[:, i].reshape(pc.nz * DH, rows), dg[i], preferred_element_type=F32
         )
     go_ref[...] = total.astype(BF16)
+    io.put(3)
     y_ref[...] = jnp.where(valid, hid_ref[...] + hy.total(), 0.0)
+    io.put(0)
     hy.finish()
     mine.wait()
     for cp in pairs:
@@ -1375,6 +1460,7 @@
         others = jnp.sum(nearb[:, d].astype(F32), axis=0)
         gb_out[d] = (gb_ref[d].astype(F32) + others).astype(BF16)
 
+    io.put(4)
     grads_out(pc, dots, do_in, qsem, "wait_send")
     for zi in range(pc.nz):
         wait_on(stretch_lanes(do_in, zi, rows), qsem.at[1, zi])
@@ -1414,10 +1500,12 @@
         ],
         (lengths, dpart, ypart, hid, g, wo, og, gb),
         vmem=60 << 20,
+        late=(1, 3, 4, 2, 5, 6),
+        early=(0, 1, 3, 4),
     )
 
 
-def grads_back_body(nh, nb, hl, dq_ref, dkv_ref, cos_ref, sin_ref, n1_hbm, w_hbm, go_ref, gb_ref, gq_ref, dpart, do_ref, gb_sum, got, sums, dq_out, dkv_out, dqkv, n1_ref, w_ref, nearo, sumo, goto, lsem, gotb, bsem, qsem, psem, ksem, stage, po):
+def grads_back_body(nh, nb, hl, io, dq_ref, dkv_ref, cos_ref, sin_ref, n1_hbm, w_hbm, go_ref, gb_ref, gq_ref, dpart, do_ref, gb_sum, got, sums, dq_out, dkv_out, dqkv, n1_ref, w_ref, nearo, sumo, goto, lsem, gotb, bsem, qsem, psem, ksem, stage, po):
     pc = Place(nh, nb, hl)
     loads = [
         pltpu.make_async_copy(n1_hbm, n1_ref, stage.at[0]),
@@ -1425,8 +1513,8 @@
     ]
     for cp in loads:
         cp.start()
-    signal_all(nh, nb, pc.h, pc.b)
-    wait_all(nh, nb)
+    signal_near(pc)
+    wait_near(pc)
     rows = dkv_ref.shape[3]
     group = pc.nz * rows
     width = n1_ref.shape[1]
@@ -1476,11 +1564,14 @@
     along_o = StretchSum(pc, sumo, goto, lsem)
     along_b = StretchSum(pc, gb_ref, gotb, bsem)
 
+    io.need(1)
+
     @pl.loop(0, count)
     def _(k):
         pair(k).start()
 
     queries_back("start")
+    io.need(6, 7)
     for cp in pairs_o:
         cp.start()
     along_b.start()
@@ -1496,6 +1587,7 @@
         cp.wait_recv()
     sumo[...] = (go_ref[:, pc.s].astype(F32) + jnp.sum(nearo[...].astype(F32), axis=0)).astype(BF16)
     along_o.start()
+    io.need(2, 3)
     cos, sin = cos_ref[...], -sin_ref[...]
     for l in range(nh):
         wait_on(dq_out.at[l], qsem.at[1, l])
@@ -1527,6 +1619,8 @@
             n1_ref[:, cols], dqkv[...], tn, preferred_element_type=F32
         ).astype(BF16)
 
+    io.put(0)
+
     @pl.loop(0, pc.nz)
     def _(i):
         at = pl.ds(pl.multiple_of(i * rows, rows), rows)
@@ -1534,6 +1628,8 @@
             dqkv[at, :], w_ref[...], nt, preferred_element_type=F32
         ).astype(BF16)
 
+    io.put(1)
+
     @pl.loop(0, count)
     def _(k):
         pair(k).wait_send()
@@ -1541,7 +1637,9 @@
 
     queries_back("wait_send")
     do_ref[...] = along_o.total()
+    io.put(2)
     gb_sum[...] = along_b.total().astype(BF16)
+    io.put(3)
     along_o.finish()
     along_b.finish()
     for cp in pairs_o:
@@ -1590,14 +1688,16 @@
         ],
         (dq, dkv, cos, sin, n1, wq, go, gb),
         vmem=60 << 20,
+        late=(1, 6, 7, 2, 3),
+        early=(0, 1, 2, 3),
     )
 
 
-def last_body(nh, nb, hl, dpart, gq_ref, gma_ref, gmb_ref, dn_ref, quarters, gma_all, gmb_all, nearq, sumq, farq, totq, sentz, gotz, zsem, pq, fq, cq, msem):
+def last_body(nh, nb, hl, io, dpart, gq_ref, gma_ref, gmb_ref, dn_ref, quarters, gma_all, gmb_all, nearq, sumq, farq, totq, sentz, gotz, zsem, pq, fq, cq, msem):
     pc = Place(nh, nb, hl)
     h, b = pc.h, pc.b
-    signal_all(nh, nb, h, b)
-    wait_all(nh, nb)
+    signal_near(pc)
+    wait_near(pc)
     nx, nz, qs = nh // 2, pc.nz, pc.qs
     def pair_q(k):
         return remote(
@@ -1623,8 +1723,10 @@
             totq.at[to], quarters.at[pc.zi], cq.at[0, i], cq.at[1, i], h, to * qs + pc.s
         )
 
+    io.need(1)
     for k in range(nx):
         pair_q(k).start()
+    io.need(0)
     line.lead(0)
     moves = []
     for n, (ref, dst) in enumerate(((gma_ref, gma_all), (gmb_ref, gmb_all))):
@@ -1661,9 +1763,11 @@
         if j + 1 < nz - 1:
             line.lead(j + 1)
     line.total(dn_ref)
+    io.put(0)
     line.finish()
     for i in range(1, nz):
         quarter(i).wait()
+    io.put(1)
     for cp in moves:
         cp.wait()
     for k in range(nx):
@@ -1708,6 +1812,8 @@
         ],
         (dpart, gq, gma, gmb),
         vmem=60 << 20,
+        late=(1, 0),
+        early=(0, 1),
     )
 
 
@@ -1793,19 +1899,19 @@
 
     gain_attn = ln_attn.reshape(1, own_rows)
     gain_mlp = ln_mlp.reshape(1, own_rows)
-    n1, wma, wmb, wq, gg, cos, sin = first_exchange(
+    n1, wma, wmb, wmc, wq, gg, cos, sin = first_exchange(
         lengths, layer_input, w_qkv, gain_attn, w_in, gain_mlp, w_mlp_out.T, out_grad, hl, fl
     )
     wma = lax.all_gather(wma, "blk", axis=1, tiled=True).reshape(width, -1)
     wq = wq.reshape(width, 3 * lw)
     n1 = n1.reshape(group, width)
-    qin, kvin, wo = to_heads(n1, wq, cos, sin, w_attn_out[None], hl)
+    qin, kvin, wo, wmb = to_heads(n1, wq, cos, sin, w_attn_out[None], wmb, hl)
     wo = wo.reshape(nz * DH, width)
     kv_all = kvin.reshape(slots, 2 * DH)
-    ot, of, lse = attend(lengths, qin, kv_all, 2 * rows, hl)
-    og, hid, n2, wmb = mid_exchange(ot, wo, layer_input, wmb, hl)
-    wmb = wmb.reshape(width, -1)
-    ypart, dpart, gma, gmb = ffn(lengths, n2, gg, wma, wmb, fl, own_rows, GRAD_CUT)
+    ot, of, lse = attend(lengths, qin, kv_all, 4 * rows, 1024, hl)
+    og, hid, n2, wmc = mid_exchange(ot, wo, layer_input, wmc, hl)
+    weights = [w.reshape(width, -1) for w in (wma, wmb, wmc)]
+    ypart, dpart, gma, gmb = ffn(lengths, n2, gg, weights, fl, own_rows, GRAD_CUT)
     if gma.ndim == 4:
         gma = lax.psum_scatter(gma, "blk", scatter_dimension=0, tiled=True)
         gmb = gmb.reshape((nz, qs) + gmb.shape[1:])
@@ -1817,7 +1923,7 @@
     y_out, dh, do_in, go, gmb = back_exchange(
         lengths, dpart, ypart, hid, out_grad, wo, og, gmb
     )
-    dq, dkv = attend_grad(lengths, qin, do_in, of, kv_all, lse, hl)
+    dq, dkv = attend_grad(lengths, qin, do_in, of, kv_all, lse, 2 * rows, 1024, hl)
     go = go.reshape(nz, qs, own_rows, width)
     gq, dpart1, d_wout, gmb = grads_back(
         dq, dkv.reshape(kvin.shape), cos, sin, n1, wq, go, gmb, hl

time: 289 us -> 266 us (0.920); the launches traced: 285 us -> 265 us
  Pallas kernels: 271 us -> 234 us
  waiting for transfers between devices: 0.08 us -> 16.5 us
    pallas_call x8, Pallas kernels: 250 us -> 214 us  [the longest x6 191 us: comm_call(): pl.pallas_call(staged_body, out_shape=out_shape, in_specs=in_specs, out_s...]
    reduce_scatter x1, waiting for transfers between devices: 0.02 us -> 16.4 us  [shards(): gma = lax.psum_scatter(gma, 'blk', scatter_dimension=0, tiled=True)]
  transfers between devices with their start and end apart: 2 -> 2, of which waited for: 0 -> 1; matrix products, arithmetic and copies ran while one was open for 0% -> 0% of each run, Pallas kernels for 64% -> 57%
where the time goes in v4:
time: 266 us; the launch traced here: 265 us
  Pallas kernels  234 us (88%)
  waiting for transfers between devices  16.5 us (6%)
  between operations  14.1 us (5%)
    pallas_call x6, Pallas kernels, comm_call(): pl.pallas_call(staged_body, out_shape=out_shape, in_specs=in_specs, out_s...  191 us
    reduce_scatter x1, waiting for transfers between devices, shards(): gma = lax.psum_scatter(gma, 'blk', scatter_dimension=0, tiled=True)  16.4 us
    pallas_call x1, Pallas kernels, ffn(): pl.pallas_call(functools.partial(ffn_body, nh, nb, fl, split_rows, cut),...  14.8 us
    pallas_call x1, Pallas kernels, attend_grad(): pl.pallas_call(functools.partial(attend_grad_body, nh, nb, hl, size), gri...  13.5 us
    pallas_call x1, Pallas kernels, attend(): pl.pallas_call(functools.partial(attend_body, nh, nb, hl, size), grid_spe...  9.28 us
    pallas_call x1, Pallas kernels, finish(): pl.pallas_call(functools.partial(finish_body, nh, fl), out_shape=(f32(row...  5.81 us
  transfers between devices with their start and end apart: 2, of which 1 were waited for; matrix products, arithmetic and copies ran while one was open for 0% of the time, Pallas kernels for 57%

profile of v4, /device:TPU:0, one launch (start us, length us, event | category | flops | bytes accessed | tf_op | source)
XLA Modules:
  0.0 265.3 jit_solution(93882627486324334)
XLA Ops:
  7.2 0.0 all-gather.2.cloned.1.call-start
  7.2 34.4 %first_exchange.1 = (bf16[4,128,1024]{2,1,0:T(8,128)(2,1)}, bf16[4,32,768]{2,1,0:T(8,128)(2,1)}, bf16[4,32,256]{2,1,0:T(8,128)(2,1)}, bf16[4,32,1024]{2,1,0:T(8,...) custom-call(s32[4]{0:T(128)} %len_ref.5, ...), custom_call_target="tpu_custom_call" | custom-call | tf_op jit(solution)/shard_map/first_exchange/pallas_call | solution.py:76
  41.7 0.0 all-gather.2.cloned.1.call-update
  41.7 0.2 reduce-scatter.2.cloned.1.call-start
  41.9 27.2 %to_heads.1 = (bf16[4,64,512]{2,1,0:T(8,128)(2,1)}, bf16[4,4,2,128,128]{4,3,2,1,0:T(8,128)(2,1)}, bf16[1,4,2,32,1024]{4,3,2,1,0:T(8,128)(2,1)}, bf16[4,4,2,32,256]{4,3,2,1,0:T(8,128)(2,1)}) custom-call(bf16[512,1024]{1,0:T(8,128)(2,1)} %bitcast.24, bf16[1024,768]{1,0:T(8,128)(2,1)} %bitcast.20, f32[512,128]{1,0:T(8,128)} %get-tuple-element.56.refs_2_, ...), custom_call_target="tpu_custom_call" | custom-call | tf_op jit(solution)/shard_map/to_heads/pallas_call | solution.py:76
  69.1 9.3 %attend.1 = (bf16[4,64,512]{2,1,0:T(8,128)(2,1)}, f32[4,64,512]{2,1,0:T(8,128)}, f32[4,1,512]{2,1,0:T(1,128)}) custom-call(s32[4]{0:T(128)} %len_ref.5, bf16[4,64,512]{2,1,0:T(8,128)(2,1)} %get-tuple-element.59.q_ref, bf16[4096,128]{1,0:T(8,128)(2,1)} %bitcast.22), custom_call_target="tpu_custom_call" | custom-call | tf_op jit(solution)/shard_map/attend/pallas_call | solution.py:977
  78.4 41.3 %mid_exchange.1 = (bf16[4,4,64,128]{3,2,1,0:T(8,128)(2,1)}, f32[128,1024]{1,0:T(8,128)}, bf16[4,128,1024]{2,1,0:T(8,128)(2,1)}, bf16[4,4,2,32,1024]{4,3,2,1,0:T(8,128)(2,1)}) custom-call(bf16[4,64,512]{2,1,0:T(8,128)(2,1)} %get-tuple-element.61.refs_0_, bf16[256,1024]{1,0:T(8,128)(2,1)} %bitcast.27, bf16[128,1024]{1,0:T(8,128)(2,1)} %x_ref.1, ...), custom_call_target="tpu_custom_call" | custom-call | tf_op jit(solution)/shard_map/mid_exchange/pallas_call | solution.py:76
  119.7 0.0 all-gather.2.cloned.1.call-done
  119.8 14.8 %ffn.1 = (bf16[4,128,1024]{2,1,0:T(8,128)(2,1)}, bf16[4,128,1024]{2,1,0:T(8,128)(2,1)}, bf16[8,4,32,1536]{3,2,1,0:T(8,128)(2,1)}, bf16[8,4,32,512]{3,2,1,0:T(8,128)(2,1)}) custom-call(s32[4]{0:T(128)} %len_ref.5, bf16[4,128,1024]{2,1,0:T(8,128)(2,1)} %get-tuple-element.64.n_hbm, bf16[4,128,1024]{2,1,0:T(8,128)(2,1)} %get-tuple-element.65.g_hbm, ...), custom_call_target="tpu_custom_call" | custom-call | tf_op jit(solution)/shard_map/ffn/pallas_call | solution.py:1358
  134.6 0.0 reduce-scatter.2.cloned.1.call-update
  134.6 31.9 %back_exchange.1 = (f32[128,1024]{1,0:T(8,128)}, f32[128,1024]{1,0:T(8,128)}, bf16[4,64,512]{2,1,0:T(8,128)(2,1)}, bf16[256,1024]{1,0:T(8,128)(2,1)}, bf16[4,4,32,512]{3,2,1,0:T(8,128)(2,1)}) custom-call(s32[4]{0:T(128)} %len_ref.5, bf16[4,128,1024]{2,1,0:T(8,128)(2,1)} %get-tuple-element.69.refs_1_, bf16[4,128,1024]{2,1,0:T(8,128)(2,1)} %get-tuple-element.70.refs_2_, ...), custom_call_target="tpu_custom_call" | custom-call | tf_op jit(solution)/shard_map/back_exchange/pallas_call | solution.py:76
  166.5 13.5 %attend_grad.1 = (bf16[4,64,512]{2,1,0:T(8,128)(2,1)}, bf16[4096,128]{1,0:T(8,128)(2,1)}) custom-call(s32[4]{0:T(128)} %len_ref.5, bf16[4,64,512]{2,1,0:T(8,128)(2,1)} %get-tuple-element.59.q_ref, bf16[4,64,512]{2,1,0:T(8,128)(2,1)} %get-tuple-element.74.do_ref, f32[4,64,512]{2,1,0:T(8,128)} %get-tuple-element.75.of_ref, bf16[4096,128]{1,0:T(8,128)(2,1)} %bitcast.23, ...), custom_call_target="tpu_custom_call" | custom-call | tf_op jit(solution)/shard_map/attend_grad/pallas_call | solution.py:1047
  180.0 28.9 %grads_back.1 = (bf16[1024,768]{1,0:T(8,128)(2,1)}, bf16[4,128,1024]{2,1,0:T(8,128)(2,1)}, f32[32,1024]{1,0:T(8,128)}, bf16[4,32,512]{2,1,0:T(8,128)(2,1)}) custom-call(bf16[4,64,512]{2,1,0:T(8,128)(2,1)} %get-tuple-element.77.refs_0_, bf16[4,4,2,128,128]{4,3,2,1,0:T(8,128)(2,1)} %bitcast.32, f32[512,128]{1,0:T(8,128)} %get-tuple-element.56.refs_2_, ...), custom_call_target="tpu_custom_call" | custom-call | tf_op jit(solution)/shard_map/grads_back/pallas_call | solution.py:76
  208.9 16.4 %reduce-scatter.2.cloned.1.call-done = bf16[1,4,32,1536]{3,2,1,0:T(8,128)(2,1)} async-done(((bf16[8,4,32,1536]{3,2,1,0:T(8,128)(2,1)}), bf16[1,4,32,1536]{3,2,1,0:T(8,128)(2,1)}) %reduce-scatter.2.cloned.1.call-update) | async-done | bytes 393232 | tf_op jit(solution)/shard_map/reduce_scatter | solution.py:1916
  225.3 27.3 %last_exchange.1 = (f32[128,1024]{1,0:T(8,128)}, bf16[4,32,768]{2,1,0:T(8,128)(2,1)}, bf16[4,32,1536]{2,1,0:T(8,128)(2,1)}, bf16[4,32,512]{2,1,0:T(8,128)(2,1)}) custom-call(bf16[4,128,1024]{2,1,0:T(8,128)(2,1)} %get-tuple-element.81.refs_0_, bf16[4,4,2,32,768]{4,3,2,1,0:T(8,128)(2,1)} %bitcast.29, bf16[4,32,1536]{2,1,0:T(8,128)(2,1)} %bitcast.35, ...), custom_call_target="tpu_custom_call" | custom-call | tf_op jit(solution)/shard_map/last_exchange/pallas_call | solution.py:76
  252.6 5.8 %finish.1 = (f32[128,1024]{1,0:T(8,128)}, f32[128,1024]{1,0:T(8,128)}, f32[1,32]{1,0:T(1,128)}, f32[32,3072]{1,0:T(8,128)}, f32[32,1024]{1,0:T(8,128)}, /*index=...) custom-call(f32[128,1024]{1,0:T(8,128)} %get-tuple-element.85.dn_ref, bf16[128,1024]{1,0:T(8,128)(2,1)} %x_ref.1, ...), custom_call_target="tpu_custom_call" | custom-call | tf_op jit(solution)/shard_map/finish/pallas_call | solution.py:1867
Async XLA Ops:
  7.2 112.6 %all-gather.2.cloned.1.call-start = ((), (), s32[]{:S(2)}) async-start(), calls=%async_computation.1 | async-start | bytes 1769472 | tf_op jit(solution)/shard_map/all_gather | solution.py:1905
  41.7 183.6 %reduce-scatter.2.cloned.1.call-start = ((), (), s32[]{:S(2)}) async-start(), calls=%async_computation.2 | async-start | bytes 3538944 | tf_op jit(solution)/shard_map/reduce_scatter | solution.py:1916
Sparse Core Ops, SparseCore 0:
  41.8 51.3 all-gather.1
  134.7 90.5 reduce-scatter.1

commit v5 on v4

--- a/solution.py
+++ b/solution.py
@@ -12,9 +12,9 @@
 ROPE_BASE = 160000.0
 NORM_EPS = 1e-05
 MASK_FLOOR = -1e30
-GRAD_CUT = 1536
+GRAD_CUT = 1280
 FF_BLOCKS = 2
-WEIGHT_CUTS = (768, 1024)
+WEIGHT_CUTS = (1280, 1408)
 EXP_SCALE = 0.125 * math.log2(math.e)
 BF16 = jnp.bfloat16
 F32 = jnp.float32
@@ -772,7 +772,7 @@
     return tile * cos + halves_swapped(tile) * sin
 
 
-def to_heads_body(nh, nb, hl, io, n1_hbm, w_hbm, cos_ref, sin_ref, wo_ref, wmb_ref, qin, kvin, wo_all, wmb_all, qbuf, kvbuf, n1_ref, w_ref, qsem, ksem, fsem, osem, osem2, bsem, bsem2, stage):
+def to_heads_body(nh, nb, hl, io, n1_hbm, w_hbm, cos_ref, sin_ref, wo_ref, wmb_ref, wmc_ref, qin, kvin, wo_all, wmb_all, wmc_line, qbuf, kvbuf, n1_ref, w_ref, qsem, ksem, fsem, osem, osem2, bsem, bsem2, csem, stage):
     pc = Place(nh, nb, hl)
     loads = [
         pltpu.make_async_copy(n1_hbm, n1_ref, stage.at[0]),
@@ -825,9 +825,11 @@
 
     spread = BlkGather(pc, wo_ref, wo_all, osem, osem2)
     spread_b = BlkGather(pc, wmb_ref, wmb_all, bsem, bsem2)
+    line_c = LineGather(pc, wmc_ref, lambda zi: wmc_line.at[:, zi], csem)
     keys_out("start")
     spread.start()
     spread_b.start()
+    line_c.start()
     qq = jnp.dot(n1, w_ref[:, :lw], preferred_element_type=F32)
     for p in range(nh // 2):
         q = turned(qq[:, p * 128 : (p + 1) * 128], cos, sin).T.astype(BF16)
@@ -848,6 +850,7 @@
     for t in range(1, pc.nz):
         spread.step(t)
         spread_b.step(t)
+        line_c.step(t)
     keys_out("wait_send")
     queries_out("wait_send")
     for i in range(nh):
@@ -859,9 +862,10 @@
 
     spread.finish()
     spread_b.finish()
-
-
-def to_heads(n1, wq, cos, sin, wo, wmb, hl):
+    line_c.finish()
+
+
+def to_heads(n1, wq, cos, sin, wo, wmb, wmc, hl):
     nh, nb = dims()
     group, width = n1.shape
     nz, qs = hl, nb // hl
@@ -877,9 +881,10 @@
             jax.ShapeDtypeStruct((nh, nz, qs, rows, 2 * DH), BF16),
             jax.ShapeDtypeStruct((1, nz, qs) + wo.shape[1:], BF16),
             jax.ShapeDtypeStruct((nh, nz, qs) + wmb.shape[1:], BF16),
+            jax.ShapeDtypeStruct((nh, nz) + wmc.shape[1:], BF16),
         ),
-        [ANY, ANY, VM, VM, ANY, ANY],
-        [ANY] * 4,
+        [ANY, ANY, VM, VM, ANY, ANY, ANY],
+        [ANY] * 5,
         [
             pltpu.VMEM((nh, DH, group), BF16),
             pltpu.VMEM((nh, nz, rows, 2 * DH), BF16),
@@ -890,8 +895,8 @@
             dma((2, nh * cb)),
         ]
         + BlkGather.sem_shapes(nz, qs) * 2
-        + [dma((2,))],
-        (n1, wq, cos, sin, wo, wmb),
+        + [LineGather.sem_shape(nz), dma((2,))],
+        (n1, wq, cos, sin, wo, wmb, wmc),
         vmem=60 << 20,
         late=(2, 3),
     )
@@ -1171,14 +1176,26 @@
     return pltpu.SemaphoreType.DMA((CHUNKS, 4, nh // 2))
 
 
-def mid_body(nh, nb, hl, io, o_ref, wo_ref, x_ref, wmb_ref, og, hid_ref, ng_ref, wmb_all, part, near, far, out, nbuf, osem, ssem, gsem, wsem, wsem2):
+def mid_body(nh, nb, hl, io, o_ref, wo_ref, x_ref, wmb_ref, og, hid_ref, ng_ref, wmb_all, part, near, far, out, nbuf, osem, ssem, gsem, wsem):
     pc = Place(nh, nb, hl)
     h, b = pc.h, pc.b
     enter_with(pc, lambda zi: pc.attends(zi, h, pc.s % 2, pc.s // 2))
     rows, width = x_ref.shape
     outputs_back(pc, o_ref, og, osem, "start")
-    spread = BlkGather(pc, wmb_ref, wmb_all, wsem, wsem2)
-    spread.start()
+    sides = [
+        remote(
+            wmb_ref,
+            wmb_all.at[:, :, pc.s],
+            wsem.at[0, ds],
+            wsem.at[1, ds],
+            h,
+            pc.zi * pc.qs + (pc.s + ds) % pc.qs,
+        )
+        for ds in range(1, pc.qs)
+    ]
+    sides.append(pltpu.make_async_copy(wmb_ref, wmb_all.at[:, :, pc.s], wsem.at[0, 0]))
+    for cp in sides:
+        cp.start()
     outputs_back(pc, o_ref, og, osem, "wait_send")
     for zi in range(pc.nz):
         wait_on(og.at[zi], osem.at[1, zi])
@@ -1196,7 +1213,6 @@
     hgs = head_gathers(nh, h, b, nbuf, ng_ref, gsem)
     for hs in hss:
         hs.start()
-    spread.step(1)
     for hs in hss:
         hs.send()
     size = rows // CHUNKS
@@ -1208,15 +1224,13 @@
         nbuf[at, :] = norm_of(hid)[0].astype(BF16)
         hg.start()
     io.put(1)
-    spread.step(2)
     for hg in hgs:
         hg.pass_on()
-    for t in range(3, pc.nz):
-        spread.step(t)
     for hs, hg in zip(hss, hgs):
         hs.finish()
         hg.finish()
-    spread.finish()
+    for cp in sides:
+        cp.wait()
 
 
 def mid_exchange(ot, wo, x, wmb, hl):
@@ -1231,7 +1245,7 @@
             jax.ShapeDtypeStruct((nz, nh, DH, rows), BF16),
             jax.ShapeDtypeStruct(x.shape, F32),
             jax.ShapeDtypeStruct((nh, rows, width), BF16),
-            jax.ShapeDtypeStruct((nh, nz, nb // nz) + wmb.shape[1:], BF16),
+            jax.ShapeDtypeStruct((nh, nz, nb // nz) + wmb.shape[2:], BF16),
         ),
         [ANY] * 4,
         [ANY] * 4,
@@ -1242,8 +1256,8 @@
             pltpu.SemaphoreType.DMA((2, nz)),
             chunk_sems(nh),
             chunk_sems(nh),
-        ]
-        + BlkGather.sem_shapes(nz, nb // nz),
+            pltpu.SemaphoreType.DMA((2, nb // nz)),
+        ],
         (ot, wo, x, wmb),
         vmem=60 << 20,
         late=(1, 2),
@@ -1905,7 +1919,7 @@
     wma = lax.all_gather(wma, "blk", axis=1, tiled=True).reshape(width, -1)
     wq = wq.reshape(width, 3 * lw)
     n1 = n1.reshape(group, width)
-    qin, kvin, wo, wmb = to_heads(n1, wq, cos, sin, w_attn_out[None], wmb, hl)
+    qin, kvin, wo, wmb, wmc = to_heads(n1, wq, cos, sin, w_attn_out[None], wmb, wmc, hl)
     wo = wo.reshape(nz * DH, width)
     kv_all = kvin.reshape(slots, 2 * DH)
     ot, of, lse = attend(lengths, qin, kv_all, 4 * rows, 1024, hl)

time: 266 us -> 256 us (0.962)
  waiting for transfers between devices: 16.5 us -> 5.88 us
    reduce_scatter x1, waiting for transfers between devices: 16.4 us -> 5.83 us  [shards(): gma = lax.psum_scatter(gma, 'blk', scatter_dimension=0, tiled=True)]
  transfers between devices with their start and end apart: 2 -> 2, of which waited for: 1 -> 1; matrix products, arithmetic and copies ran while one was open for 0% -> 0% of each run, Pallas kernels for 57% -> 60%
where the time goes in v5:
time: 256 us; the launch traced here: 255 us
  Pallas kernels  235 us (92%)
  between operations  14.1 us (6%)
  waiting for transfers between devices  5.88 us (2%)
    pallas_call x6, Pallas kernels, comm_call(): pl.pallas_call(staged_body, out_shape=out_shape, in_specs=in_specs, out_s...  192 us
    pallas_call x1, Pallas kernels, ffn(): pl.pallas_call(functools.partial(ffn_body, nh, nb, fl, split_rows, cut),...  14.6 us
    pallas_call x1, Pallas kernels, attend_grad(): pl.pallas_call(functools.partial(attend_grad_body, nh, nb, hl, size), gri...  13.5 us
    pallas_call x1, Pallas kernels, attend(): pl.pallas_call(functools.partial(attend_body, nh, nb, hl, size), grid_spe...  9.27 us
    reduce_scatter x1, waiting for transfers between devices, shards(): gma = lax.psum_scatter(gma, 'blk', scatter_dimension=0, tiled=True)  5.83 us
    pallas_call x1, Pallas kernels, finish(): pl.pallas_call(functools.partial(finish_body, nh, fl), out_shape=(f32(row...  5.8 us
  transfers between devices with their start and end apart: 2, of which 1 were waited for; matrix products, arithmetic and copies ran while one was open for 0% of the time, Pallas kernels for 60%

profile of v5, /device:TPU:0, one launch (start us, length us, event | category | flops | bytes accessed | tf_op | source)
XLA Modules:
  0.0 255.2 jit_solution(3248641264593355144)
XLA Ops:
  7.2 0.0 all-gather.2.cloned.1.call-start
  7.2 34.4 %first_exchange.1 = (bf16[4,128,1024]{2,1,0:T(8,128)(2,1)}, bf16[4,32,1280]{2,1,0:T(8,128)(2,1)}, bf16[4,32,128]{2,1,0:T(8,128)(2,1)}, bf16[4,32,640]{2,1,0:T(8,...) custom-call(s32[4]{0:T(128)} %len_ref.5, ...), custom_call_target="tpu_custom_call" | custom-call | tf_op jit(solution)/shard_map/first_exchange/pallas_call | solution.py:76
  41.7 0.0 all-gather.2.cloned.1.call-update
  41.7 0.2 reduce-scatter.2.cloned.1.call-start
  41.9 32.8 %to_heads.1 = (bf16[4,64,512]{2,1,0:T(8,128)(2,1)}, bf16[4,4,2,128,128]{4,3,2,1,0:T(8,128)(2,1)}, bf16[1,4,2,32,1024]{4,3,2,1,0:T(8,128)(2,1)}, bf16[4,4,2,32,12...) custom-call(bf16[512,1024]{1,0:T(8,128)(2,1)} %bitcast.24, bf16[1024,768]{1,0:T(8,128)(2,1)} %bitcast.20, ...), custom_call_target="tpu_custom_call" | custom-call | tf_op jit(solution)/shard_map/to_heads/pallas_call | solution.py:76
  74.7 9.3 %attend.1 = (bf16[4,64,512]{2,1,0:T(8,128)(2,1)}, f32[4,64,512]{2,1,0:T(8,128)}, f32[4,1,512]{2,1,0:T(1,128)}) custom-call(s32[4]{0:T(128)} %len_ref.5, bf16[4,64,512]{2,1,0:T(8,128)(2,1)} %get-tuple-element.61.q_ref, bf16[4096,128]{1,0:T(8,128)(2,1)} %bitcast.22), custom_call_target="tpu_custom_call" | custom-call | tf_op jit(solution)/shard_map/attend/pallas_call | solution.py:982
  84.0 28.0 %mid_exchange.1 = (bf16[4,4,64,128]{3,2,1,0:T(8,128)(2,1)}, f32[128,1024]{1,0:T(8,128)}, bf16[4,128,1024]{2,1,0:T(8,128)(2,1)}, bf16[4,4,2,32,640]{4,3,2,1,0:T(8,128)(2,1)}) custom-call(bf16[4,64,512]{2,1,0:T(8,128)(2,1)} %get-tuple-element.63.refs_0_, bf16[256,1024]{1,0:T(8,128)(2,1)} %bitcast.27, bf16[128,1024]{1,0:T(8,128)(2,1)} %x_ref.1, ...), custom_call_target="tpu_custom_call" | custom-call | tf_op jit(solution)/shard_map/mid_exchange/pallas_call | solution.py:76
  112.0 0.0 all-gather.2.cloned.1.call-done
  112.0 14.6 %ffn.1 = (bf16[4,128,1024]{2,1,0:T(8,128)(2,1)}, bf16[4,128,1024]{2,1,0:T(8,128)(2,1)}, bf16[8,4,32,1280]{3,2,1,0:T(8,128)(2,1)}, bf16[8,4,32,768]{3,2,1,0:T(8,128)(2,1)}) custom-call(s32[4]{0:T(128)} %len_ref.5, bf16[4,128,1024]{2,1,0:T(8,128)(2,1)} %get-tuple-element.66.n_hbm, bf16[4,128,1024]{2,1,0:T(8,128)(2,1)} %get-tuple-element.67.g_hbm, ...), custom_call_target="tpu_custom_call" | custom-call | tf_op jit(solution)/shard_map/ffn/pallas_call | solution.py:1372
  126.6 0.0 reduce-scatter.2.cloned.1.call-update
  126.7 35.8 %back_exchange.1 = (f32[128,1024]{1,0:T(8,128)}, f32[128,1024]{1,0:T(8,128)}, bf16[4,64,512]{2,1,0:T(8,128)(2,1)}, bf16[256,1024]{1,0:T(8,128)(2,1)}, bf16[4,4,32,768]{3,2,1,0:T(8,128)(2,1)}) custom-call(s32[4]{0:T(128)} %len_ref.5, bf16[4,128,1024]{2,1,0:T(8,128)(2,1)} %get-tuple-element.71.refs_1_, bf16[4,128,1024]{2,1,0:T(8,128)(2,1)} %get-tuple-element.72.refs_2_, ...), custom_call_target="tpu_custom_call" | custom-call | tf_op jit(solution)/shard_map/back_exchange/pallas_call | solution.py:76
  162.5 13.5 %attend_grad.1 = (bf16[4,64,512]{2,1,0:T(8,128)(2,1)}, bf16[4096,128]{1,0:T(8,128)(2,1)}) custom-call(s32[4]{0:T(128)} %len_ref.5, bf16[4,64,512]{2,1,0:T(8,128)(2,1)} %get-tuple-element.61.q_ref, bf16[4,64,512]{2,1,0:T(8,128)(2,1)} %get-tuple-element.76.do_ref, f32[4,64,512]{2,1,0:T(8,128)} %get-tuple-element.77.of_ref, bf16[4096,128]{1,0:T(8,128)(2,1)} %bitcast.23, ...), custom_call_target="tpu_custom_call" | custom-call | tf_op jit(solution)/shard_map/attend_grad/pallas_call | solution.py:1052
  176.0 32.8 %grads_back.1 = (bf16[1024,768]{1,0:T(8,128)(2,1)}, bf16[4,128,1024]{2,1,0:T(8,128)(2,1)}, f32[32,1024]{1,0:T(8,128)}, bf16[4,32,768]{2,1,0:T(8,128)(2,1)}) custom-call(bf16[4,64,512]{2,1,0:T(8,128)(2,1)} %get-tuple-element.79.refs_0_, bf16[4,4,2,128,128]{4,3,2,1,0:T(8,128)(2,1)} %bitcast.32, f32[512,128]{1,0:T(8,128)} %get-tuple-element.57.refs_2_, ...), custom_call_target="tpu_custom_call" | custom-call | tf_op jit(solution)/shard_map/grads_back/pallas_call | solution.py:76
  208.8 5.8 %reduce-scatter.2.cloned.1.call-done = bf16[1,4,32,1280]{3,2,1,0:T(8,128)(2,1)} async-done(((bf16[8,4,32,1280]{3,2,1,0:T(8,128)(2,1)}), bf16[1,4,32,1280]{3,2,1,0:T(8,128)(2,1)}) %reduce-scatter.2.cloned.1.call-update) | async-done | bytes 327696 | tf_op jit(solution)/shard_map/reduce_scatter | solution.py:1930
  214.6 28.0 %last_exchange.1 = (f32[128,1024]{1,0:T(8,128)}, bf16[4,32,768]{2,1,0:T(8,128)(2,1)}, bf16[4,32,1280]{2,1,0:T(8,128)(2,1)}, bf16[4,32,768]{2,1,0:T(8,128)(2,1)}) custom-call(bf16[4,128,1024]{2,1,0:T(8,128)(2,1)} %get-tuple-element.83.refs_0_, bf16[4,4,2,32,768]{4,3,2,1,0:T(8,128)(2,1)} %bitcast.29, bf16[4,32,1280]{2,1,0:T(8,128)(2,1)} %bitcast.34, ...), custom_call_target="tpu_custom_call" | custom-call | tf_op jit(solution)/shard_map/last_exchange/pallas_call | solution.py:76
  242.6 5.8 %finish.1 = (f32[128,1024]{1,0:T(8,128)}, f32[128,1024]{1,0:T(8,128)}, f32[1,32]{1,0:T(1,128)}, f32[32,3072]{1,0:T(8,128)}, f32[32,1024]{1,0:T(8,128)}, /*index=...) custom-call(f32[128,1024]{1,0:T(8,128)} %get-tuple-element.87.dn_ref, bf16[128,1024]{1,0:T(8,128)(2,1)} %x_ref.1, ...), custom_call_target="tpu_custom_call" | custom-call | tf_op jit(solution)/shard_map/finish/pallas_call | solution.py:1881
Async XLA Ops:
  7.2 104.8 %all-gather.2.cloned.1.call-start = ((), (), s32[]{:S(2)}) async-start(), calls=%async_computation.1 | async-start | bytes 2949120 | tf_op jit(solution)/shard_map/all_gather | solution.py:1919
  41.7 172.9 %reduce-scatter.2.cloned.1.call-start = ((), (), s32[]{:S(2)}) async-start(), calls=%async_computation.2 | async-start | bytes 2949120 | tf_op jit(solution)/shard_map/reduce_scatter | solution.py:1930
Sparse Core Ops, SparseCore 0:
  41.8 64.1 all-gather.1
  126.8 87.7 reduce-scatter.1

commit v6 on v5

--- a/solution.py
+++ b/solution.py
@@ -1707,7 +1707,7 @@
     )
 
 
-def last_body(nh, nb, hl, io, dpart, gq_ref, gma_ref, gmb_ref, dn_ref, quarters, gma_all, gmb_all, nearq, sumq, farq, totq, sentz, gotz, zsem, pq, fq, cq, msem):
+def last_body(nh, nb, hl, io, dpart, gq_ref, gma_ref, gmb_ref, dn_ref, quarters, gma_all, gmb_all, nearq, sumq, farq, totq, sentz, gotz, zsem, pq, fq, cq, msem, asem):
     pc = Place(nh, nb, hl)
     h, b = pc.h, pc.b
     signal_near(pc)
@@ -1742,12 +1742,33 @@
         pair_q(k).start()
     io.need(0)
     line.lead(0)
-    moves = []
-    for n, (ref, dst) in enumerate(((gma_ref, gma_all), (gmb_ref, gmb_all))):
-        for i in range(1, nh):
-            th = (h + i) % nh
-            moves.append(remote(ref.at[th], dst.at[h], msem.at[0, n, i], msem.at[1, n, i], th, b))
-        moves.append(pltpu.make_async_copy(ref.at[h], dst.at[h], msem.at[0, n, 0]))
+    moves = [
+        remote(
+            gmb_ref.at[(h + i) % nh],
+            gmb_all.at[h],
+            msem.at[0, i],
+            msem.at[1, i],
+            (h + i) % nh,
+            b,
+        )
+        for i in range(1, nh)
+    ]
+    moves.append(pltpu.make_async_copy(gmb_ref.at[h], gmb_all.at[h], msem.at[0, 0]))
+    moves.append(
+        pltpu.make_async_copy(gma_ref.at[pc.s, h], gma_all.at[pc.s, h], asem.at[0, 0])
+    )
+
+    def plane_move(i):
+        th, ts = (h + i // qs) % nh, (pc.s + i % qs) % qs
+        return remote(
+            gma_ref.at[ts, th],
+            gma_all.at[pc.s, h],
+            asem.at[0, i],
+            asem.at[1, i],
+            th,
+            pc.zi * qs + ts,
+        )
+
     for k in range(nx):
         pair_q(k).wait_recv()
         sumq[k] = (gq_ref[2 * k + pc.c].astype(F32) + nearq[k].astype(F32)).astype(BF16)
@@ -1759,6 +1780,11 @@
     farq[pc.x, pc.s] = sumq[pc.x, :, pc.s]
     for cp in moves:
         cp.start()
+
+    @pl.loop(1, nh * qs)
+    def _(i):
+        plane_move(i).start()
+
     line.follow(0)
     line.lead(1)
 
@@ -1784,6 +1810,11 @@
     io.put(1)
     for cp in moves:
         cp.wait()
+
+    @pl.loop(1, nh * qs)
+    def _(i):
+        plane_move(i).wait()
+
     for k in range(nx):
         pair_q(k).wait_send()
 
@@ -1822,7 +1853,8 @@
             dma((2, nx)),
             dma((2, nx * qs)),
             dma((2, nz)),
-            dma((2, 2, nh)),
+            dma((2, nh)),
+            dma((2, nh * qs)),
         ],
         (dpart, gq, gma, gmb),
         vmem=60 << 20,
@@ -1858,7 +1890,8 @@
     tiles = lambda v: (v + 127) // 128 * 128
     gate_up, down = 0.0, 0.0
     for i in range(nh):
-        piece = jnp.concatenate([gma[i].astype(F32), gmb[i].astype(F32)], axis=1)
+        first = jnp.sum(gma[:, i].astype(F32), axis=0)
+        piece = jnp.concatenate([first, gmb[i].astype(F32)], axis=1)
         lane = lanes_of(piece)
         gate = widen(jnp.where(lane < fl, piece, 0.0), tiles(2 * ff))
         up = jnp.where(jnp.logical_and(lane >= fl, lane < 2 * fl), piece, 0.0)
@@ -1926,14 +1959,18 @@
     og, hid, n2, wmc = mid_exchange(ot, wo, layer_input, wmc, hl)
     weights = [w.reshape(width, -1) for w in (wma, wmb, wmc)]
     ypart, dpart, gma, gmb = ffn(lengths, n2, gg, weights, fl, own_rows, GRAD_CUT)
-    if gma.ndim == 4:
-        gma = lax.psum_scatter(gma, "blk", scatter_dimension=0, tiled=True)
-        gmb = gmb.reshape((nz, qs) + gmb.shape[1:])
-    else:
-        gma = gma.reshape(nh, nb * own_rows, gma.shape[1])
-        gma = lax.psum_scatter(gma, "blk", scatter_dimension=1, tiled=True)
-        gmb = gmb.reshape(nh, nz, qs, own_rows, gmb.shape[1]).transpose(1, 2, 0, 3, 4)
-    gma = gma.reshape(nh, own_rows, gma.shape[-1])
+    by_owner = []
+    for gm in (gma, gmb):
+        if gm.ndim == 4:
+            gm = gm.reshape((nz, qs) + gm.shape[1:])
+        else:
+            gm = gm.reshape(nh, nz, qs, own_rows, gm.shape[1]).transpose(1, 2, 0, 3, 4)
+        by_owner.append(gm)
+    gma, gmb = by_owner
+    lines = [[zi * qs + s for zi in range(nz)] for s in range(qs)]
+    gma = lax.psum_scatter(
+        gma, "blk", scatter_dimension=0, tiled=True, axis_index_groups=lines
+    ).reshape(gma.shape[1:])
     y_out, dh, do_in, go, gmb = back_exchange(
         lengths, dpart, ypart, hid, out_grad, wo, og, gmb
     )

time: 256 us -> 258 us (level)
  Pallas kernels: 235 us -> 243 us
  waiting for transfers between devices: 5.88 us -> 0.08 us
    reduce_scatter x1, waiting for transfers between devices: 5.83 us -> 0.02 us  [shards(): lax.psum_scatter(gma, 'blk', scatter_dimension=0, tiled=True, axis_index_...]
    pallas_call x1, Pallas kernels: 13.5 us -> 19.1 us  [attend_grad(): pl.pallas_call(functools.partial(attend_grad_body, nh, nb, hl, size), gri...]
    pallas_call x1, Pallas kernels: 9.27 us -> 13.8 us  [attend(): pl.pallas_call(functools.partial(attend_body, nh, nb, hl, size), grid_spe...]
  transfers between devices with their start and end apart: 2 -> 2, of which waited for: 1 -> 0; matrix products, arithmetic and copies ran while one was open for 0% -> 0% of each run, Pallas kernels for 60% -> 62%
where the time goes in v6:
time: 258 us; the launch traced here: 257 us
  Pallas kernels  243 us (94%)
  between operations  14.1 us (5%)
    pallas_call x6, Pallas kernels, comm_call(): pl.pallas_call(staged_body, out_shape=out_shape, in_specs=in_specs, out_s...  189 us
    pallas_call x1, Pallas kernels, attend_grad(): pl.pallas_call(functools.partial(attend_grad_body, nh, nb, hl, size), gri...  19.1 us
    pallas_call x1, Pallas kernels, ffn(): pl.pallas_call(functools.partial(ffn_body, nh, nb, fl, split_rows, cut),...  14.6 us
    pallas_call x1, Pallas kernels, attend(): pl.pallas_call(functools.partial(attend_body, nh, nb, hl, size), grid_spe...  13.8 us
    pallas_call x1, Pallas kernels, finish(): pl.pallas_call(functools.partial(finish_body, nh, fl), out_shape=(f32(row...  5.96 us
  transfers between devices with their start and end apart: 2, of which 0 were waited for; matrix products, arithmetic and copies ran while one was open for 0% of the time, Pallas kernels for 62%

profile of v6, /device:TPU:0, one launch (start us, length us, event | category | flops | bytes accessed | tf_op | source)
XLA Modules:
  0.0 257.4 jit_solution(15322655446293340079)
XLA Ops:
  7.2 0.0 all-gather.2.cloned.1.call-start
  7.2 34.4 %first_exchange.1 = (bf16[4,128,1024]{2,1,0:T(8,128)(2,1)}, bf16[4,32,1280]{2,1,0:T(8,128)(2,1)}, bf16[4,32,128]{2,1,0:T(8,128)(2,1)}, bf16[4,32,640]{2,1,0:T(8,...) custom-call(s32[4]{0:T(128)} %len_ref.5, ...), custom_call_target="tpu_custom_call" | custom-call | tf_op jit(solution)/shard_map/first_exchange/pallas_call | solution.py:76
  41.7 0.0 all-gather.2.cloned.1.call-update
  41.7 0.2 reduce-scatter.2.cloned.1.call-start
  41.9 32.8 %to_heads.1 = (bf16[4,64,512]{2,1,0:T(8,128)(2,1)}, bf16[4,4,2,128,128]{4,3,2,1,0:T(8,128)(2,1)}, bf16[1,4,2,32,1024]{4,3,2,1,0:T(8,128)(2,1)}, bf16[4,4,2,32,12...) custom-call(bf16[512,1024]{1,0:T(8,128)(2,1)} %bitcast.25, bf16[1024,768]{1,0:T(8,128)(2,1)} %bitcast.21, ...), custom_call_target="tpu_custom_call" | custom-call | tf_op jit(solution)/shard_map/to_heads/pallas_call | solution.py:76
  74.7 13.8 %attend.1 = (bf16[4,64,512]{2,1,0:T(8,128)(2,1)}, f32[4,64,512]{2,1,0:T(8,128)}, f32[4,1,512]{2,1,0:T(1,128)}) custom-call(s32[4]{0:T(128)} %len_ref.5, bf16[4,64,512]{2,1,0:T(8,128)(2,1)} %get-tuple-element.61.q_ref, bf16[4096,128]{1,0:T(8,128)(2,1)} %bitcast.23), custom_call_target="tpu_custom_call" | custom-call | tf_op jit(solution)/shard_map/attend/pallas_call | solution.py:982
  88.5 28.3 %mid_exchange.1 = (bf16[4,4,64,128]{3,2,1,0:T(8,128)(2,1)}, f32[128,1024]{1,0:T(8,128)}, bf16[4,128,1024]{2,1,0:T(8,128)(2,1)}, bf16[4,4,2,32,640]{4,3,2,1,0:T(8,128)(2,1)}) custom-call(bf16[4,64,512]{2,1,0:T(8,128)(2,1)} %get-tuple-element.63.refs_0_, bf16[256,1024]{1,0:T(8,128)(2,1)} %bitcast.29, bf16[128,1024]{1,0:T(8,128)(2,1)} %x_ref.1, ...), custom_call_target="tpu_custom_call" | custom-call | tf_op jit(solution)/shard_map/mid_exchange/pallas_call | solution.py:76
  116.8 0.0 all-gather.2.cloned.1.call-done
  116.8 14.6 %ffn.1 = (bf16[4,128,1024]{2,1,0:T(8,128)(2,1)}, bf16[4,128,1024]{2,1,0:T(8,128)(2,1)}, bf16[8,4,32,1280]{3,2,1,0:T(8,128)(2,1)}, bf16[8,4,32,768]{3,2,1,0:T(8,128)(2,1)}) custom-call(s32[4]{0:T(128)} %len_ref.5, bf16[4,128,1024]{2,1,0:T(8,128)(2,1)} %get-tuple-element.66.n_hbm, bf16[4,128,1024]{2,1,0:T(8,128)(2,1)} %get-tuple-element.67.g_hbm, ...), custom_call_target="tpu_custom_call" | custom-call | tf_op jit(solution)/shard_map/ffn/pallas_call | solution.py:1372
  131.5 0.0 reduce-scatter.2.cloned.1.call-update
  131.5 33.7 %back_exchange.1 = (f32[128,1024]{1,0:T(8,128)}, f32[128,1024]{1,0:T(8,128)}, bf16[4,64,512]{2,1,0:T(8,128)(2,1)}, bf16[256,1024]{1,0:T(8,128)(2,1)}, bf16[4,4,32,768]{3,2,1,0:T(8,128)(2,1)}) custom-call(s32[4]{0:T(128)} %len_ref.5, bf16[4,128,1024]{2,1,0:T(8,128)(2,1)} %get-tuple-element.71.refs_1_, bf16[4,128,1024]{2,1,0:T(8,128)(2,1)} %get-tuple-element.72.refs_2_, ...), custom_call_target="tpu_custom_call" | custom-call | tf_op jit(solution)/shard_map/back_exchange/pallas_call | solution.py:76
  165.1 19.1 %attend_grad.1 = (bf16[4,64,512]{2,1,0:T(8,128)(2,1)}, bf16[4096,128]{1,0:T(8,128)(2,1)}) custom-call(s32[4]{0:T(128)} %len_ref.5, bf16[4,64,512]{2,1,0:T(8,128)(2,1)} %get-tuple-element.61.q_ref, bf16[4,64,512]{2,1,0:T(8,128)(2,1)} %get-tuple-element.76.do_ref, f32[4,64,512]{2,1,0:T(8,128)} %get-tuple-element.77.of_ref, bf16[4096,128]{1,0:T(8,128)(2,1)} %bitcast.24, ...), custom_call_target="tpu_custom_call" | custom-call | tf_op jit(solution)/shard_map/attend_grad/pallas_call | solution.py:1052
  184.3 31.1 %grads_back.1 = (bf16[1024,768]{1,0:T(8,128)(2,1)}, bf16[4,128,1024]{2,1,0:T(8,128)(2,1)}, f32[32,1024]{1,0:T(8,128)}, bf16[4,32,768]{2,1,0:T(8,128)(2,1)}) custom-call(bf16[4,64,512]{2,1,0:T(8,128)(2,1)} %get-tuple-element.79.refs_0_, bf16[4,4,2,128,128]{4,3,2,1,0:T(8,128)(2,1)} %bitcast.34, f32[512,128]{1,0:T(8,128)} %get-tuple-element.57.refs_2_, ...), custom_call_target="tpu_custom_call" | custom-call | tf_op jit(solution)/shard_map/grads_back/pallas_call | solution.py:76
  215.4 0.0 reduce-scatter.2.cloned.1.call-done
  215.4 29.1 %last_exchange.1 = (f32[128,1024]{1,0:T(8,128)}, bf16[4,32,768]{2,1,0:T(8,128)(2,1)}, bf16[2,4,32,1280]{3,2,1,0:T(8,128)(2,1)}, bf16[4,32,768]{2,1,0:T(8,128)(2,1)}) custom-call(bf16[4,128,1024]{2,1,0:T(8,128)(2,1)} %get-tuple-element.83.refs_0_, bf16[4,4,2,32,768]{4,3,2,1,0:T(8,128)(2,1)} %bitcast.31, bf16[2,4,32,1280]{3,2,1,0:T(8,128)(2,1)} %bitcast.35, ...), custom_call_target="tpu_custom_call" | custom-call | tf_op jit(solution)/shard_map/last_exchange/pallas_call | solution.py:76
  244.6 6.0 %finish.1 = (f32[128,1024]{1,0:T(8,128)}, f32[128,1024]{1,0:T(8,128)}, f32[1,32]{1,0:T(1,128)}, f32[32,3072]{1,0:T(8,128)}, f32[32,1024]{1,0:T(8,128)}, /*index=...) custom-call(f32[128,1024]{1,0:T(8,128)} %get-tuple-element.87.dn_ref, bf16[128,1024]{1,0:T(8,128)(2,1)} %x_ref.1, ...), custom_call_target="tpu_custom_call" | custom-call | tf_op jit(solution)/shard_map/finish/pallas_call | solution.py:1914
Async XLA Ops:
  7.2 109.7 %all-gather.2.cloned.1.call-start = ((), (), s32[]{:S(2)}) async-start(), calls=%async_computation.1 | async-start | bytes 2949120 | tf_op jit(solution)/shard_map/all_gather | solution.py:1952
  41.7 173.7 %reduce-scatter.2.cloned.1.call-start = ((), (), s32[]{:S(2)}) async-start(), calls=%async_computation.2 | async-start | bytes 3276800 | tf_op jit(solution)/shard_map/reduce_scatter | solution.py:1971
Sparse Core Ops, SparseCore 0:
  41.8 64.6 all-gather.1
  131.6 59.1 reduce-scatter.1

commit v7 on v6

--- a/solution.py
+++ b/solution.py
@@ -747,20 +747,24 @@
         )
 
 
-def grads_out(pc, dots, do_in, qsem, act):
+def grads_out(pc, dots, do_in, qsem, i, act):
     rows = dots.shape[3]
     for zi in range(pc.nz):
         th, tb = pc.attends(zi, pc.h, pc.s % 2, pc.s // 2)
         routed(
             pc,
-            dots.at[zi],
-            stretch_lanes(do_in, pc.zi, rows),
-            qsem.at[0, zi],
-            qsem.at[1, pc.zi],
+            dots.at[zi, i],
+            stretch_of(do_in, i, pc.zi, rows),
+            qsem.at[0, zi, i],
+            qsem.at[1, pc.zi, i],
             th,
             tb,
             act,
         )
+
+
+def stretch_of(ref, i, zi, rows):
+    return ref.at[i, :, pl.ds(pl.multiple_of(zi * rows, rows), rows)]
 
 
 def halves_swapped(tile):
@@ -1441,19 +1445,36 @@
     io.put(1)
     io.need(2)
     hy.start()
-    for hg in hgs:
-        hg.pass_on()
-    hy.send()
-    for hd, hg in zip(hds, hgs):
-        hd.finish()
-        hg.finish()
     io.need(5)
     wo = wo_ref[...]
     nt = (((1,), (1,)), ((), ()))
-    for i in range(nh):
+
+    def emit(i):
         part = lax.dot_general(wo, dg[i], nt, preferred_element_type=F32).astype(BF16)
         dots[:, i] = part.reshape(pc.nz, DH, rows)
-    grads_out(pc, dots, do_in, qsem, "start")
+        grads_out(pc, dots, do_in, qsem, i, "start")
+
+    nx = nh // 2
+    for hg in hgs:
+        hg.local.wait()
+        hg.near.wait_recv()
+    emit(h)
+    emit(pc.sib)
+    for hg in hgs:
+        hg.pass_on()
+    for k in range(1, nx):
+        emit(((pc.x + nx - k) % nx) * 2 + pc.c)
+    hy.send()
+    for hg in hgs:
+        for cp in hg.forward:
+            cp.wait_recv()
+    for k in range(1, nx):
+        emit(((pc.x + nx - k) % nx) * 2 + 1 - pc.c)
+    for hd, hg in zip(hds, hgs):
+        hd.finish()
+        hg.near.wait_send()
+        for cp in hg.across + hg.forward:
+            cp.wait_send()
     total = 0.0
     io.need(6)
     for i in range(nh):
@@ -1475,9 +1496,12 @@
         gb_out[d] = (gb_ref[d].astype(F32) + others).astype(BF16)
 
     io.put(4)
-    grads_out(pc, dots, do_in, qsem, "wait_send")
-    for zi in range(pc.nz):
-        wait_on(stretch_lanes(do_in, zi, rows), qsem.at[1, zi])
+
+    @pl.loop(0, nh)
+    def _(i):
+        grads_out(pc, dots, do_in, qsem, i, "wait_send")
+        for zi in range(pc.nz):
+            wait_on(stretch_of(do_in, i, zi, rows), qsem.at[1, zi, i])
 
 
 def back_exchange(lengths, dpart, ypart, hid, g, wo, og, gb):
@@ -1508,7 +1532,7 @@
             chunk_sems(nh),
             HeadSum.sem_shape(nh),
             chunk_sems(nh),
-            pltpu.SemaphoreType.DMA((2, nz)),
+            pltpu.SemaphoreType.DMA((2, nz, nh)),
             pltpu.SemaphoreType.DMA((2, gb.shape[1])),
             pltpu.SemaphoreType.DMA,
         ],

time: 258 us -> 251 us (0.973)
  Pallas kernels: 243 us -> 236 us
    pallas_call x1, Pallas kernels: 19.1 us -> 13.5 us  [attend_grad(): pl.pallas_call(functools.partial(attend_grad_body, nh, nb, hl, size), gri...]
    pallas_call x1, Pallas kernels: 13.8 us -> 9.28 us  [attend(): pl.pallas_call(functools.partial(attend_body, nh, nb, hl, size), grid_spe...]
    pallas_call x6, Pallas kernels: 189 us -> 193 us  [comm_call(): pl.pallas_call(staged_body, out_shape=out_shape, in_specs=in_specs, out_s...]
  transfers between devices with their start and end apart: 2 -> 2, of which waited for: 0 -> 0; matrix products, arithmetic and copies ran while one was open for 0% -> 0% of each run, Pallas kernels for 62% -> 61%
where the time goes in v7:
time: 251 us; the launch traced here: 250 us
  Pallas kernels  236 us (94%)
  between operations  14.1 us (6%)
    pallas_call x6, Pallas kernels, comm_call(): pl.pallas_call(staged_body, out_shape=out_shape, in_specs=in_specs, out_s...  193 us
    pallas_call x1, Pallas kernels, ffn(): pl.pallas_call(functools.partial(ffn_body, nh, nb, fl, split_rows, cut),...  14.6 us
    pallas_call x1, Pallas kernels, attend_grad(): pl.pallas_call(functools.partial(attend_grad_body, nh, nb, hl, size), gri...  13.5 us
    pallas_call x1, Pallas kernels, attend(): pl.pallas_call(functools.partial(attend_body, nh, nb, hl, size), grid_spe...  9.28 us
    pallas_call x1, Pallas kernels, finish(): pl.pallas_call(functools.partial(finish_body, nh, fl), out_shape=(f32(row...  5.96 us
  transfers between devices with their start and end apart: 2, of which 0 were waited for; matrix products, arithmetic and copies ran while one was open for 0% of the time, Pallas kernels for 61%

profile of v7, /device:TPU:0, one launch (start us, length us, event | category | flops | bytes accessed | tf_op | source)
XLA Modules:
  0.0 250.3 jit_solution(18257656007433631351)
XLA Ops:
  7.2 0.0 all-gather.2.cloned.1.call-start
  7.2 34.4 %first_exchange.1 = (bf16[4,128,1024]{2,1,0:T(8,128)(2,1)}, bf16[4,32,1280]{2,1,0:T(8,128)(2,1)}, bf16[4,32,128]{2,1,0:T(8,128)(2,1)}, bf16[4,32,640]{2,1,0:T(8,...) custom-call(s32[4]{0:T(128)} %len_ref.5, ...), custom_call_target="tpu_custom_call" | custom-call | tf_op jit(solution)/shard_map/first_exchange/pallas_call | solution.py:76
  41.7 0.0 all-gather.2.cloned.1.call-update
  41.7 0.2 reduce-scatter.2.cloned.1.call-start
  41.9 32.8 %to_heads.1 = (bf16[4,64,512]{2,1,0:T(8,128)(2,1)}, bf16[4,4,2,128,128]{4,3,2,1,0:T(8,128)(2,1)}, bf16[1,4,2,32,1024]{4,3,2,1,0:T(8,128)(2,1)}, bf16[4,4,2,32,12...) custom-call(bf16[512,1024]{1,0:T(8,128)(2,1)} %bitcast.25, bf16[1024,768]{1,0:T(8,128)(2,1)} %bitcast.21, ...), custom_call_target="tpu_custom_call" | custom-call | tf_op jit(solution)/shard_map/to_heads/pallas_call | solution.py:76
  74.7 9.3 %attend.1 = (bf16[4,64,512]{2,1,0:T(8,128)(2,1)}, f32[4,64,512]{2,1,0:T(8,128)}, f32[4,1,512]{2,1,0:T(1,128)}) custom-call(s32[4]{0:T(128)} %len_ref.5, bf16[4,64,512]{2,1,0:T(8,128)(2,1)} %get-tuple-element.61.q_ref, bf16[4096,128]{1,0:T(8,128)(2,1)} %bitcast.23), custom_call_target="tpu_custom_call" | custom-call | tf_op jit(solution)/shard_map/attend/pallas_call | solution.py:986
  84.0 28.0 %mid_exchange.1 = (bf16[4,4,64,128]{3,2,1,0:T(8,128)(2,1)}, f32[128,1024]{1,0:T(8,128)}, bf16[4,128,1024]{2,1,0:T(8,128)(2,1)}, bf16[4,4,2,32,640]{4,3,2,1,0:T(8,128)(2,1)}) custom-call(bf16[4,64,512]{2,1,0:T(8,128)(2,1)} %get-tuple-element.63.refs_0_, bf16[256,1024]{1,0:T(8,128)(2,1)} %bitcast.29, bf16[128,1024]{1,0:T(8,128)(2,1)} %x_ref.1, ...), custom_call_target="tpu_custom_call" | custom-call | tf_op jit(solution)/shard_map/mid_exchange/pallas_call | solution.py:76
  112.0 0.0 all-gather.2.cloned.1.call-done
  112.0 14.6 %ffn.1 = (bf16[4,128,1024]{2,1,0:T(8,128)(2,1)}, bf16[4,128,1024]{2,1,0:T(8,128)(2,1)}, bf16[8,4,32,1280]{3,2,1,0:T(8,128)(2,1)}, bf16[8,4,32,768]{3,2,1,0:T(8,128)(2,1)}) custom-call(s32[4]{0:T(128)} %len_ref.5, bf16[4,128,1024]{2,1,0:T(8,128)(2,1)} %get-tuple-element.66.n_hbm, bf16[4,128,1024]{2,1,0:T(8,128)(2,1)} %get-tuple-element.67.g_hbm, ...), custom_call_target="tpu_custom_call" | custom-call | tf_op jit(solution)/shard_map/ffn/pallas_call | solution.py:1376
  126.6 0.0 reduce-scatter.2.cloned.1.call-update
  126.7 31.5 %back_exchange.1 = (f32[128,1024]{1,0:T(8,128)}, f32[128,1024]{1,0:T(8,128)}, bf16[4,64,512]{2,1,0:T(8,128)(2,1)}, bf16[256,1024]{1,0:T(8,128)(2,1)}, bf16[4,4,32,768]{3,2,1,0:T(8,128)(2,1)}) custom-call(s32[4]{0:T(128)} %len_ref.5, bf16[4,128,1024]{2,1,0:T(8,128)(2,1)} %get-tuple-element.71.refs_1_, bf16[4,128,1024]{2,1,0:T(8,128)(2,1)} %get-tuple-element.72.refs_2_, ...), custom_call_target="tpu_custom_call" | custom-call | tf_op jit(solution)/shard_map/back_exchange/pallas_call | solution.py:76
  158.2 13.5 %attend_grad.1 = (bf16[4,64,512]{2,1,0:T(8,128)(2,1)}, bf16[4096,128]{1,0:T(8,128)(2,1)}) custom-call(s32[4]{0:T(128)} %len_ref.5, bf16[4,64,512]{2,1,0:T(8,128)(2,1)} %get-tuple-element.61.q_ref, bf16[4,64,512]{2,1,0:T(8,128)(2,1)} %get-tuple-element.76.do_ref, f32[4,64,512]{2,1,0:T(8,128)} %get-tuple-element.77.of_ref, bf16[4096,128]{1,0:T(8,128)(2,1)} %bitcast.24, ...), custom_call_target="tpu_custom_call" | custom-call | tf_op jit(solution)/shard_map/attend_grad/pallas_call | solution.py:1056
  171.7 36.6 %grads_back.1 = (bf16[1024,768]{1,0:T(8,128)(2,1)}, bf16[4,128,1024]{2,1,0:T(8,128)(2,1)}, f32[32,1024]{1,0:T(8,128)}, bf16[4,32,768]{2,1,0:T(8,128)(2,1)}) custom-call(bf16[4,64,512]{2,1,0:T(8,128)(2,1)} %get-tuple-element.79.refs_0_, bf16[4,4,2,128,128]{4,3,2,1,0:T(8,128)(2,1)} %bitcast.34, f32[512,128]{1,0:T(8,128)} %get-tuple-element.57.refs_2_, ...), custom_call_target="tpu_custom_call" | custom-call | tf_op jit(solution)/shard_map/grads_back/pallas_call | solution.py:76
  208.3 0.0 reduce-scatter.2.cloned.1.call-done
  208.3 29.2 %last_exchange.1 = (f32[128,1024]{1,0:T(8,128)}, bf16[4,32,768]{2,1,0:T(8,128)(2,1)}, bf16[2,4,32,1280]{3,2,1,0:T(8,128)(2,1)}, bf16[4,32,768]{2,1,0:T(8,128)(2,1)}) custom-call(bf16[4,128,1024]{2,1,0:T(8,128)(2,1)} %get-tuple-element.83.refs_0_, bf16[4,4,2,32,768]{4,3,2,1,0:T(8,128)(2,1)} %bitcast.31, bf16[2,4,32,1280]{3,2,1,0:T(8,128)(2,1)} %bitcast.35, ...), custom_call_target="tpu_custom_call" | custom-call | tf_op jit(solution)/shard_map/last_exchange/pallas_call | solution.py:76
  237.5 6.0 %finish.1 = (f32[128,1024]{1,0:T(8,128)}, f32[128,1024]{1,0:T(8,128)}, f32[1,32]{1,0:T(1,128)}, f32[32,3072]{1,0:T(8,128)}, f32[32,1024]{1,0:T(8,128)}, /*index=...) custom-call(f32[128,1024]{1,0:T(8,128)} %get-tuple-element.87.dn_ref, bf16[128,1024]{1,0:T(8,128)(2,1)} %x_ref.1, ...), custom_call_target="tpu_custom_call" | custom-call | tf_op jit(solution)/shard_map/finish/pallas_call | solution.py:1938
Async XLA Ops:
  7.2 104.8 %all-gather.2.cloned.1.call-start = ((), (), s32[]{:S(2)}) async-start(), calls=%async_computation.1 | async-start | bytes 2949120 | tf_op jit(solution)/shard_map/all_gather | solution.py:1976
  41.7 166.6 %reduce-scatter.2.cloned.1.call-start = ((), (), s32[]{:S(2)}) async-start(), calls=%async_computation.2 | async-start | bytes 3276800 | tf_op jit(solution)/shard_map/reduce_scatter | solution.py:1995
Sparse Core Ops, SparseCore 0:
  41.8 64.1 all-gather.1
  126.8 65.5 reduce-scatter.1

commit v8 on v7

--- a/solution.py
+++ b/solution.py
@@ -12,7 +12,7 @@
 ROPE_BASE = 160000.0
 NORM_EPS = 1e-05
 MASK_FLOOR = -1e30
-GRAD_CUT = 1280
+GRAD_CUT = 1152
 FF_BLOCKS = 2
 WEIGHT_CUTS = (1280, 1408)
 EXP_SCALE = 0.125 * math.log2(math.e)

time: 251 us -> 254 us (1.012)
    pallas_call x6, Pallas kernels: 193 us -> 185 us  [comm_call(): pl.pallas_call(staged_body, out_shape=out_shape, in_specs=in_specs, out_s...]
    pallas_call x1, Pallas kernels: 13.5 us -> 19.1 us  [attend_grad(): pl.pallas_call(functools.partial(attend_grad_body, nh, nb, hl, size), gri...]
    pallas_call x1, Pallas kernels: 9.28 us -> 13.8 us  [attend(): pl.pallas_call(functools.partial(attend_body, nh, nb, hl, size), grid_spe...]
  transfers between devices with their start and end apart: 2 -> 2, of which waited for: 0 -> 0; matrix products, arithmetic and copies ran while one was open for 0% -> 0% of each run, Pallas kernels for 61% -> 62%
where the time goes in v8:
time: 254 us; the launch traced here: 253 us
  Pallas kernels  238 us (94%)
  between operations  14.1 us (6%)
    pallas_call x6, Pallas kernels, comm_call(): pl.pallas_call(staged_body, out_shape=out_shape, in_specs=in_specs, out_s...  185 us
    pallas_call x1, Pallas kernels, attend_grad(): pl.pallas_call(functools.partial(attend_grad_body, nh, nb, hl, size), gri...  19.1 us
    pallas_call x1, Pallas kernels, ffn(): pl.pallas_call(functools.partial(ffn_body, nh, nb, fl, split_rows, cut),...  14.6 us
    pallas_call x1, Pallas kernels, attend(): pl.pallas_call(functools.partial(attend_body, nh, nb, hl, size), grid_spe...  13.8 us
    pallas_call x1, Pallas kernels, finish(): pl.pallas_call(functools.partial(finish_body, nh, fl), out_shape=(f32(row...  5.94 us
  transfers between devices with their start and end apart: 2, of which 0 were waited for; matrix products, arithmetic and copies ran while one was open for 0% of the time, Pallas kernels for 62%

profile of v8, /device:TPU:0, one launch (start us, length us, event | category | flops | bytes accessed | tf_op | source)
XLA Modules:
  0.0 252.7 jit_solution(13645150303449508859)
XLA Ops:
  7.2 0.0 all-gather.2.cloned.1.call-start
  7.2 34.4 %first_exchange.1 = (bf16[4,128,1024]{2,1,0:T(8,128)(2,1)}, bf16[4,32,1280]{2,1,0:T(8,128)(2,1)}, bf16[4,32,128]{2,1,0:T(8,128)(2,1)}, bf16[4,32,640]{2,1,0:T(8,...) custom-call(s32[4]{0:T(128)} %len_ref.5, ...), custom_call_target="tpu_custom_call" | custom-call | tf_op jit(solution)/shard_map/first_exchange/pallas_call | solution.py:76
  41.7 0.0 all-gather.2.cloned.1.call-update
  41.7 0.2 reduce-scatter.2.cloned.1.call-start
  41.9 32.8 %to_heads.1 = (bf16[4,64,512]{2,1,0:T(8,128)(2,1)}, bf16[4,4,2,128,128]{4,3,2,1,0:T(8,128)(2,1)}, bf16[1,4,2,32,1024]{4,3,2,1,0:T(8,128)(2,1)}, bf16[4,4,2,32,12...) custom-call(bf16[512,1024]{1,0:T(8,128)(2,1)} %bitcast.25, bf16[1024,768]{1,0:T(8,128)(2,1)} %bitcast.21, ...), custom_call_target="tpu_custom_call" | custom-call | tf_op jit(solution)/shard_map/to_heads/pallas_call | solution.py:76
  74.7 13.8 %attend.1 = (bf16[4,64,512]{2,1,0:T(8,128)(2,1)}, f32[4,64,512]{2,1,0:T(8,128)}, f32[4,1,512]{2,1,0:T(1,128)}) custom-call(s32[4]{0:T(128)} %len_ref.5, bf16[4,64,512]{2,1,0:T(8,128)(2,1)} %get-tuple-element.61.q_ref, bf16[4096,128]{1,0:T(8,128)(2,1)} %bitcast.23), custom_call_target="tpu_custom_call" | custom-call | tf_op jit(solution)/shard_map/attend/pallas_call | solution.py:986
  88.5 28.3 %mid_exchange.1 = (bf16[4,4,64,128]{3,2,1,0:T(8,128)(2,1)}, f32[128,1024]{1,0:T(8,128)}, bf16[4,128,1024]{2,1,0:T(8,128)(2,1)}, bf16[4,4,2,32,640]{4,3,2,1,0:T(8,128)(2,1)}) custom-call(bf16[4,64,512]{2,1,0:T(8,128)(2,1)} %get-tuple-element.63.refs_0_, bf16[256,1024]{1,0:T(8,128)(2,1)} %bitcast.29, bf16[128,1024]{1,0:T(8,128)(2,1)} %x_ref.1, ...), custom_call_target="tpu_custom_call" | custom-call | tf_op jit(solution)/shard_map/mid_exchange/pallas_call | solution.py:76
  116.8 0.0 all-gather.2.cloned.1.call-done
  116.8 14.6 %ffn.1 = (bf16[4,128,1024]{2,1,0:T(8,128)(2,1)}, bf16[4,128,1024]{2,1,0:T(8,128)(2,1)}, bf16[8,4,32,1152]{3,2,1,0:T(8,128)(2,1)}, bf16[8,4,32,896]{3,2,1,0:T(8,128)(2,1)}) custom-call(s32[4]{0:T(128)} %len_ref.5, bf16[4,128,1024]{2,1,0:T(8,128)(2,1)} %get-tuple-element.66.n_hbm, bf16[4,128,1024]{2,1,0:T(8,128)(2,1)} %get-tuple-element.67.g_hbm, ...), custom_call_target="tpu_custom_call" | custom-call | tf_op jit(solution)/shard_map/ffn/pallas_call | solution.py:1376
  131.5 0.0 reduce-scatter.2.cloned.1.call-update
  131.5 32.7 %back_exchange.1 = (f32[128,1024]{1,0:T(8,128)}, f32[128,1024]{1,0:T(8,128)}, bf16[4,64,512]{2,1,0:T(8,128)(2,1)}, bf16[256,1024]{1,0:T(8,128)(2,1)}, bf16[4,4,32,896]{3,2,1,0:T(8,128)(2,1)}) custom-call(s32[4]{0:T(128)} %len_ref.5, bf16[4,128,1024]{2,1,0:T(8,128)(2,1)} %get-tuple-element.71.refs_1_, bf16[4,128,1024]{2,1,0:T(8,128)(2,1)} %get-tuple-element.72.refs_2_, ...), custom_call_target="tpu_custom_call" | custom-call | tf_op jit(solution)/shard_map/back_exchange/pallas_call | solution.py:76
  164.2 19.1 %attend_grad.1 = (bf16[4,64,512]{2,1,0:T(8,128)(2,1)}, bf16[4096,128]{1,0:T(8,128)(2,1)}) custom-call(s32[4]{0:T(128)} %len_ref.5, bf16[4,64,512]{2,1,0:T(8,128)(2,1)} %get-tuple-element.61.q_ref, bf16[4,64,512]{2,1,0:T(8,128)(2,1)} %get-tuple-element.76.do_ref, f32[4,64,512]{2,1,0:T(8,128)} %get-tuple-element.77.of_ref, bf16[4096,128]{1,0:T(8,128)(2,1)} %bitcast.24, ...), custom_call_target="tpu_custom_call" | custom-call | tf_op jit(solution)/shard_map/attend_grad/pallas_call | solution.py:1056
  183.3 30.4 %grads_back.1 = (bf16[1024,768]{1,0:T(8,128)(2,1)}, bf16[4,128,1024]{2,1,0:T(8,128)(2,1)}, f32[32,1024]{1,0:T(8,128)}, bf16[4,32,896]{2,1,0:T(8,128)(2,1)}) custom-call(bf16[4,64,512]{2,1,0:T(8,128)(2,1)} %get-tuple-element.79.refs_0_, bf16[4,4,2,128,128]{4,3,2,1,0:T(8,128)(2,1)} %bitcast.34, f32[512,128]{1,0:T(8,128)} %get-tuple-element.57.refs_2_, ...), custom_call_target="tpu_custom_call" | custom-call | tf_op jit(solution)/shard_map/grads_back/pallas_call | solution.py:76
  213.7 0.0 reduce-scatter.2.cloned.1.call-done
  213.8 26.2 %last_exchange.1 = (f32[128,1024]{1,0:T(8,128)}, bf16[4,32,768]{2,1,0:T(8,128)(2,1)}, bf16[2,4,32,1152]{3,2,1,0:T(8,128)(2,1)}, bf16[4,32,896]{2,1,0:T(8,128)(2,1)}) custom-call(bf16[4,128,1024]{2,1,0:T(8,128)(2,1)} %get-tuple-element.83.refs_0_, bf16[4,4,2,32,768]{4,3,2,1,0:T(8,128)(2,1)} %bitcast.32, bf16[2,4,32,1152]{3,2,1,0:T(8,128)(2,1)} %bitcast.35, ...), custom_call_target="tpu_custom_call" | custom-call | tf_op jit(solution)/shard_map/last_exchange/pallas_call | solution.py:76
  240.0 5.9 %finish.1 = (f32[128,1024]{1,0:T(8,128)}, f32[128,1024]{1,0:T(8,128)}, f32[1,32]{1,0:T(1,128)}, f32[32,3072]{1,0:T(8,128)}, f32[32,1024]{1,0:T(8,128)}, /*index=...) custom-call(f32[128,1024]{1,0:T(8,128)} %get-tuple-element.87.dn_ref, bf16[128,1024]{1,0:T(8,128)(2,1)} %x_ref.1, ...), custom_call_target="tpu_custom_call" | custom-call | tf_op jit(solution)/shard_map/finish/pallas_call | solution.py:1938
Async XLA Ops:
  7.2 109.7 %all-gather.2.cloned.1.call-start = ((), (), s32[]{:S(2)}) async-start(), calls=%async_computation.1 | async-start | bytes 2949120 | tf_op jit(solution)/shard_map/all_gather | solution.py:1976
  41.7 172.1 %reduce-scatter.2.cloned.1.call-start = ((), (), s32[]{:S(2)}) async-start(), calls=%async_computation.2 | async-start | bytes 2949120 | tf_op jit(solution)/shard_map/reduce_scatter | solution.py:1995
Sparse Core Ops, SparseCore 0:
  41.8 64.6 all-gather.1
  131.6 55.1 reduce-scatter.1

commit v9 on v8

--- a/solution.py
+++ b/solution.py
@@ -14,7 +14,7 @@
 MASK_FLOOR = -1e30
 GRAD_CUT = 1152
 FF_BLOCKS = 2
-WEIGHT_CUTS = (1280, 1408)
+WEIGHT_CUTS = (1408, 1536)
 EXP_SCALE = 0.125 * math.log2(math.e)
 BF16 = jnp.bfloat16
 F32 = jnp.float32

time: 254 us -> 248 us (0.976)
  Pallas kernels: 238 us -> 233 us
    pallas_call x1, Pallas kernels: 19.1 us -> 13.5 us  [attend_grad(): pl.pallas_call(functools.partial(attend_grad_body, nh, nb, hl, size), gri...]
    pallas_call x6, Pallas kernels: 185 us -> 190 us  [comm_call(): pl.pallas_call(staged_body, out_shape=out_shape, in_specs=in_specs, out_s...]
    pallas_call x1, Pallas kernels: 13.8 us -> 9.45 us  [attend(): pl.pallas_call(functools.partial(attend_body, nh, nb, hl, size), grid_spe...]
  transfers between devices with their start and end apart: 2 -> 2, of which waited for: 0 -> 0; matrix products, arithmetic and copies ran while one was open for 0% -> 0% of each run, Pallas kernels for 62% -> 60%
where the time goes in v9:
time: 248 us
  Pallas kernels  233 us (94%)
  between operations  14.1 us (6%)
    pallas_call x6, Pallas kernels, comm_call(): pl.pallas_call(staged_body, out_shape=out_shape, in_specs=in_specs, out_s...  190 us
    pallas_call x1, Pallas kernels, ffn(): pl.pallas_call(functools.partial(ffn_body, nh, nb, fl, split_rows, cut),...  14.6 us
    pallas_call x1, Pallas kernels, attend_grad(): pl.pallas_call(functools.partial(attend_grad_body, nh, nb, hl, size), gri...  13.5 us
    pallas_call x1, Pallas kernels, attend(): pl.pallas_call(functools.partial(attend_body, nh, nb, hl, size), grid_spe...  9.45 us
    pallas_call x1, Pallas kernels, finish(): pl.pallas_call(functools.partial(finish_body, nh, fl), out_shape=(f32(row...  5.94 us
  transfers between devices with their start and end apart: 2, of which 0 were waited for; matrix products, arithmetic and copies ran while one was open for 0% of the time, Pallas kernels for 60%

profile of v9, /device:TPU:0, one launch (start us, length us, event | category | flops | bytes accessed | tf_op | source)
XLA Modules:
  0.0 247.8 jit_solution(14012582750055067829)
XLA Ops:
  7.2 0.0 all-gather.2.cloned.1.call-start
  7.2 34.4 %first_exchange.1 = (bf16[4,128,1024]{2,1,0:T(8,128)(2,1)}, bf16[4,32,1408]{2,1,0:T(8,128)(2,1)}, bf16[4,32,128]{2,1,0:T(8,128)(2,1)}, bf16[4,32,512]{2,1,0:T(8,...) custom-call(s32[4]{0:T(128)} %len_ref.5, ...), custom_call_target="tpu_custom_call" | custom-call | tf_op jit(solution)/shard_map/first_exchange/pallas_call | solution.py:76
  41.7 0.0 all-gather.2.cloned.1.call-update
  41.7 0.2 reduce-scatter.2.cloned.1.call-start
  41.9 32.0 %to_heads.1 = (bf16[4,64,512]{2,1,0:T(8,128)(2,1)}, bf16[4,4,2,128,128]{4,3,2,1,0:T(8,128)(2,1)}, bf16[1,4,2,32,1024]{4,3,2,1,0:T(8,128)(2,1)}, bf16[4,4,2,32,12...) custom-call(bf16[512,1024]{1,0:T(8,128)(2,1)} %bitcast.25, bf16[1024,768]{1,0:T(8,128)(2,1)} %bitcast.21, ...), custom_call_target="tpu_custom_call" | custom-call | tf_op jit(solution)/shard_map/to_heads/pallas_call | solution.py:76
  73.9 9.4 %attend.1 = (bf16[4,64,512]{2,1,0:T(8,128)(2,1)}, f32[4,64,512]{2,1,0:T(8,128)}, f32[4,1,512]{2,1,0:T(1,128)}) custom-call(s32[4]{0:T(128)} %len_ref.5, bf16[4,64,512]{2,1,0:T(8,128)(2,1)} %get-tuple-element.61.q_ref, bf16[4096,128]{1,0:T(8,128)(2,1)} %bitcast.23), custom_call_target="tpu_custom_call" | custom-call | tf_op jit(solution)/shard_map/attend/pallas_call | solution.py:986
  83.4 29.1 %mid_exchange.1 = (bf16[4,4,64,128]{3,2,1,0:T(8,128)(2,1)}, f32[128,1024]{1,0:T(8,128)}, bf16[4,128,1024]{2,1,0:T(8,128)(2,1)}, bf16[4,4,2,32,512]{4,3,2,1,0:T(8,128)(2,1)}) custom-call(bf16[4,64,512]{2,1,0:T(8,128)(2,1)} %get-tuple-element.63.refs_0_, bf16[256,1024]{1,0:T(8,128)(2,1)} %bitcast.29, bf16[128,1024]{1,0:T(8,128)(2,1)} %x_ref.1, ...), custom_call_target="tpu_custom_call" | custom-call | tf_op jit(solution)/shard_map/mid_exchange/pallas_call | solution.py:76
  112.5 0.0 all-gather.2.cloned.1.call-done
  112.6 14.6 %ffn.1 = (bf16[4,128,1024]{2,1,0:T(8,128)(2,1)}, bf16[4,128,1024]{2,1,0:T(8,128)(2,1)}, bf16[8,4,32,1152]{3,2,1,0:T(8,128)(2,1)}, bf16[8,4,32,896]{3,2,1,0:T(8,128)(2,1)}) custom-call(s32[4]{0:T(128)} %len_ref.5, bf16[4,128,1024]{2,1,0:T(8,128)(2,1)} %get-tuple-element.66.n_hbm, bf16[4,128,1024]{2,1,0:T(8,128)(2,1)} %get-tuple-element.67.g_hbm, ...), custom_call_target="tpu_custom_call" | custom-call | tf_op jit(solution)/shard_map/ffn/pallas_call | solution.py:1376
  127.2 0.0 reduce-scatter.2.cloned.1.call-update
  127.2 31.2 %back_exchange.1 = (f32[128,1024]{1,0:T(8,128)}, f32[128,1024]{1,0:T(8,128)}, bf16[4,64,512]{2,1,0:T(8,128)(2,1)}, bf16[256,1024]{1,0:T(8,128)(2,1)}, bf16[4,4,32,896]{3,2,1,0:T(8,128)(2,1)}) custom-call(s32[4]{0:T(128)} %len_ref.5, bf16[4,128,1024]{2,1,0:T(8,128)(2,1)} %get-tuple-element.71.refs_1_, bf16[4,128,1024]{2,1,0:T(8,128)(2,1)} %get-tuple-element.72.refs_2_, ...), custom_call_target="tpu_custom_call" | custom-call | tf_op jit(solution)/shard_map/back_exchange/pallas_call | solution.py:76
  158.5 13.5 %attend_grad.1 = (bf16[4,64,512]{2,1,0:T(8,128)(2,1)}, bf16[4096,128]{1,0:T(8,128)(2,1)}) custom-call(s32[4]{0:T(128)} %len_ref.5, bf16[4,64,512]{2,1,0:T(8,128)(2,1)} %get-tuple-element.61.q_ref, bf16[4,64,512]{2,1,0:T(8,128)(2,1)} %get-tuple-element.76.do_ref, f32[4,64,512]{2,1,0:T(8,128)} %get-tuple-element.77.of_ref, bf16[4096,128]{1,0:T(8,128)(2,1)} %bitcast.24, ...), custom_call_target="tpu_custom_call" | custom-call | tf_op jit(solution)/shard_map/attend_grad/pallas_call | solution.py:1056
  171.9 34.3 %grads_back.1 = (bf16[1024,768]{1,0:T(8,128)(2,1)}, bf16[4,128,1024]{2,1,0:T(8,128)(2,1)}, f32[32,1024]{1,0:T(8,128)}, bf16[4,32,896]{2,1,0:T(8,128)(2,1)}) custom-call(bf16[4,64,512]{2,1,0:T(8,128)(2,1)} %get-tuple-element.79.refs_0_, bf16[4,4,2,128,128]{4,3,2,1,0:T(8,128)(2,1)} %bitcast.34, f32[512,128]{1,0:T(8,128)} %get-tuple-element.57.refs_2_, ...), custom_call_target="tpu_custom_call" | custom-call | tf_op jit(solution)/shard_map/grads_back/pallas_call | solution.py:76
  206.2 0.0 reduce-scatter.2.cloned.1.call-done
  206.2 28.8 %last_exchange.1 = (f32[128,1024]{1,0:T(8,128)}, bf16[4,32,768]{2,1,0:T(8,128)(2,1)}, bf16[2,4,32,1152]{3,2,1,0:T(8,128)(2,1)}, bf16[4,32,896]{2,1,0:T(8,128)(2,1)}) custom-call(bf16[4,128,1024]{2,1,0:T(8,128)(2,1)} %get-tuple-element.83.refs_0_, bf16[4,4,2,32,768]{4,3,2,1,0:T(8,128)(2,1)} %bitcast.32, bf16[2,4,32,1152]{3,2,1,0:T(8,128)(2,1)} %bitcast.35, ...), custom_call_target="tpu_custom_call" | custom-call | tf_op jit(solution)/shard_map/last_exchange/pallas_call | solution.py:76
  235.1 5.9 %finish.1 = (f32[128,1024]{1,0:T(8,128)}, f32[128,1024]{1,0:T(8,128)}, f32[1,32]{1,0:T(1,128)}, f32[32,3072]{1,0:T(8,128)}, f32[32,1024]{1,0:T(8,128)}, /*index=...) custom-call(f32[128,1024]{1,0:T(8,128)} %get-tuple-element.87.dn_ref, bf16[128,1024]{1,0:T(8,128)(2,1)} %x_ref.1, ...), custom_call_target="tpu_custom_call" | custom-call | tf_op jit(solution)/shard_map/finish/pallas_call | solution.py:1938
Async XLA Ops:
  7.2 105.4 %all-gather.2.cloned.1.call-start = ((), (), s32[]{:S(2)}) async-start(), calls=%async_computation.1 | async-start | bytes 3244032 | tf_op jit(solution)/shard_map/all_gather | solution.py:1976
  41.7 164.5 %reduce-scatter.2.cloned.1.call-start = ((), (), s32[]{:S(2)}) async-start(), calls=%async_computation.2 | async-start | bytes 2949120 | tf_op jit(solution)/shard_map/reduce_scatter | solution.py:1995
Sparse Core Ops, SparseCore 0:
  41.8 70.6 all-gather.1
  127.3 54.5 reduce-scatter.1
